TPU v7x, 128 devices: a whole 4x4x4 slice. The times are simulated.
128 devices in a mesh: dom: 32 (over z, y_lo, x), feat: 4 (over y_hi, core).
Axes of the slice: x: 4, y: 4 (y_hi: 2, y_lo: 2; y = y_hi * 2 + y_lo), z: 4, core: 2. Of those that a mesh axis runs over, the one named last changes fastest.
Arguments:
- items: bfloat16 [8192, 1024], P('dom', 'feat'), may hold values from -6 to 6
- self_ids: int32 [8192], P('dom'), may hold values from 0 to 8191
- neighbor_ids: int32 [8192, 50], P('dom'), may hold values from 0 to 8191
- visit_counts: int32 [8192, 50], P('dom'), may hold values from 1 to 63
- w_self: bfloat16 [1024, 1024], P('feat'), may hold values from -0.1875 to 0.1875
- w_neighbor: bfloat16 [1024, 1024], P('feat'), may hold values from -0.75 to 0.75
- bias: float32 [1024], replicated, may hold values from -3 to 3
Outputs:
- embedding: float32 [8192, 1024], P('dom', 'feat')
All inputs are finite; a program needn't handle non-finite values.
Results may differ from a plain program's by a relative error of at most 0.0018.
Values may be sent and summed in bfloat16 or wider, within the bound.
No kernel may reach another device: no remote copies, remote signals or barrier semaphores. Data moves between devices by JAX's collectives and lax.ppermute only.
A program may use at most 64 MiB of HBM per device.

v0:
```python
import jax
import jax.numpy as jnp
from jax import lax
from jax.experimental import pallas as pl
from jax.experimental.pallas import tpu as pltpu
from jax.sharding import Mesh
from jax.sharding import PartitionSpec as P


DOM = ("z", "yl", "x")
LANES = 128
SLOTS = 64
TILES = 32
EIGHT = 8
GROUP = 16
SCALE = 16.0


def moved(value, axis, target):
    n = lax.axis_size(axis)
    return lax.ppermute(value, axis, [(i, target(i) % n) for i in range(n)])


def count_kernel(here_ref, ids_ref, count_ref, self_ref, *rest):
    out_refs, (turned, code_ref, low_ref, times_ref, own_tile_ref, own_low_ref) = rest[:-6], rest[-6:]
    nodes = out_refs[0].shape[0] // 2
    nbr = ids_ref.shape[0]
    here = here_ref[0]
    places = [(o, c) for o in range(len(out_refs)) for c in range(0, out_refs[o].shape[1], LANES)]

    def column(row):
        return jnp.broadcast_to(row.astype(jnp.float32), (LANES, LANES)).T.astype(jnp.bfloat16)

    node = lax.broadcasted_iota(jnp.int32, (nbr, LANES), 1) & (EIGHT - 1)
    for part in range(nodes // LANES):
        span = pl.ds(part * LANES, LANES)
        tile, low = located(ids_ref[:, span], here)
        code = jnp.where(tile < 0, -1, tile * EIGHT + node)
        for ref, value, blank in (
            (code_ref, code, -1.0),
            (low_ref, low, -1.0),
            (times_ref, count_ref[:, span], 0.0),
        ):
            turned[...] = jnp.full((LANES, LANES), blank, jnp.float32)
            for slot in range(0, LANES, SLOTS):
                turned[slot : slot + nbr, :] = value.astype(jnp.float32)
            ref[span, :] = turned[...].T
        own_tile, own_low = located(self_ref[part : part + 1, :], here)
        own_tile_ref[span, :] = column(own_tile)
        own_low_ref[span, :] = column(own_low)

    row = lax.broadcasted_iota(jnp.int32, (GROUP, LANES), 0).astype(jnp.float32)
    rows = [(row + r * GROUP).astype(jnp.bfloat16) for r in range(TILES * EIGHT // GROUP)]
    lane = lax.broadcasted_iota(jnp.int32, (GROUP, LANES), 1)
    left = lane < SLOTS
    lane = lane.astype(jnp.float32).astype(jnp.bfloat16)
    zero = jnp.zeros((GROUP, LANES), jnp.bfloat16)
    one = jnp.ones((GROUP, LANES), jnp.bfloat16)

    def pair(table, n):
        first, second = (
            jnp.broadcast_to(table[i : i + 1, :], (GROUP, LANES)) for i in (n, n + 1)
        )
        return jnp.where(left, first, second).astype(jnp.bfloat16)

    @pl.loop(0, nodes // GROUP)
    def _(g):
        first = pl.multiple_of(g * GROUP, GROUP)
        span = pl.ds(first, GROUP)
        tables = [r[span, :] for r in (code_ref, low_ref, times_ref)]
        sides = []
        for eight in range(0, GROUP, EIGHT):
            marks, lows = [], []
            for n in range(eight, eight + EIGHT, 2):
                code, low, times = (pair(t, n) for t in tables)
                marks.append(
                    jnp.concatenate([jnp.where(code == r, times, zero) for r in rows], axis=0)
                )
                lows.append(
                    jnp.concatenate(
                        [jnp.where(low == r, one, zero) for r in rows[: LANES // GROUP]], axis=0
                    )
                )
            sides.append(
                lax.dot_general(
                    jnp.concatenate(marks, axis=1),
                    jnp.concatenate(lows, axis=1),
                    (((1,), (1,)), ((), ())),
                    preferred_element_type=jnp.float32,
                )
            )
        own_tile = own_tile_ref[span, :]
        hit = jnp.where(own_low_ref[span, :] == lane, one, zero)
        for t, (o, col) in enumerate(places):
            block = jnp.concatenate([side[t * EIGHT : t * EIGHT + EIGHT, :] for side in sides], axis=0)
            out_refs[o][span, col : col + LANES] = block.astype(jnp.bfloat16)
            out_refs[o][pl.ds(nodes + first, GROUP), col : col + LANES] = jnp.where(
                own_tile == jnp.bfloat16(t), hit, zero
            )


def located(ids, here):
    block = ids >> 8
    dz = ((here >> 3) - (block >> 3)) & 3
    dx = (here - block) & 3
    same = (((here ^ block) >> 2) & 1) == 0
    first_half = (ids & 128) == 0
    far = jnp.where(first_half, dz, dx)
    near = jnp.where(first_half, here ^ block, (here ^ block) >> 3) & 3
    tile = jnp.where(first_half, 0, 16) + (far ^ (far >> 1)) * 4 + (near ^ (near >> 1))
    return jnp.where(same, tile, -1), ids & 127


def count_blocks(here, ids, counts, own, widths):
    nodes = ids.shape[1]
    vmem = pl.BlockSpec(memory_space=pltpu.VMEM)
    return pl.pallas_call(
        count_kernel,
        out_shape=[jax.ShapeDtypeStruct((2 * nodes, w), jnp.bfloat16) for w in widths],
        in_specs=[pl.BlockSpec(memory_space=pltpu.SMEM)] + [vmem] * 3,
        out_specs=[vmem] * len(widths),
        scratch_shapes=[pltpu.VMEM((LANES, LANES), jnp.float32)]
        + [pltpu.VMEM((nodes, LANES), jnp.float32)] * 3
        + [pltpu.VMEM((nodes, LANES), jnp.bfloat16)] * 2,
        compiler_params=pltpu.CompilerParams(vmem_limit_bytes=16 * 2**20),
        cost_estimate=pl.CostEstimate(
            flops=4_000_000_000, bytes_accessed=9_000_000, transcendentals=0
        ),
        name="counts",
    )(here, ids, counts, own)


def shards(items, self_ids, neighbor_ids, visit_counts, w_self, w_neighbor, bias):
    core, yh = lax.axis_index("core"), lax.axis_index("yh")
    batch, share = self_ids.shape[0], items.shape[1]
    nbr = neighbor_ids.shape[1]
    half = items.shape[0] // 2
    here = lax.axis_index(DOM).reshape(1)

    table = jnp.concatenate([neighbor_ids.T, visit_counts.T, self_ids[None, :]], axis=0)
    theirs = moved(table.astype(jnp.int16), "yl", lambda i: i ^ 1).astype(jnp.int32)
    table = jnp.concatenate([table, theirs], axis=1)
    ids, counts, own_ids = table[:nbr], table[nbr : 2 * nbr], table[2 * nbr]

    axes = [("x", "z"), ("z", "x")]
    halves = [items[:half], items[half:]]
    lines = []
    for block, (near, _) in zip(halves, axes):
        pair = jnp.concatenate([block, moved(block, near, lambda i: i ^ 1)], axis=0)
        lines.append(jnp.concatenate([pair, moved(pair, near, lambda i: i ^ 3)], axis=0))
    pieces = []
    for line, (_, far) in zip(lines, axes):
        up, down = moved(line, far, lambda i: i + 1), moved(line, far, lambda i: i + 3)
        pieces += [line, up, down, moved(up, far, lambda i: i + 1)]

    blocks = count_blocks(
        here, ids, counts, own_ids.reshape(-1, LANES), [p.shape[0] for p in pieces]
    )
    sums = sum(
        jnp.dot(blocks[i], pieces[i], preferred_element_type=jnp.float32)
        for i in (0, 4, 1, 5, 2, 6, 3, 7)
    )
    total = jnp.sum(counts.astype(jnp.float32), axis=0)
    own = sums[2 * batch :].astype(jnp.bfloat16)
    pooled = sums[: 2 * batch] / total[:, None]
    high = lax.reduce_precision(pooled, 8, 7)
    both = jnp.concatenate(
        [own, high.astype(jnp.bfloat16), (pooled - high).astype(jnp.bfloat16)], axis=1
    )

    wide = 2 * share
    weights = jnp.concatenate([w_self, w_neighbor, w_neighbor], axis=0)
    weights = weights.reshape(3 * share, 2, 2, share)

    def columns(which):
        return lax.dynamic_index_in_dim(weights, which, 2, False).reshape(3 * share, wide)

    given = jnp.dot(both, columns(1 - core), preferred_element_type=jnp.float32)
    got = moved((given * SCALE).astype(jnp.float16), "core", lambda i: i ^ 1)
    kept = jnp.dot(both, columns(core), preferred_element_type=jnp.float32)
    kept = lax.optimization_barrier(kept)
    chip = kept * SCALE + got.astype(jnp.float32)
    sent = chip.astype(jnp.float16)
    from_yh = moved(sent[:batch], "yh", lambda i: i ^ 1)
    from_yl = moved(sent[batch:], "yl", lambda i: i ^ 1)
    across = lax.ppermute(sent[batch:], ("yl", "yh"), [(i, i ^ 3) for i in range(4)])
    pre = chip[:batch] + from_yh.astype(jnp.float32)
    pre = pre + from_yl.astype(jnp.float32) + across.astype(jnp.float32)
    my_bias = lax.dynamic_index_in_dim(bias.reshape(2, 2, share), core, 1, False).reshape(1, wide)
    hidden = jnp.maximum(pre * (1.0 / SCALE) + my_bias, 0.0)
    squares = jnp.sum(hidden * hidden, axis=1)
    squares = squares + moved(squares, "core", lambda i: i ^ 1)
    scale = jnp.sqrt(squares / bias.shape[0] + 1e-06)[:, None]
    out = jnp.where(yh == 0, hidden[:, :share], hidden[:, share:])
    return out / scale


def solution(mesh):
    torus = Mesh(mesh.devices.reshape(4, 2, 4, 2, 2), ("z", "yl", "x", "yh", "core"))
    feat = ("yh", "core")
    placed = (
        P(DOM, feat),
        P(DOM),
        P(DOM, None),
        P(DOM, None),
        P(feat, None),
        P(feat, None),
        P(),
    )

    return jax.shard_map(
        shards, mesh=torus, in_specs=placed, out_specs=P(DOM, feat), check_vma=False
    )
```

profile of v0, /device:TPU:1, one launch (start us, length us, event | category | flops | bytes accessed | tf_op | source)
XLA Modules:
  0.0 67.6 jit_solution(3967120664059745730)
XLA Ops:
  0.0 0.9 %add_convert_fusion = s16[101,256]{1,0:T(8,128)(2,1)S(1)} fusion(s32[1,256]{1,0:T(1,128)} %bitcast.35, s32[50,256]{1,0:T(8,128)} %bitcast.29, s32[50,256]{1,0:T(8,128)} %bitcast.32), kind=kLoop, calls=%fused_computation.33 | loop fusion | flops 77568 | bytes 155136 | tf_op jit(solution)/shard_map/convert_element_type | solution.py:141
  0.9 2.2 %collective-permute-start = (s16[101,256]{1,0:T(8,128)(2,1)S(1)}, s16[101,256]{1,0:T(8,128)(2,1)S(1)}, u32[]{:S(2)}, u32[]{:S(2)}) collective-permute-start(s16[101,256]{1,0:T(8,128)(2,1)S(1)} %add_convert_fusion), channel_id=1, source_target_pairs={{0,16},{16,0},{1,17},{17,1},{2,18},{18,2},{3,19},{19,3},{4,20},{20... | collective-permute-start | bytes 155144 | tf_op jit(solution)/shard_map/ppermute | solution.py:21
  3.1 0.9 %fusion.21 = (bf16[128,256]{1,0:T(8,128)(2,1)S(1)}, bf16[128,256]{1,0:T(8,128)(2,1)S(1)}) fusion(bf16[256,256]{1,0:T(8,128)(2,1)} %param.7), kind=kLoop, calls=%fused_computation.45 | loop fusion | bytes 262144 | tf_op jit(solution)/shard_map/slice | solution.py:146
  4.0 1.3 %collective-permute-start.1 = (bf16[128,256]{1,0:T(8,128)(2,1)S(1)}, bf16[128,256]{1,0:T(8,128)(2,1)S(1)}, u32[]{:S(2)}, u32[]{:S(2)}) collective-permute-start(bf16[128,256]{1,0:T(8,128)(2,1)S(1)} %get-tuple-element.33), channel_id=1, source_target_pairs={{0,4},{4,0},{8,12},{12,8},{1,5},{5,1},{9,13},{13,9},{2,6},{6,2},{1... | collective-permute-start | bytes 196616 | tf_op jit(solution)/shard_map/ppermute | solution.py:21
  5.3 1.6 %collective-permute-start.3 = (bf16[128,256]{1,0:T(8,128)(2,1)S(1)}, bf16[128,256]{1,0:T(8,128)(2,1)S(1)}, u32[]{:S(2)}, u32[]{:S(2)}) collective-permute-start(bf16[128,256]{1,0:T(8,128)(2,1)S(1)} %get-tuple-element.34), channel_id=1, source_target_pairs={{0,32},{32,0},{64,96},{96,64},{1,33},{33,1},{65,97},{97,65},{2,34}... | collective-permute-start | bytes 196616 | tf_op jit(solution)/shard_map/ppermute | solution.py:21
  6.9 1.2 %copy.8 = bf16[256,1024]{0,1:T(8,128)(2,1)S(1)} copy(bf16[256,1024]{1,0:T(8,128)(2,1)} %param.11) | data formatting | bytes 1048576 | tf_op args[4]
  8.7 0.6 copy-done.1
  9.4 10.1 %counts.1 = (bf16[1024,512]{1,0:T(8,128)(2,1)S(1)}, bf16[1024,512]{1,0:T(8,128)(2,1)S(1)}, bf16[1024,512]{1,0:T(8,128)(2,1)S(1)}, bf16[1024,512]{1,0:T(8,128)(2,...) custom-call(s32[1]{0:T(128)} %bitcast.here_ref, ...), custom_call_target="tpu_custom_call" | custom-call | flops 4000000000 | bytes 9000000 | tf_op jit(solution)/shard_map/counts/pallas_call | solution.py:117
  19.6 1.9 %collective-permute-start.2 = (bf16[256,256]{1,0:T(8,128)(2,1)S(1)}, bf16[256,256]{1,0:T(8,128)(2,1)S(1)}, u32[]{:S(2)}, u32[]{:S(2)}) collective-permute-start(bf16[256,256]{1,0:T(8,128)(2,1)S(1)} %pad_maximum_fusion.6), channel_id=1, source_target_pairs={{0,12},{4,8},{8,4},{12,0},{1,13},{5,9},{9,5},{13,1},{2,14},{6,10},... | collective-permute-start | bytes 393224 | tf_op jit(solution)/shard_map/ppermute | solution.py:21
  21.5 2.3 %collective-permute-start.4 = (bf16[256,256]{1,0:T(8,128)(2,1)S(1)}, bf16[256,256]{1,0:T(8,128)(2,1)S(1)}, u32[]{:S(2)}, u32[]{:S(2)}) collective-permute-start(bf16[256,256]{1,0:T(8,128)(2,1)S(1)} %pad_maximum_fusion.7), channel_id=1, source_target_pairs={{0,96},{32,64},{64,32},{96,0},{1,97},{33,65},{65,33},{97,1},{2,98}... | collective-permute-start | bytes 393224 | tf_op jit(solution)/shard_map/ppermute | solution.py:21
  23.8 0.8 %collective-permute-done.2 = bf16[256,256]{1,0:T(8,128)(2,1)S(1)} collective-permute-done((bf16[256,256]{1,0:T(8,128)(2,1)S(1)}, bf16[256,256]{1,0:T(8,128)(2,1)S(1)}, u32[]{:S(2)}, u32[]{:S(2)}) %collective-permute-start.2) | collective-permute-done | bytes 131104 | tf_op jit(solution)/shard_map/ppermute | solution.py:21
  24.8 2.7 %collective-permute-start.7 = (bf16[512,256]{1,0:T(8,128)(2,1)S(1)}, bf16[512,256]{1,0:T(8,128)(2,1)S(1)}, u32[]{:S(2)}, u32[]{:S(2)}) collective-permute-start(bf16[512,256]{1,0:T(8,128)(2,1)S(1)} %pad_maximum_fusion.4), channel_id=1, source_target_pairs={{0,96},{32,0},{64,32},{96,64},{1,97},{33,1},{65,33},{97,65},{2,98}... | collective-permute-start | bytes 786440 | tf_op jit(solution)/shard_map/ppermute | solution.py:21
  27.6 2.7 %collective-permute-start.8 = (bf16[512,256]{1,0:T(8,128)(2,1)S(1)}, bf16[512,256]{1,0:T(8,128)(2,1)S(1)}, u32[]{:S(2)}, u32[]{:S(2)}) collective-permute-start(bf16[512,256]{1,0:T(8,128)(2,1)S(1)} %pad_maximum_fusion.5), channel_id=1, source_target_pairs={{0,12},{4,0},{8,4},{12,8},{1,13},{5,1},{9,5},{13,9},{2,14},{6,2},{... | collective-permute-start | bytes 786440 | tf_op jit(solution)/shard_map/ppermute | solution.py:21
  30.7 1.4 %collective-permute-done.5 = bf16[512,256]{1,0:T(8,128)(2,1)S(1)} collective-permute-done((bf16[512,256]{1,0:T(8,128)(2,1)S(1)}, bf16[512,256]{1,0:T(8,128)(2,1)S(1)}, u32[]{:S(2)}, u32[]{:S(2)}) %collective-permute-start.5) | collective-permute-done | bytes 262176 | tf_op jit(solution)/shard_map/ppermute | solution.py:21
  32.1 0.5 fusion.22
  32.6 1.7 %collective-permute-done.6 = bf16[512,256]{1,0:T(8,128)(2,1)S(1)} collective-permute-done((bf16[512,256]{1,0:T(8,128)(2,1)S(1)}, bf16[512,256]{1,0:T(8,128)(2,1)S(1)}, u32[]{:S(2)}, u32[]{:S(2)}) %collective-permute-start.6) | collective-permute-done | bytes 262176 | tf_op jit(solution)/shard_map/ppermute | solution.py:21
  34.8 0.5 fusion.24
  35.8 0.6 fusion.4
  36.4 4.6 %collective-permute-done.10 = bf16[512,256]{1,0:T(8,128)(2,1)S(1)} collective-permute-done((bf16[512,256]{1,0:T(8,128)(2,1)S(1)}, bf16[512,256]{1,0:T(8,128)(2,1)S(1)}, u32[]{:S(2)}, u32[]{:S(2)}) %collective-permute-start.10) | collective-permute-done | bytes 262176 | tf_op jit(solution)/shard_map/ppermute | solution.py:21
  41.5 0.5 fusion
  42.2 0.6 fusion.5
  42.8 5.0 %collective-permute-start.11 = (f16[512,512]{1,0:T(8,128)(2,1)S(1)}, f16[512,512]{1,0:T(8,128)(2,1)S(1)}, u32[]{:S(2)}, u32[]{:S(2)}) collective-permute-start(f16[512,512]{1,0:T(8,128)(2,1)S(1)} %fusion.5), channel_id=1, source_target_pairs={{0,1},{1,0},{2,3},{3,2},{4,5},{5,4},{6,7},{7,6},{8,9},{9,8},{10,11... | collective-permute-start | bytes 1572872 | tf_op jit(solution)/shard_map/ppermute | solution.py:21
  47.8 0.6 fusion.12
  48.5 0.9 %collective-permute-done.11 = f16[512,512]{1,0:T(8,128)(2,1)S(1)} collective-permute-done((f16[512,512]{1,0:T(8,128)(2,1)S(1)}, f16[512,512]{1,0:T(8,128)(2,1)S(1)}, u32[]{:S(2)}, u32[]{:S(2)}) %collective-permute-start.11) | collective-permute-done | bytes 524320 | tf_op jit(solution)/shard_map/ppermute | solution.py:21
  49.7 2.7 %collective-permute-start.12 = (f16[256,512]{1,0:T(8,128)(2,1)S(1)}, f16[256,512]{1,0:T(8,128)(2,1)S(1)}, u32[]{:S(2)}, u32[]{:S(2)}) collective-permute-start(f16[256,512]{1,0:T(8,128)(2,1)S(1)} %get-tuple-element.29), channel_id=1, source_target_pairs={{0,2},{2,0},{1,3},{3,1},{4,6},{6,4},{5,7},{7,5},{8,10},{10,8},{9,1... | collective-permute-start | bytes 786440 | tf_op jit(solution)/shard_map/ppermute | solution.py:21
  52.4 0.6 collective-permute-start.14
  53.0 5.8 %collective-permute-done.12 = f16[256,512]{1,0:T(8,128)(2,1)S(1)} collective-permute-done((f16[256,512]{1,0:T(8,128)(2,1)S(1)}, f16[256,512]{1,0:T(8,128)(2,1)S(1)}, u32[]{:S(2)}, u32[]{:S(2)}) %collective-permute-start.12) | collective-permute-done | bytes 262176 | tf_op jit(solution)/shard_map/ppermute | solution.py:21
  58.8 5.1 %collective-permute-done.13 = f16[256,512]{1,0:T(8,128)(2,1)S(1)} collective-permute-done((f16[256,512]{1,0:T(8,128)(2,1)S(1)}, f16[256,512]{1,0:T(8,128)(2,1)S(1)}, u32[]{:S(2)}, u32[]{:S(2)}) %collective-permute-start.13) | collective-permute-done | bytes 262176 | tf_op jit(solution)/shard_map/ppermute | solution.py:21
  63.9 1.2 %collective-permute-done.14 = f16[256,512]{1,0:T(8,128)(2,1)S(1)} collective-permute-done((f16[256,512]{1,0:T(8,128)(2,1)S(1)}, f16[256,512]{1,0:T(8,128)(2,1)S(1)}, u32[]{:S(2)}, u32[]{:S(2)}) %collective-permute-start.14) | collective-permute-done | bytes 262176 | tf_op jit(solution)/shard_map/ppermute | solution.py:186
  65.4 0.6 collective-permute-start.15
  65.9 0.8 %collective-permute-done.15 = f32[256]{0:T(256)S(1)} collective-permute-done((f32[256]{0:T(256)S(1)}, f32[256]{0:T(256)S(1)}, u32[]{:S(2)}, u32[]{:S(2)}) %collective-permute-start.15) | collective-permute-done | bytes 1056 | tf_op jit(solution)/shard_map/ppermute | solution.py:21
  66.8 0.8 %fusion.13 = f32[256,256]{1,0:T(8,128)} fusion(f32[256,512]{1,0:T(8,128)S(1)} %get-tuple-element.22, f32[256]{0:T(256)S(1)} %add_sqrt_fusion, pred[]{:T(512)S(6)} %eq.3), kind=kLoop, calls=%fused_computation.26 | loop fusion | flops 131072 | bytes 787457 | tf_op jit(solution)/shard_map/div | solution.py:195
  (45 shorter events, 3.4 us)
Async XLA Ops:
  0.0 8.2 %copy-start = (bf16[256,1024]{1,0:T(8,128)(2,1)S(1)}, bf16[256,1024]{1,0:T(8,128)(2,1)}, u32[]{:S(2)}) copy-start(bf16[256,1024]{1,0:T(8,128)(2,1)} %param.12) | copy-start | bytes 1572868
  0.9 7.8 %collective-permute-start = (s16[101,256]{1,0:T(8,128)(2,1)S(1)}, s16[101,256]{1,0:T(8,128)(2,1)S(1)}, u32[]{:S(2)}, u32[]{:S(2)}) collective-permute-start(s16[101,256]{1,0:T(8,128)(2,1)S(1)} %add_convert_fusion), channel_id=1, source_target_pairs={{0,16},{16,0},{1,17},{17,1},{2,18},{18,2},{3,19},{19,3},{4,20},{20... | collective-permute-start | bytes 155144 | tf_op jit(solution)/shard_map/ppermute | solution.py:21
  4.0 15.5 %collective-permute-start.1 = (bf16[128,256]{1,0:T(8,128)(2,1)S(1)}, bf16[128,256]{1,0:T(8,128)(2,1)S(1)}, u32[]{:S(2)}, u32[]{:S(2)}) collective-permute-start(bf16[128,256]{1,0:T(8,128)(2,1)S(1)} %get-tuple-element.33), channel_id=1, source_target_pairs={{0,4},{4,0},{8,12},{12,8},{1,5},{5,1},{9,13},{13,9},{2,6},{6,2},{1... | collective-permute-start | bytes 196616 | tf_op jit(solution)/shard_map/ppermute | solution.py:21
  5.3 16.2 %collective-permute-start.3 = (bf16[128,256]{1,0:T(8,128)(2,1)S(1)}, bf16[128,256]{1,0:T(8,128)(2,1)S(1)}, u32[]{:S(2)}, u32[]{:S(2)}) collective-permute-start(bf16[128,256]{1,0:T(8,128)(2,1)S(1)} %get-tuple-element.34), channel_id=1, source_target_pairs={{0,32},{32,0},{64,96},{96,64},{1,33},{33,1},{65,97},{97,65},{2,34}... | collective-permute-start | bytes 196616 | tf_op jit(solution)/shard_map/ppermute | solution.py:21
  8.5 0.8 %copy-start.1 = (s32[256,50]{0,1:T(8,128)S(1)}, s32[256,50]{0,1:T(8,128)}, u32[]{:S(2)}) copy-start(s32[256,50]{0,1:T(8,128)} %param.10) | copy-start | bytes 153604
  8.5 0.8 %copy-start.2 = (s32[256,50]{0,1:T(8,128)S(1)}, s32[256,50]{0,1:T(8,128)}, u32[]{:S(2)}) copy-start(s32[256,50]{0,1:T(8,128)} %param.9) | copy-start | bytes 153604
  8.5 0.8 %copy-start.3 = (s32[256]{0:T(256)S(1)}, s32[256]{0:T(256)}, u32[]{:S(2)}) copy-start(s32[256]{0:T(256)} %param.8) | copy-start | bytes 3076
  19.6 5.1 %collective-permute-start.2 = (bf16[256,256]{1,0:T(8,128)(2,1)S(1)}, bf16[256,256]{1,0:T(8,128)(2,1)S(1)}, u32[]{:S(2)}, u32[]{:S(2)}) collective-permute-start(bf16[256,256]{1,0:T(8,128)(2,1)S(1)} %pad_maximum_fusion.6), channel_id=1, source_target_pairs={{0,12},{4,8},{8,4},{12,0},{1,13},{5,9},{9,5},{13,1},{2,14},{6,10},... | collective-permute-start | bytes 393224 | tf_op jit(solution)/shard_map/ppermute | solution.py:21
  21.5 6.0 %collective-permute-start.4 = (bf16[256,256]{1,0:T(8,128)(2,1)S(1)}, bf16[256,256]{1,0:T(8,128)(2,1)S(1)}, u32[]{:S(2)}, u32[]{:S(2)}) collective-permute-start(bf16[256,256]{1,0:T(8,128)(2,1)S(1)} %pad_maximum_fusion.7), channel_id=1, source_target_pairs={{0,96},{32,64},{64,32},{96,0},{1,97},{33,65},{65,33},{97,1},{2,98}... | collective-permute-start | bytes 393224 | tf_op jit(solution)/shard_map/ppermute | solution.py:21
  24.7 7.4 %collective-permute-start.5 = (bf16[512,256]{1,0:T(8,128)(2,1)S(1)}, bf16[512,256]{1,0:T(8,128)(2,1)S(1)}, u32[]{:S(2)}, u32[]{:S(2)}) collective-permute-start(bf16[512,256]{1,0:T(8,128)(2,1)S(1)} %pad_maximum_fusion.4), channel_id=1, source_target_pairs={{0,32},{32,64},{64,96},{96,0},{1,33},{33,65},{65,97},{97,1},{2,34}... | collective-permute-start | bytes 786440 | tf_op jit(solution)/shard_map/ppermute | solution.py:21
  24.8 10.0 %collective-permute-start.7 = (bf16[512,256]{1,0:T(8,128)(2,1)S(1)}, bf16[512,256]{1,0:T(8,128)(2,1)S(1)}, u32[]{:S(2)}, u32[]{:S(2)}) collective-permute-start(bf16[512,256]{1,0:T(8,128)(2,1)S(1)} %pad_maximum_fusion.4), channel_id=1, source_target_pairs={{0,96},{32,0},{64,32},{96,64},{1,97},{33,1},{65,33},{97,65},{2,98}... | collective-permute-start | bytes 786440 | tf_op jit(solution)/shard_map/ppermute | solution.py:21
  27.5 6.8 %collective-permute-start.6 = (bf16[512,256]{1,0:T(8,128)(2,1)S(1)}, bf16[512,256]{1,0:T(8,128)(2,1)S(1)}, u32[]{:S(2)}, u32[]{:S(2)}) collective-permute-start(bf16[512,256]{1,0:T(8,128)(2,1)S(1)} %pad_maximum_fusion.5), channel_id=1, source_target_pairs={{0,4},{4,8},{8,12},{12,0},{1,5},{5,9},{9,13},{13,1},{2,6},{6,10},{... | collective-permute-start | bytes 786440 | tf_op jit(solution)/shard_map/ppermute | solution.py:21
  27.6 7.7 %collective-permute-start.8 = (bf16[512,256]{1,0:T(8,128)(2,1)S(1)}, bf16[512,256]{1,0:T(8,128)(2,1)S(1)}, u32[]{:S(2)}, u32[]{:S(2)}) collective-permute-start(bf16[512,256]{1,0:T(8,128)(2,1)S(1)} %pad_maximum_fusion.5), channel_id=1, source_target_pairs={{0,12},{4,0},{8,4},{12,8},{1,13},{5,1},{9,5},{13,9},{2,14},{6,2},{... | collective-permute-start | bytes 786440 | tf_op jit(solution)/shard_map/ppermute | solution.py:21
  32.1 9.4 %collective-permute-start.9 = (bf16[512,256]{1,0:T(8,128)(2,1)S(1)}, bf16[512,256]{1,0:T(8,128)(2,1)S(1)}, u32[]{:S(2)}, u32[]{:S(2)}) collective-permute-start(bf16[512,256]{1,0:T(8,128)(2,1)S(1)} %collective-permute-done.5), channel_id=1, source_target_pairs={{0,32},{32,64},{64,96},{96,0},{1,33},{33,65},{65,97},{97,1},{2,34}... | collective-permute-start | bytes 786440 | tf_op jit(solution)/shard_map/ppermute | solution.py:21
  34.3 6.7 %collective-permute-start.10 = (bf16[512,256]{1,0:T(8,128)(2,1)S(1)}, bf16[512,256]{1,0:T(8,128)(2,1)S(1)}, u32[]{:S(2)}, u32[]{:S(2)}) collective-permute-start(bf16[512,256]{1,0:T(8,128)(2,1)S(1)} %collective-permute-done.6), channel_id=1, source_target_pairs={{0,4},{4,8},{8,12},{12,0},{1,5},{5,9},{9,13},{13,1},{2,6},{6,10},{... | collective-permute-start | bytes 786440 | tf_op jit(solution)/shard_map/ppermute | solution.py:21
  42.8 6.6 %collective-permute-start.11 = (f16[512,512]{1,0:T(8,128)(2,1)S(1)}, f16[512,512]{1,0:T(8,128)(2,1)S(1)}, u32[]{:S(2)}, u32[]{:S(2)}) collective-permute-start(f16[512,512]{1,0:T(8,128)(2,1)S(1)} %fusion.5), channel_id=1, source_target_pairs={{0,1},{1,0},{2,3},{3,2},{4,5},{5,4},{6,7},{7,6},{8,9},{9,8},{10,11... | collective-permute-start | bytes 1572872 | tf_op jit(solution)/shard_map/ppermute | solution.py:21
  48.4 4.6 %copy-start.4 = (f32[1024]{0:T(1024)S(1)}, f32[1024]{0:T(1024)}, u32[]{:S(2)}) copy-start(f32[1024]{0:T(1024)} %param.13) | copy-start | bytes 12292
  49.7 9.1 %collective-permute-start.12 = (f16[256,512]{1,0:T(8,128)(2,1)S(1)}, f16[256,512]{1,0:T(8,128)(2,1)S(1)}, u32[]{:S(2)}, u32[]{:S(2)}) collective-permute-start(f16[256,512]{1,0:T(8,128)(2,1)S(1)} %get-tuple-element.29), channel_id=1, source_target_pairs={{0,2},{2,0},{1,3},{3,1},{4,6},{6,4},{5,7},{7,5},{8,10},{10,8},{9,1... | collective-permute-start | bytes 786440 | tf_op jit(solution)/shard_map/ppermute | solution.py:21
  52.4 11.5 %collective-permute-start.13 = (f16[256,512]{1,0:T(8,128)(2,1)S(1)}, f16[256,512]{1,0:T(8,128)(2,1)S(1)}, u32[]{:S(2)}, u32[]{:S(2)}) collective-permute-start(f16[256,512]{1,0:T(8,128)(2,1)S(1)} %get-tuple-element.30), channel_id=1, source_target_pairs={{0,16},{16,0},{1,17},{17,1},{2,18},{18,2},{3,19},{19,3},{4,20},{20... | collective-permute-start | bytes 786440 | tf_op jit(solution)/shard_map/ppermute | solution.py:21
  52.4 12.7 %collective-permute-start.14 = (f16[256,512]{1,0:T(8,128)(2,1)S(1)}, f16[256,512]{1,0:T(8,128)(2,1)S(1)}, u32[]{:S(2)}, u32[]{:S(2)}) collective-permute-start(f16[256,512]{1,0:T(8,128)(2,1)S(1)} %get-tuple-element.30), channel_id=1, source_target_pairs={{0,18},{2,16},{16,2},{18,0},{1,19},{3,17},{17,3},{19,1},{4,22},{6,... | collective-permute-start | bytes 786440 | tf_op jit(solution)/shard_map/ppermute | solution.py:186
  65.4 1.4 %collective-permute-start.15 = (f32[256]{0:T(256)S(1)}, f32[256]{0:T(256)S(1)}, u32[]{:S(2)}, u32[]{:S(2)}) collective-permute-start(f32[256]{0:T(256)S(1)} %get-tuple-element.21), channel_id=1, source_target_pairs={{0,1},{1,0},{2,3},{3,2},{4,5},{5,4},{6,7},{7,6},{8,9},{9,8},{10,11... | collective-permute-start | bytes 3080 | tf_op jit(solution)/shard_map/ppermute | solution.py:21
where the time goes:
time: 67.8 us; the launch traced here: 67.6 us
  starting transfers between devices  23.7 us (35%)
  waiting for transfers between devices  22.3 us (33%)
  Pallas kernels  10.1 us (15%)
  matrix products  5.25 us (8%)
  local copies, waits for them, and re-layouts  3.28 us (5%)
  other arithmetic  2.55 us (4%)
    ppermute x15, starting transfers between devices, moved(): return lax.ppermute(value, axis, [(i, target(i) % n) for i in range(n)])  23.1 us
    ppermute x15, waiting for transfers between devices, moved(): return lax.ppermute(value, axis, [(i, target(i) % n) for i in range(n)])  21.2 us
    pallas_call x1, Pallas kernels, count_blocks(): pl.pallas_call(count_kernel, out_shape=[jax.ShapeDtypeStruct((2 * nodes,...  10.1 us
    dot_general x8, matrix products, shards(): jnp.dot(blocks[i], pieces[i], preferred_element_type=jnp.float32)  4.01 us
    unnamed x12, local copies, waits for them, and re-layouts  2.12 us
  transfers between devices with their start and end apart: 16, of which 9 were waited for; matrix products, arithmetic and copies ran while one was open for 10% of the time, Pallas kernels for 15%

commit v1 on v0

--- a/solution.py
+++ b/solution.py
@@ -1,3 +1,5 @@
+import functools
+
 import jax
 import jax.numpy as jnp
 from jax import lax
@@ -21,10 +23,11 @@
     return lax.ppermute(value, axis, [(i, target(i) % n) for i in range(n)])
 
 
-def count_kernel(here_ref, ids_ref, count_ref, self_ref, *rest):
+def count_kernel(group, n_given, here_ref, ids_ref, count_ref, self_ref, *rest):
+    rest = rest[n_given:]
     out_refs, (turned, code_ref, low_ref, times_ref, own_tile_ref, own_low_ref) = rest[:-6], rest[-6:]
-    nodes = out_refs[0].shape[0] // 2
-    nbr = ids_ref.shape[0]
+    nbr, nodes = ids_ref.shape
+    counts_row, own_row = group * nodes, (2 + group) * nodes
     here = here_ref[0]
     places = [(o, c) for o in range(len(out_refs)) for c in range(0, out_refs[o].shape[1], LANES)]
 
@@ -63,7 +66,7 @@
         )
         return jnp.where(left, first, second).astype(jnp.bfloat16)
 
-    @pl.loop(0, nodes // GROUP)
+    @pl.loop(0, nodes // GROUP, unroll=2)
     def _(g):
         first = pl.multiple_of(g * GROUP, GROUP)
         span = pl.ds(first, GROUP)
@@ -93,8 +96,8 @@
         hit = jnp.where(own_low_ref[span, :] == lane, one, zero)
         for t, (o, col) in enumerate(places):
             block = jnp.concatenate([side[t * EIGHT : t * EIGHT + EIGHT, :] for side in sides], axis=0)
-            out_refs[o][span, col : col + LANES] = block.astype(jnp.bfloat16)
-            out_refs[o][pl.ds(nodes + first, GROUP), col : col + LANES] = jnp.where(
+            out_refs[o][pl.ds(counts_row + first, GROUP), col : col + LANES] = block.astype(jnp.bfloat16)
+            out_refs[o][pl.ds(own_row + first, GROUP), col : col + LANES] = jnp.where(
                 own_tile == jnp.bfloat16(t), hit, zero
             )
 
@@ -111,23 +114,30 @@
     return jnp.where(same, tile, -1), ids & 127
 
 
-def count_blocks(here, ids, counts, own, widths):
-    nodes = ids.shape[1]
+def count_blocks(group, given, here, table, nbr, widths):
+    nodes = table.shape[1]
     vmem = pl.BlockSpec(memory_space=pltpu.VMEM)
     return pl.pallas_call(
-        count_kernel,
-        out_shape=[jax.ShapeDtypeStruct((2 * nodes, w), jnp.bfloat16) for w in widths],
-        in_specs=[pl.BlockSpec(memory_space=pltpu.SMEM)] + [vmem] * 3,
+        functools.partial(count_kernel, group, len(given)),
+        out_shape=[jax.ShapeDtypeStruct((4 * nodes, w), jnp.bfloat16) for w in widths],
+        in_specs=[pl.BlockSpec(memory_space=pltpu.SMEM)] + [vmem] * (3 + len(given)),
         out_specs=[vmem] * len(widths),
+        input_output_aliases={4 + i: i for i in range(len(given))},
         scratch_shapes=[pltpu.VMEM((LANES, LANES), jnp.float32)]
         + [pltpu.VMEM((nodes, LANES), jnp.float32)] * 3
         + [pltpu.VMEM((nodes, LANES), jnp.bfloat16)] * 2,
         compiler_params=pltpu.CompilerParams(vmem_limit_bytes=16 * 2**20),
         cost_estimate=pl.CostEstimate(
-            flops=4_000_000_000, bytes_accessed=9_000_000, transcendentals=0
+            flops=2_000_000_000, bytes_accessed=4_500_000, transcendentals=0
         ),
         name="counts",
-    )(here, ids, counts, own)
+    )(
+        here,
+        table[:nbr],
+        table[nbr : 2 * nbr],
+        table[2 * nbr].reshape(nodes // LANES, LANES),
+        *given,
+    )
 
 
 def shards(items, self_ids, neighbor_ids, visit_counts, w_self, w_neighbor, bias):
@@ -139,28 +149,29 @@
 
     table = jnp.concatenate([neighbor_ids.T, visit_counts.T, self_ids[None, :]], axis=0)
     theirs = moved(table.astype(jnp.int16), "yl", lambda i: i ^ 1).astype(jnp.int32)
-    table = jnp.concatenate([table, theirs], axis=1)
-    ids, counts, own_ids = table[:nbr], table[nbr : 2 * nbr], table[2 * nbr]
 
     axes = [("x", "z"), ("z", "x")]
     halves = [items[:half], items[half:]]
     lines = []
     for block, (near, _) in zip(halves, axes):
         pair = jnp.concatenate([block, moved(block, near, lambda i: i ^ 1)], axis=0)
-        lines.append(jnp.concatenate([pair, moved(pair, near, lambda i: i ^ 3)], axis=0))
+        rest = moved(pair, near, lambda i: i ^ 3)
+        lines.append(jnp.concatenate([pair, rest], axis=0))
     pieces = []
     for line, (_, far) in zip(lines, axes):
         up, down = moved(line, far, lambda i: i + 1), moved(line, far, lambda i: i + 3)
         pieces += [line, up, down, moved(up, far, lambda i: i + 1)]
 
-    blocks = count_blocks(
-        here, ids, counts, own_ids.reshape(-1, LANES), [p.shape[0] for p in pieces]
-    )
+    widths = [p.shape[0] for p in pieces]
+    blocks = count_blocks(0, [], here, table, nbr, widths)
+    blocks = count_blocks(1, blocks, here, theirs, nbr, widths)
     sums = sum(
         jnp.dot(blocks[i], pieces[i], preferred_element_type=jnp.float32)
         for i in (0, 4, 1, 5, 2, 6, 3, 7)
     )
-    total = jnp.sum(counts.astype(jnp.float32), axis=0)
+    total = jnp.concatenate(
+        [jnp.sum(t[nbr : 2 * nbr].astype(jnp.float32), axis=0) for t in (table, theirs)]
+    )
     own = sums[2 * batch :].astype(jnp.bfloat16)
     pooled = sums[: 2 * batch] / total[:, None]
     high = lax.reduce_precision(pooled, 8, 7)
@@ -170,10 +181,11 @@
 
     wide = 2 * share
     weights = jnp.concatenate([w_self, w_neighbor, w_neighbor], axis=0)
-    weights = weights.reshape(3 * share, 2, 2, share)
 
     def columns(which):
-        return lax.dynamic_index_in_dim(weights, which, 2, False).reshape(3 * share, wide)
+        firsts = [which * share, wide + which * share]
+        cut = [lax.dynamic_slice_in_dim(weights, first, share, 1) for first in firsts]
+        return jnp.concatenate(cut, axis=1)
 
     given = jnp.dot(both, columns(1 - core), preferred_element_type=jnp.float32)
     got = moved((given * SCALE).astype(jnp.float16), "core", lambda i: i ^ 1)

time: 67.8 us -> 64.9 us (0.957)
  Pallas kernels: 10.1 us -> 7.52 us
  local copies, waits for them, and re-layouts: 3.28 us -> 2.45 us
    pallas_call x1 -> x2, Pallas kernels: 10.1 us -> 7.52 us  [count_blocks(): pl.pallas_call(functools.partial(count_kernel, group, len(given)), out_sh...]
    another operation x0 -> x2, other arithmetic: none -> 1.59 us
    unnamed x12, local copies, waits for them, and re-layouts: 2.12 us -> 1.14 us
    convert_element_type x1 -> x0, other arithmetic: 0.93 us -> none  [shards(): table.astype(jnp.int16)]
  transfers between devices with their start and end apart: 16 -> 16, of which waited for: 9 -> 9; matrix products, arithmetic and copies ran while one was open for 10% -> 10% of each run, Pallas kernels for 15% -> 12%
where the time goes in v1:
time: 64.9 us; the launch traced here: 64.7 us
  starting transfers between devices  23.7 us (37%)
  waiting for transfers between devices  22.4 us (35%)
  Pallas kernels  7.52 us (12%)
  matrix products  5.19 us (8%)
  other arithmetic  3.13 us (5%)
  local copies, waits for them, and re-layouts  2.45 us (4%)
    ppermute x15, starting transfers between devices, moved(): return lax.ppermute(value, axis, [(i, target(i) % n) for i in range(n)])  23.1 us
    ppermute x15, waiting for transfers between devices, moved(): return lax.ppermute(value, axis, [(i, target(i) % n) for i in range(n)])  21.2 us
    pallas_call x2, Pallas kernels, count_blocks(): pl.pallas_call(functools.partial(count_kernel, group, len(given)), out_sh...  7.52 us
    dot_general x8, matrix products, shards(): jnp.dot(blocks[i], pieces[i], preferred_element_type=jnp.float32)  3.99 us
    another operation x2, other arithmetic  1.59 us
  transfers between devices with their start and end apart: 16, of which 9 were waited for; matrix products, arithmetic and copies ran while one was open for 10% of the time, Pallas kernels for 12%

profile of v1, /device:TPU:1, one launch (start us, length us, event | category | flops | bytes accessed | tf_op | source)
XLA Modules:
  0.0 64.7 jit_solution(9207157647989923451)
XLA Ops:
  0.0 0.7 %convert.15 = s16[256]{0:T(256)(128)(2,1)S(1)} convert(s32[256]{0:T(256)} %param.8) | non-fusion elementwise | flops 256 | bytes 1536 | tf_op jit(solution)/shard_map/convert.4
  0.7 0.9 %bitcast_convert_fusion = (s16[50,256]{1,0:T(8,128)(2,1)S(1)}, s16[50,256]{1,0:T(8,128)(2,1)S(1)}) fusion(s32[256,50]{0,1:T(8,128)} %param.10, s32[256,50]{0,1:T(8,128)} %param.9), kind=kLoop, calls=%fused_computation.51 | loop fusion | flops 25600 | bytes 153600 | tf_op jit(solution)/shard_map/convert.2
  1.6 2.2 %collective-permute-start = (s16[101,256]{1,0:T(8,128)(2,1)S(1)}, s16[101,256]{1,0:T(8,128)(2,1)S(1)}, u32[]{:S(2)}, u32[]{:S(2)}) collective-permute-start(s16[101,256]{1,0:T(8,128)(2,1)S(1)} %pad_add_fusion), channel_id=1, source_target_pairs={{0,16},{16,0},{1,17},{17,1},{2,18},{18,2},{3,19},{19,3},{4,20},{20... | collective-permute-start | bytes 155144 | tf_op jit(solution)/shard_map/ppermute | solution.py:23
  3.8 0.9 %fusion.26 = (bf16[128,256]{1,0:T(8,128)(2,1)S(1)}, bf16[128,256]{1,0:T(8,128)(2,1)S(1)}) fusion(bf16[256,256]{1,0:T(8,128)(2,1)} %param.7), kind=kLoop, calls=%fused_computation.56 | loop fusion | bytes 262144 | tf_op jit(solution)/shard_map/slice | solution.py:154
  4.7 1.3 %collective-permute-start.1 = (bf16[128,256]{1,0:T(8,128)(2,1)S(1)}, bf16[128,256]{1,0:T(8,128)(2,1)S(1)}, u32[]{:S(2)}, u32[]{:S(2)}) collective-permute-start(bf16[128,256]{1,0:T(8,128)(2,1)S(1)} %get-tuple-element.49), channel_id=1, source_target_pairs={{0,4},{4,0},{8,12},{12,8},{1,5},{5,1},{9,13},{13,9},{2,6},{6,2},{1... | collective-permute-start | bytes 196616 | tf_op jit(solution)/shard_map/ppermute | solution.py:23
  6.0 1.6 %collective-permute-start.3 = (bf16[128,256]{1,0:T(8,128)(2,1)S(1)}, bf16[128,256]{1,0:T(8,128)(2,1)S(1)}, u32[]{:S(2)}, u32[]{:S(2)}) collective-permute-start(bf16[128,256]{1,0:T(8,128)(2,1)S(1)} %get-tuple-element.50), channel_id=1, source_target_pairs={{0,32},{32,0},{64,96},{96,64},{1,33},{33,1},{65,97},{97,65},{2,34}... | collective-permute-start | bytes 196616 | tf_op jit(solution)/shard_map/ppermute | solution.py:23
  7.6 1.1 %constant_dynamic-update-slice_fusion.2 = bf16[768,1024]{1,0:T(8,128)(2,1)S(1)} fusion(bf16[256,1024]{1,0:T(8,128)(2,1)} %param.11), kind=kLoop, calls=%fused_computation.41 | loop fusion | bytes 1048576
  8.9 3.8 %counts.2 = (bf16[1024,512]{1,0:T(8,128)(2,1)S(1)}, bf16[1024,512]{1,0:T(8,128)(2,1)S(1)}, bf16[1024,512]{1,0:T(8,128)(2,1)S(1)}, bf16[1024,512]{1,0:T(8,128)(2,...) custom-call(s32[1]{0:T(128)} %bitcast.here_ref, ...), custom_call_target="tpu_custom_call" | custom-call | flops 2000000000 | bytes 4500000 | tf_op jit(solution)/shard_map/counts/pallas_call | solution.py:120
  12.9 3.8 %counts.3 = (bf16[1024,512]{1,0:T(8,128)(2,1)S(1)}, bf16[1024,512]{1,0:T(8,128)(2,1)S(1)}, bf16[1024,512]{1,0:T(8,128)(2,1)S(1)}, bf16[1024,512]{1,0:T(8,128)(2,...) custom-call(s32[1]{0:T(128)} %bitcast.here_ref, ...), custom_call_target="tpu_custom_call", output_to_operand_aliasing={{0}: (4, {}), {1}: (5, {}), {2}: (6, {}), {3}: (7, {}), {4}... | custom-call | flops 2000000000 | bytes 4500000 | tf_op jit(solution)/shard_map/counts/pallas_call | solution.py:120
  16.8 1.9 %collective-permute-start.2 = (bf16[256,256]{1,0:T(8,128)(2,1)S(1)}, bf16[256,256]{1,0:T(8,128)(2,1)S(1)}, u32[]{:S(2)}, u32[]{:S(2)}) collective-permute-start(bf16[256,256]{1,0:T(8,128)(2,1)S(1)} %pad_maximum_fusion.5), channel_id=1, source_target_pairs={{0,12},{4,8},{8,4},{12,0},{1,13},{5,9},{9,5},{13,1},{2,14},{6,10},... | collective-permute-start | bytes 393224 | tf_op jit(solution)/shard_map/ppermute | solution.py:23
  18.7 2.3 %collective-permute-start.4 = (bf16[256,256]{1,0:T(8,128)(2,1)S(1)}, bf16[256,256]{1,0:T(8,128)(2,1)S(1)}, u32[]{:S(2)}, u32[]{:S(2)}) collective-permute-start(bf16[256,256]{1,0:T(8,128)(2,1)S(1)} %pad_maximum_fusion.6), channel_id=1, source_target_pairs={{0,96},{32,64},{64,32},{96,0},{1,97},{33,65},{65,33},{97,1},{2,98}... | collective-permute-start | bytes 393224 | tf_op jit(solution)/shard_map/ppermute | solution.py:23
  21.0 0.9 %collective-permute-done.2 = bf16[256,256]{1,0:T(8,128)(2,1)S(1)} collective-permute-done((bf16[256,256]{1,0:T(8,128)(2,1)S(1)}, bf16[256,256]{1,0:T(8,128)(2,1)S(1)}, u32[]{:S(2)}, u32[]{:S(2)}) %collective-permute-start.2) | collective-permute-done | bytes 131104 | tf_op jit(solution)/shard_map/ppermute | solution.py:23
  22.0 2.7 %collective-permute-start.7 = (bf16[512,256]{1,0:T(8,128)(2,1)S(1)}, bf16[512,256]{1,0:T(8,128)(2,1)S(1)}, u32[]{:S(2)}, u32[]{:S(2)}) collective-permute-start(bf16[512,256]{1,0:T(8,128)(2,1)S(1)} %pad_maximum_fusion.3), channel_id=1, source_target_pairs={{0,96},{32,0},{64,32},{96,64},{1,97},{33,1},{65,33},{97,65},{2,98}... | collective-permute-start | bytes 786440 | tf_op jit(solution)/shard_map/ppermute | solution.py:23
  24.8 2.7 %collective-permute-start.8 = (bf16[512,256]{1,0:T(8,128)(2,1)S(1)}, bf16[512,256]{1,0:T(8,128)(2,1)S(1)}, u32[]{:S(2)}, u32[]{:S(2)}) collective-permute-start(bf16[512,256]{1,0:T(8,128)(2,1)S(1)} %pad_maximum_fusion.4), channel_id=1, source_target_pairs={{0,12},{4,0},{8,4},{12,8},{1,13},{5,1},{9,5},{13,9},{2,14},{6,2},{... | collective-permute-start | bytes 786440 | tf_op jit(solution)/shard_map/ppermute | solution.py:23
  27.4 0.5 fusion.22
  27.9 1.4 %collective-permute-done.5 = bf16[512,256]{1,0:T(8,128)(2,1)S(1)} collective-permute-done((bf16[512,256]{1,0:T(8,128)(2,1)S(1)}, bf16[512,256]{1,0:T(8,128)(2,1)S(1)}, u32[]{:S(2)}, u32[]{:S(2)}) %collective-permute-start.5) | collective-permute-done | bytes 262176 | tf_op jit(solution)/shard_map/ppermute | solution.py:23
  29.8 1.7 %collective-permute-done.6 = bf16[512,256]{1,0:T(8,128)(2,1)S(1)} collective-permute-done((bf16[512,256]{1,0:T(8,128)(2,1)S(1)}, bf16[512,256]{1,0:T(8,128)(2,1)S(1)}, u32[]{:S(2)}, u32[]{:S(2)}) %collective-permute-start.6) | collective-permute-done | bytes 262176 | tf_op jit(solution)/shard_map/ppermute | solution.py:23
  33.0 0.6 fusion.4
  33.6 4.6 %collective-permute-done.10 = bf16[512,256]{1,0:T(8,128)(2,1)S(1)} collective-permute-done((bf16[512,256]{1,0:T(8,128)(2,1)S(1)}, bf16[512,256]{1,0:T(8,128)(2,1)S(1)}, u32[]{:S(2)}, u32[]{:S(2)}) %collective-permute-start.10) | collective-permute-done | bytes 262176 | tf_op jit(solution)/shard_map/ppermute | solution.py:23
  38.7 0.5 fusion
  39.3 0.6 fusion.5
  40.0 5.0 %collective-permute-start.11 = (f16[512,512]{1,0:T(8,128)(2,1)S(1)}, f16[512,512]{1,0:T(8,128)(2,1)S(1)}, u32[]{:S(2)}, u32[]{:S(2)}) collective-permute-start(f16[512,512]{1,0:T(8,128)(2,1)S(1)} %fusion.5), channel_id=1, source_target_pairs={{0,1},{1,0},{2,3},{3,2},{4,5},{5,4},{6,7},{7,6},{8,9},{9,8},{10,11... | collective-permute-start | bytes 1572872 | tf_op jit(solution)/shard_map/ppermute | solution.py:23
  45.0 0.6 fusion.6
  45.6 0.9 %collective-permute-done.11 = f16[512,512]{1,0:T(8,128)(2,1)S(1)} collective-permute-done((f16[512,512]{1,0:T(8,128)(2,1)S(1)}, f16[512,512]{1,0:T(8,128)(2,1)S(1)}, u32[]{:S(2)}, u32[]{:S(2)}) %collective-permute-start.11) | collective-permute-done | bytes 524320 | tf_op jit(solution)/shard_map/ppermute | solution.py:23
  46.8 2.7 %collective-permute-start.12 = (f16[256,512]{1,0:T(8,128)(2,1)S(1)}, f16[256,512]{1,0:T(8,128)(2,1)S(1)}, u32[]{:S(2)}, u32[]{:S(2)}) collective-permute-start(f16[256,512]{1,0:T(8,128)(2,1)S(1)} %get-tuple-element.47), channel_id=1, source_target_pairs={{0,2},{2,0},{1,3},{3,1},{4,6},{6,4},{5,7},{7,5},{8,10},{10,8},{9,1... | collective-permute-start | bytes 786440 | tf_op jit(solution)/shard_map/ppermute | solution.py:23
  49.5 0.6 collective-permute-start.14
  50.2 5.8 %collective-permute-done.12 = f16[256,512]{1,0:T(8,128)(2,1)S(1)} collective-permute-done((f16[256,512]{1,0:T(8,128)(2,1)S(1)}, f16[256,512]{1,0:T(8,128)(2,1)S(1)}, u32[]{:S(2)}, u32[]{:S(2)}) %collective-permute-start.12) | collective-permute-done | bytes 262176 | tf_op jit(solution)/shard_map/ppermute | solution.py:23
  55.9 5.1 %collective-permute-done.13 = f16[256,512]{1,0:T(8,128)(2,1)S(1)} collective-permute-done((f16[256,512]{1,0:T(8,128)(2,1)S(1)}, f16[256,512]{1,0:T(8,128)(2,1)S(1)}, u32[]{:S(2)}, u32[]{:S(2)}) %collective-permute-start.13) | collective-permute-done | bytes 262176 | tf_op jit(solution)/shard_map/ppermute | solution.py:23
  61.1 1.2 %collective-permute-done.14 = f16[256,512]{1,0:T(8,128)(2,1)S(1)} collective-permute-done((f16[256,512]{1,0:T(8,128)(2,1)S(1)}, f16[256,512]{1,0:T(8,128)(2,1)S(1)}, u32[]{:S(2)}, u32[]{:S(2)}) %collective-permute-start.14) | collective-permute-done | bytes 262176 | tf_op jit(solution)/shard_map/ppermute | solution.py:198
  62.5 0.6 collective-permute-start.15
  63.1 0.8 %collective-permute-done.15 = f32[256]{0:T(256)S(1)} collective-permute-done((f32[256]{0:T(256)S(1)}, f32[256]{0:T(256)S(1)}, u32[]{:S(2)}, u32[]{:S(2)}) %collective-permute-start.15) | collective-permute-done | bytes 1056 | tf_op jit(solution)/shard_map/ppermute | solution.py:23
  63.9 0.8 %fusion.19 = f32[256,256]{1,0:T(8,128)} fusion(f32[256,512]{1,0:T(8,128)S(1)} %get-tuple-element.38, f32[256]{0:T(256)S(1)} %add_sqrt_fusion, pred[]{:T(512)S(6)} %eq.3), kind=kLoop, calls=%fused_computation.31 | loop fusion | flops 131072 | bytes 787457 | tf_op jit(solution)/shard_map/div | solution.py:207
  (50 shorter events, 3.8 us)
Async XLA Ops:
  0.0 8.7 %copy-start.3 = (bf16[256,1024]{1,0:T(8,128)(2,1)S(1)}, bf16[256,1024]{1,0:T(8,128)(2,1)}, u32[]{:S(2)}) copy-start(bf16[256,1024]{1,0:T(8,128)(2,1)} %param.12) | copy-start | bytes 1572868
  1.6 11.3 %collective-permute-start = (s16[101,256]{1,0:T(8,128)(2,1)S(1)}, s16[101,256]{1,0:T(8,128)(2,1)S(1)}, u32[]{:S(2)}, u32[]{:S(2)}) collective-permute-start(s16[101,256]{1,0:T(8,128)(2,1)S(1)} %pad_add_fusion), channel_id=1, source_target_pairs={{0,16},{16,0},{1,17},{17,1},{2,18},{18,2},{3,19},{19,3},{4,20},{20... | collective-permute-start | bytes 155144 | tf_op jit(solution)/shard_map/ppermute | solution.py:23
  4.7 12.0 %collective-permute-start.1 = (bf16[128,256]{1,0:T(8,128)(2,1)S(1)}, bf16[128,256]{1,0:T(8,128)(2,1)S(1)}, u32[]{:S(2)}, u32[]{:S(2)}) collective-permute-start(bf16[128,256]{1,0:T(8,128)(2,1)S(1)} %get-tuple-element.49), channel_id=1, source_target_pairs={{0,4},{4,0},{8,12},{12,8},{1,5},{5,1},{9,13},{13,9},{2,6},{6,2},{1... | collective-permute-start | bytes 196616 | tf_op jit(solution)/shard_map/ppermute | solution.py:23
  6.0 12.7 %collective-permute-start.3 = (bf16[128,256]{1,0:T(8,128)(2,1)S(1)}, bf16[128,256]{1,0:T(8,128)(2,1)S(1)}, u32[]{:S(2)}, u32[]{:S(2)}) collective-permute-start(bf16[128,256]{1,0:T(8,128)(2,1)S(1)} %get-tuple-element.50), channel_id=1, source_target_pairs={{0,32},{32,0},{64,96},{96,64},{1,33},{33,1},{65,97},{97,65},{2,34}... | collective-permute-start | bytes 196616 | tf_op jit(solution)/shard_map/ppermute | solution.py:23
  7.6 1.2 %copy-start = (s32[256,50]{0,1:T(8,128)S(1)}, s32[256,50]{0,1:T(8,128)}, u32[]{:S(2)}) copy-start(s32[256,50]{0,1:T(8,128)} %param.10) | copy-start | bytes 153604
  7.6 1.2 %copy-start.1 = (s32[256,50]{0,1:T(8,128)S(1)}, s32[256,50]{0,1:T(8,128)}, u32[]{:S(2)}) copy-start(s32[256,50]{0,1:T(8,128)} %param.9) | copy-start | bytes 153604
  7.6 1.2 %copy-start.2 = (s32[256]{0:T(256)S(1)}, s32[256]{0:T(256)}, u32[]{:S(2)}) copy-start(s32[256]{0:T(256)} %param.8) | copy-start | bytes 3076
  16.8 5.1 %collective-permute-start.2 = (bf16[256,256]{1,0:T(8,128)(2,1)S(1)}, bf16[256,256]{1,0:T(8,128)(2,1)S(1)}, u32[]{:S(2)}, u32[]{:S(2)}) collective-permute-start(bf16[256,256]{1,0:T(8,128)(2,1)S(1)} %pad_maximum_fusion.5), channel_id=1, source_target_pairs={{0,12},{4,8},{8,4},{12,0},{1,13},{5,9},{9,5},{13,1},{2,14},{6,10},... | collective-permute-start | bytes 393224 | tf_op jit(solution)/shard_map/ppermute | solution.py:23
  18.7 6.0 %collective-permute-start.4 = (bf16[256,256]{1,0:T(8,128)(2,1)S(1)}, bf16[256,256]{1,0:T(8,128)(2,1)S(1)}, u32[]{:S(2)}, u32[]{:S(2)}) collective-permute-start(bf16[256,256]{1,0:T(8,128)(2,1)S(1)} %pad_maximum_fusion.6), channel_id=1, source_target_pairs={{0,96},{32,64},{64,32},{96,0},{1,97},{33,65},{65,33},{97,1},{2,98}... | collective-permute-start | bytes 393224 | tf_op jit(solution)/shard_map/ppermute | solution.py:23
  21.9 7.4 %collective-permute-start.5 = (bf16[512,256]{1,0:T(8,128)(2,1)S(1)}, bf16[512,256]{1,0:T(8,128)(2,1)S(1)}, u32[]{:S(2)}, u32[]{:S(2)}) collective-permute-start(bf16[512,256]{1,0:T(8,128)(2,1)S(1)} %pad_maximum_fusion.3), channel_id=1, source_target_pairs={{0,32},{32,64},{64,96},{96,0},{1,33},{33,65},{65,97},{97,1},{2,34}... | collective-permute-start | bytes 786440 | tf_op jit(solution)/shard_map/ppermute | solution.py:23
  22.0 10.0 %collective-permute-start.7 = (bf16[512,256]{1,0:T(8,128)(2,1)S(1)}, bf16[512,256]{1,0:T(8,128)(2,1)S(1)}, u32[]{:S(2)}, u32[]{:S(2)}) collective-permute-start(bf16[512,256]{1,0:T(8,128)(2,1)S(1)} %pad_maximum_fusion.3), channel_id=1, source_target_pairs={{0,96},{32,0},{64,32},{96,64},{1,97},{33,1},{65,33},{97,65},{2,98}... | collective-permute-start | bytes 786440 | tf_op jit(solution)/shard_map/ppermute | solution.py:23
  24.7 6.8 %collective-permute-start.6 = (bf16[512,256]{1,0:T(8,128)(2,1)S(1)}, bf16[512,256]{1,0:T(8,128)(2,1)S(1)}, u32[]{:S(2)}, u32[]{:S(2)}) collective-permute-start(bf16[512,256]{1,0:T(8,128)(2,1)S(1)} %pad_maximum_fusion.4), channel_id=1, source_target_pairs={{0,4},{4,8},{8,12},{12,0},{1,5},{5,9},{9,13},{13,1},{2,6},{6,10},{... | collective-permute-start | bytes 786440 | tf_op jit(solution)/shard_map/ppermute | solution.py:23
  24.8 7.7 %collective-permute-start.8 = (bf16[512,256]{1,0:T(8,128)(2,1)S(1)}, bf16[512,256]{1,0:T(8,128)(2,1)S(1)}, u32[]{:S(2)}, u32[]{:S(2)}) collective-permute-start(bf16[512,256]{1,0:T(8,128)(2,1)S(1)} %pad_maximum_fusion.4), channel_id=1, source_target_pairs={{0,12},{4,0},{8,4},{12,8},{1,13},{5,1},{9,5},{13,9},{2,14},{6,2},{... | collective-permute-start | bytes 786440 | tf_op jit(solution)/shard_map/ppermute | solution.py:23
  29.3 9.4 %collective-permute-start.9 = (bf16[512,256]{1,0:T(8,128)(2,1)S(1)}, bf16[512,256]{1,0:T(8,128)(2,1)S(1)}, u32[]{:S(2)}, u32[]{:S(2)}) collective-permute-start(bf16[512,256]{1,0:T(8,128)(2,1)S(1)} %collective-permute-done.5), channel_id=1, source_target_pairs={{0,32},{32,64},{64,96},{96,0},{1,33},{33,65},{65,97},{97,1},{2,34}... | collective-permute-start | bytes 786440 | tf_op jit(solution)/shard_map/ppermute | solution.py:23
  31.5 6.7 %collective-permute-start.10 = (bf16[512,256]{1,0:T(8,128)(2,1)S(1)}, bf16[512,256]{1,0:T(8,128)(2,1)S(1)}, u32[]{:S(2)}, u32[]{:S(2)}) collective-permute-start(bf16[512,256]{1,0:T(8,128)(2,1)S(1)} %collective-permute-done.6), channel_id=1, source_target_pairs={{0,4},{4,8},{8,12},{12,0},{1,5},{5,9},{9,13},{13,1},{2,6},{6,10},{... | collective-permute-start | bytes 786440 | tf_op jit(solution)/shard_map/ppermute | solution.py:23
  40.0 6.6 %collective-permute-start.11 = (f16[512,512]{1,0:T(8,128)(2,1)S(1)}, f16[512,512]{1,0:T(8,128)(2,1)S(1)}, u32[]{:S(2)}, u32[]{:S(2)}) collective-permute-start(f16[512,512]{1,0:T(8,128)(2,1)S(1)} %fusion.5), channel_id=1, source_target_pairs={{0,1},{1,0},{2,3},{3,2},{4,5},{5,4},{6,7},{7,6},{8,9},{9,8},{10,11... | collective-permute-start | bytes 1572872 | tf_op jit(solution)/shard_map/ppermute | solution.py:23
  45.6 4.6 %copy-start.4 = (f32[1024]{0:T(1024)S(1)}, f32[1024]{0:T(1024)}, u32[]{:S(2)}) copy-start(f32[1024]{0:T(1024)} %param.13) | copy-start | bytes 12292
  46.8 9.1 %collective-permute-start.12 = (f16[256,512]{1,0:T(8,128)(2,1)S(1)}, f16[256,512]{1,0:T(8,128)(2,1)S(1)}, u32[]{:S(2)}, u32[]{:S(2)}) collective-permute-start(f16[256,512]{1,0:T(8,128)(2,1)S(1)} %get-tuple-element.47), channel_id=1, source_target_pairs={{0,2},{2,0},{1,3},{3,1},{4,6},{6,4},{5,7},{7,5},{8,10},{10,8},{9,1... | collective-permute-start | bytes 786440 | tf_op jit(solution)/shard_map/ppermute | solution.py:23
  49.5 11.5 %collective-permute-start.13 = (f16[256,512]{1,0:T(8,128)(2,1)S(1)}, f16[256,512]{1,0:T(8,128)(2,1)S(1)}, u32[]{:S(2)}, u32[]{:S(2)}) collective-permute-start(f16[256,512]{1,0:T(8,128)(2,1)S(1)} %get-tuple-element.48), channel_id=1, source_target_pairs={{0,16},{16,0},{1,17},{17,1},{2,18},{18,2},{3,19},{19,3},{4,20},{20... | collective-permute-start | bytes 786440 | tf_op jit(solution)/shard_map/ppermute | solution.py:23
  49.5 12.7 %collective-permute-start.14 = (f16[256,512]{1,0:T(8,128)(2,1)S(1)}, f16[256,512]{1,0:T(8,128)(2,1)S(1)}, u32[]{:S(2)}, u32[]{:S(2)}) collective-permute-start(f16[256,512]{1,0:T(8,128)(2,1)S(1)} %get-tuple-element.48), channel_id=1, source_target_pairs={{0,18},{2,16},{16,2},{18,0},{1,19},{3,17},{17,3},{19,1},{4,22},{6,... | collective-permute-start | bytes 786440 | tf_op jit(solution)/shard_map/ppermute | solution.py:198
  62.5 1.4 %collective-permute-start.15 = (f32[256]{0:T(256)S(1)}, f32[256]{0:T(256)S(1)}, u32[]{:S(2)}, u32[]{:S(2)}) collective-permute-start(f32[256]{0:T(256)S(1)} %get-tuple-element.37), channel_id=1, source_target_pairs={{0,1},{1,0},{2,3},{3,2},{4,5},{5,4},{6,7},{7,6},{8,9},{9,8},{10,11... | collective-permute-start | bytes 3080 | tf_op jit(solution)/shard_map/ppermute | solution.py:23

commit v2 on v1

--- a/solution.py
+++ b/solution.py
@@ -12,7 +12,8 @@
 DOM = ("z", "yl", "x")
 LANES = 128
 SLOTS = 64
-TILES = 32
+TILES = 16
+WIDE = 2 * LANES
 EIGHT = 8
 GROUP = 16
 SCALE = 16.0
@@ -29,10 +30,13 @@
     nbr, nodes = ids_ref.shape
     counts_row, own_row = group * nodes, (2 + group) * nodes
     here = here_ref[0]
-    places = [(o, c) for o in range(len(out_refs)) for c in range(0, out_refs[o].shape[1], LANES)]
+    places = [(o, c) for o in range(len(out_refs)) for c in range(0, out_refs[o].shape[1], WIDE)]
 
     def column(row):
         return jnp.broadcast_to(row.astype(jnp.float32), (LANES, LANES)).T.astype(jnp.bfloat16)
+
+    def widened(value):
+        return jnp.concatenate([value] * (WIDE // LANES), axis=1)
 
     node = lax.broadcasted_iota(jnp.int32, (nbr, LANES), 1) & (EIGHT - 1)
     for part in range(nodes // LANES):
@@ -53,9 +57,9 @@
         own_low_ref[span, :] = column(own_low)
 
     row = lax.broadcasted_iota(jnp.int32, (GROUP, LANES), 0).astype(jnp.float32)
-    rows = [(row + r * GROUP).astype(jnp.bfloat16) for r in range(TILES * EIGHT // GROUP)]
-    lane = lax.broadcasted_iota(jnp.int32, (GROUP, LANES), 1)
-    left = lane < SLOTS
+    rows = [(row + r * GROUP).astype(jnp.bfloat16) for r in range(WIDE // GROUP)]
+    left = lax.broadcasted_iota(jnp.int32, (GROUP, LANES), 1) < SLOTS
+    lane = lax.broadcasted_iota(jnp.int32, (GROUP, WIDE), 1)
     lane = lane.astype(jnp.float32).astype(jnp.bfloat16)
     zero = jnp.zeros((GROUP, LANES), jnp.bfloat16)
     one = jnp.ones((GROUP, LANES), jnp.bfloat16)
@@ -77,12 +81,13 @@
             for n in range(eight, eight + EIGHT, 2):
                 code, low, times = (pair(t, n) for t in tables)
                 marks.append(
-                    jnp.concatenate([jnp.where(code == r, times, zero) for r in rows], axis=0)
+                    jnp.concatenate(
+                        [jnp.where(code == r, times, zero) for r in rows[: TILES * EIGHT // GROUP]],
+                        axis=0,
+                    )
                 )
                 lows.append(
-                    jnp.concatenate(
-                        [jnp.where(low == r, one, zero) for r in rows[: LANES // GROUP]], axis=0
-                    )
+                    jnp.concatenate([jnp.where(low == r, one, zero) for r in rows], axis=0)
                 )
             sides.append(
                 lax.dot_general(
@@ -92,13 +97,13 @@
                     preferred_element_type=jnp.float32,
                 )
             )
-        own_tile = own_tile_ref[span, :]
-        hit = jnp.where(own_low_ref[span, :] == lane, one, zero)
+        own_tile = widened(own_tile_ref[span, :])
+        hit = jnp.where(widened(own_low_ref[span, :]) == lane, widened(one), widened(zero))
         for t, (o, col) in enumerate(places):
             block = jnp.concatenate([side[t * EIGHT : t * EIGHT + EIGHT, :] for side in sides], axis=0)
-            out_refs[o][pl.ds(counts_row + first, GROUP), col : col + LANES] = block.astype(jnp.bfloat16)
-            out_refs[o][pl.ds(own_row + first, GROUP), col : col + LANES] = jnp.where(
-                own_tile == jnp.bfloat16(t), hit, zero
+            out_refs[o][pl.ds(counts_row + first, GROUP), col : col + WIDE] = block.astype(jnp.bfloat16)
+            out_refs[o][pl.ds(own_row + first, GROUP), col : col + WIDE] = jnp.where(
+                own_tile == jnp.bfloat16(t), hit, widened(zero)
             )
 
 
@@ -111,7 +116,7 @@
     far = jnp.where(first_half, dz, dx)
     near = jnp.where(first_half, here ^ block, (here ^ block) >> 3) & 3
     tile = jnp.where(first_half, 0, 16) + (far ^ (far >> 1)) * 4 + (near ^ (near >> 1))
-    return jnp.where(same, tile, -1), ids & 127
+    return jnp.where(same, tile >> 1, -1), ((tile & 1) << 7) + (ids & 127)
 
 
 def count_blocks(group, given, here, table, nbr, widths):
@@ -140,6 +145,39 @@
     )
 
 
+def project_kernel(which_ref, sums_ref, total_ref, self_ref, nbr_ref, out_ref):
+    nodes, share = sums_ref.shape[0] // 2, sums_ref.shape[1]
+    total = jnp.concatenate([total_ref[...]] * (share // LANES), axis=1)
+    own = sums_ref[nodes:, :].astype(jnp.bfloat16)
+    pooled = sums_ref[:nodes, :] / total
+    high = pooled.astype(jnp.bfloat16)
+    low = (pooled - high.astype(jnp.float32)).astype(jnp.bfloat16)
+    for part in range(2):
+        first = pl.multiple_of(part * 2 * share + which_ref[0] * share, share)
+        columns = pl.ds(first, share)
+        w_self, w_nbr = self_ref[:, columns], nbr_ref[:, columns]
+        out = jnp.dot(own, w_self, preferred_element_type=jnp.float32)
+        out += jnp.dot(high, w_nbr, preferred_element_type=jnp.float32)
+        out += jnp.dot(low, w_nbr, preferred_element_type=jnp.float32)
+        out_ref[:, part * share : (part + 1) * share] = out * SCALE
+
+
+def projected(which, sums, total, w_self, w_neighbor):
+    nodes, share = sums.shape[0] // 2, sums.shape[1]
+    vmem = pl.BlockSpec(memory_space=pltpu.VMEM)
+    return pl.pallas_call(
+        project_kernel,
+        out_shape=jax.ShapeDtypeStruct((nodes, 2 * share), jnp.float32),
+        in_specs=[pl.BlockSpec(memory_space=pltpu.SMEM)] + [vmem] * 4,
+        out_specs=vmem,
+        compiler_params=pltpu.CompilerParams(vmem_limit_bytes=12 * 2**20),
+        cost_estimate=pl.CostEstimate(
+            flops=400_000_000, bytes_accessed=4_000_000, transcendentals=0
+        ),
+        name="project",
+    )(which.reshape(1), sums, total, w_self, w_neighbor)
+
+
 def shards(items, self_ids, neighbor_ids, visit_counts, w_self, w_neighbor, bias):
     core, yh = lax.axis_index("core"), lax.axis_index("yh")
     batch, share = self_ids.shape[0], items.shape[1]
@@ -169,29 +207,15 @@
         jnp.dot(blocks[i], pieces[i], preferred_element_type=jnp.float32)
         for i in (0, 4, 1, 5, 2, 6, 3, 7)
     )
+    wide = 2 * share
     total = jnp.concatenate(
         [jnp.sum(t[nbr : 2 * nbr].astype(jnp.float32), axis=0) for t in (table, theirs)]
     )
-    own = sums[2 * batch :].astype(jnp.bfloat16)
-    pooled = sums[: 2 * batch] / total[:, None]
-    high = lax.reduce_precision(pooled, 8, 7)
-    both = jnp.concatenate(
-        [own, high.astype(jnp.bfloat16), (pooled - high).astype(jnp.bfloat16)], axis=1
-    )
-
-    wide = 2 * share
-    weights = jnp.concatenate([w_self, w_neighbor, w_neighbor], axis=0)
-
-    def columns(which):
-        firsts = [which * share, wide + which * share]
-        cut = [lax.dynamic_slice_in_dim(weights, first, share, 1) for first in firsts]
-        return jnp.concatenate(cut, axis=1)
-
-    given = jnp.dot(both, columns(1 - core), preferred_element_type=jnp.float32)
-    got = moved((given * SCALE).astype(jnp.float16), "core", lambda i: i ^ 1)
-    kept = jnp.dot(both, columns(core), preferred_element_type=jnp.float32)
-    kept = lax.optimization_barrier(kept)
-    chip = kept * SCALE + got.astype(jnp.float32)
+    total = jnp.broadcast_to(total[:, None], (2 * batch, LANES))
+    given = projected(1 - core, sums, total, w_self, w_neighbor)
+    got = moved(given.astype(jnp.float16), "core", lambda i: i ^ 1)
+    kept = projected(core, sums, total, w_self, w_neighbor)
+    chip = kept + got.astype(jnp.float32)
     sent = chip.astype(jnp.float16)
     from_yh = moved(sent[:batch], "yh", lambda i: i ^ 1)
     from_yl = moved(sent[batch:], "yl", lambda i: i ^ 1)

time: 64.9 us -> 77.3 us (1.19)
  local copies, waits for them, and re-layouts: 2.45 us -> 13.4 us
  Pallas kernels: 7.52 us -> 9.37 us
  matrix products: 5.19 us -> 3.57 us
  other arithmetic: 3.13 us -> 4.53 us
    unnamed x12 -> x38, local copies, waits for them, and re-layouts: 1.14 us -> 13.2 us
    dot_general x2 -> x0, matrix products: 1.19 us -> none  [the longest x1 0.6 us: shards(): given = jnp.dot(both, columns(1 - core), preferred_element_type=jnp.float32)]
    pallas_call x0 -> x2, Pallas kernels: none -> 1.18 us  [projected(): pl.pallas_call(project_kernel, out_shape=jax.ShapeDtypeStruct((nodes, 2 *...]
    slice x1, local copies, waits for them, and re-layouts: 0.88 us -> 0.01 us  [shards(): halves = [items[:half], items[half:]]]
    convert_element_type x1, other arithmetic: 0.02 us -> 0.82 us  [shards(): moved(table.astype(jnp.int16), 'yl', lambda i: i ^ 1).astype(jnp.int32)]
  transfers between devices with their start and end apart: 16 -> 16, of which waited for: 9 -> 9; matrix products, arithmetic and copies ran while one was open for 10% -> 5% of each run, Pallas kernels for 12% -> 11%
where the time goes in v2:
time: 77.3 us; the launch traced here: 76.8 us
  starting transfers between devices  23.7 us (31%)
  waiting for transfers between devices  21.9 us (28%)
  local copies, waits for them, and re-layouts  13.4 us (17%)
  Pallas kernels  9.37 us (12%)
  other arithmetic  4.53 us (6%)
  matrix products  3.57 us (5%)
    ppermute x15, starting transfers between devices, moved(): return lax.ppermute(value, axis, [(i, target(i) % n) for i in range(n)])  23 us
    ppermute x15, waiting for transfers between devices, moved(): return lax.ppermute(value, axis, [(i, target(i) % n) for i in range(n)])  20.7 us
    unnamed x38, local copies, waits for them, and re-layouts  13.2 us
    pallas_call x2, Pallas kernels, count_blocks(): pl.pallas_call(functools.partial(count_kernel, group, len(given)), out_sh...  8.19 us
    dot_general x8, matrix products, shards(): jnp.dot(blocks[i], pieces[i], preferred_element_type=jnp.float32)  3.57 us
    another operation x2, other arithmetic  1.57 us
  transfers between devices with their start and end apart: 16, of which 9 were waited for; matrix products, arithmetic and copies ran while one was open for 5% of the time, Pallas kernels for 11%

profile of v2, /device:TPU:1, one launch (start us, length us, event | category | flops | bytes accessed | tf_op | source)
XLA Modules:
  0.0 76.8 jit_solution(3638654234887262788)
XLA Ops:
  0.7 0.9 %bitcast_convert_fusion = (s16[50,256]{1,0:T(8,128)(2,1)S(1)}, s16[50,256]{1,0:T(8,128)(2,1)S(1)}) fusion(s32[256,50]{0,1:T(8,128)} %param.10, s32[256,50]{0,1:T(8,128)} %param.9), kind=kLoop, calls=%fused_computation.27 | loop fusion | flops 25600 | bytes 153600 | tf_op jit(solution)/shard_map/convert.1
  2.2 2.1 %collective-permute-start = (s16[101,256]{1,0:T(8,128)(2,1)}, s16[101,256]{1,0:T(8,128)(2,1)}, u32[]{:S(2)}, u32[]{:S(2)}) collective-permute-start(s16[101,256]{1,0:T(8,128)(2,1)} %pad_add_fusion), channel_id=1, source_target_pairs={{0,16},{16,0},{1,17},{17,1},{2,18},{18,2},{3,19},{19,3},{4,20},{20... | collective-permute-start | bytes 155144 | tf_op jit(solution)/shard_map/ppermute | solution.py:24
  4.4 1.3 %collective-permute-start.1 = (bf16[128,256]{1,0:T(8,128)(2,1)S(1)}, bf16[128,256]{1,0:T(8,128)(2,1)S(1)}, u32[]{:S(2)}, u32[]{:S(2)}) collective-permute-start(bf16[128,256]{1,0:T(8,128)(2,1)S(1)} %get-tuple-element.43), channel_id=1, source_target_pairs={{0,4},{4,0},{8,12},{12,8},{1,5},{5,1},{9,13},{13,9},{2,6},{6,2},{1... | collective-permute-start | bytes 196616 | tf_op jit(solution)/shard_map/ppermute | solution.py:24
  5.6 1.6 %collective-permute-start.3 = (bf16[128,256]{1,0:T(8,128)(2,1)S(1)}, bf16[128,256]{1,0:T(8,128)(2,1)S(1)}, u32[]{:S(2)}, u32[]{:S(2)}) collective-permute-start(bf16[128,256]{1,0:T(8,128)(2,1)S(1)} %get-tuple-element.44), channel_id=1, source_target_pairs={{0,32},{32,0},{64,96},{96,64},{1,33},{33,1},{65,97},{97,65},{2,34}... | collective-permute-start | bytes 196616 | tf_op jit(solution)/shard_map/ppermute | solution.py:24
  8.0 4.1 %counts.2 = (bf16[1024,512]{1,0:T(8,128)(2,1)S(1)}, bf16[1024,512]{1,0:T(8,128)(2,1)S(1)}, bf16[1024,512]{1,0:T(8,128)(2,1)S(1)}, bf16[1024,512]{1,0:T(8,128)(2,...) custom-call(s32[1]{0:T(128)} %bitcast.1.here_ref, ...), custom_call_target="tpu_custom_call" | custom-call | flops 2000000000 | bytes 4500000 | tf_op jit(solution)/shard_map/counts/pallas_call | solution.py:125
  12.1 1.0 %copy-done = bf16[1024,512]{1,0:T(8,128)(2,1)} copy-done((bf16[1024,512]{1,0:T(8,128)(2,1)}, bf16[1024,512]{1,0:T(8,128)(2,1)S(1)}, u32[]{:S(2)}) %copy-start) | copy-done | bytes 1048600
  13.0 1.0 %copy-done.2 = bf16[1024,512]{1,0:T(8,128)(2,1)} copy-done((bf16[1024,512]{1,0:T(8,128)(2,1)}, bf16[1024,512]{1,0:T(8,128)(2,1)S(1)}, u32[]{:S(2)}) %copy-start.2) | copy-done | bytes 1048600
  14.0 1.0 %copy-done.4 = bf16[1024,512]{1,0:T(8,128)(2,1)} copy-done((bf16[1024,512]{1,0:T(8,128)(2,1)}, bf16[1024,512]{1,0:T(8,128)(2,1)S(1)}, u32[]{:S(2)}) %copy-start.4) | copy-done | bytes 1048600
  15.0 1.0 %copy-done.6 = bf16[1024,512]{1,0:T(8,128)(2,1)} copy-done((bf16[1024,512]{1,0:T(8,128)(2,1)}, bf16[1024,512]{1,0:T(8,128)(2,1)S(1)}, u32[]{:S(2)}) %copy-start.6) | copy-done | bytes 1048600
  16.1 1.0 %copy-done.8 = bf16[1024,512]{1,0:T(8,128)(2,1)} copy-done((bf16[1024,512]{1,0:T(8,128)(2,1)}, bf16[1024,512]{1,0:T(8,128)(2,1)S(1)}, u32[]{:S(2)}) %copy-start.8) | copy-done | bytes 1048600
  17.1 0.8 %convert_element_type.28 = s32[101,256]{1,0:T(8,128)S(1)} convert(s16[101,256]{1,0:T(8,128)(2,1)} %collective-permute-done) | non-fusion elementwise | flops 25856 | bytes 155136 | tf_op jit(solution)/shard_map/convert_element_type | solution.py:189
  17.9 1.2 %copy-done.1 = bf16[1024,512]{1,0:T(8,128)(2,1)S(1)} copy-done((bf16[1024,512]{1,0:T(8,128)(2,1)S(1)}, bf16[1024,512]{1,0:T(8,128)(2,1)}, u32[]{:S(2)}) %copy-start.1) | copy-done | bytes 1048600
  19.2 1.2 %copy-done.3 = bf16[1024,512]{1,0:T(8,128)(2,1)S(1)} copy-done((bf16[1024,512]{1,0:T(8,128)(2,1)S(1)}, bf16[1024,512]{1,0:T(8,128)(2,1)}, u32[]{:S(2)}) %copy-start.3) | copy-done | bytes 1048600
  20.4 1.2 %copy-done.5 = bf16[1024,512]{1,0:T(8,128)(2,1)S(1)} copy-done((bf16[1024,512]{1,0:T(8,128)(2,1)S(1)}, bf16[1024,512]{1,0:T(8,128)(2,1)}, u32[]{:S(2)}) %copy-start.5) | copy-done | bytes 1048600
  21.6 1.2 %copy-done.7 = bf16[1024,512]{1,0:T(8,128)(2,1)S(1)} copy-done((bf16[1024,512]{1,0:T(8,128)(2,1)S(1)}, bf16[1024,512]{1,0:T(8,128)(2,1)}, u32[]{:S(2)}) %copy-start.7) | copy-done | bytes 1048600
  22.8 1.2 %copy-done.9 = bf16[1024,512]{1,0:T(8,128)(2,1)S(1)} copy-done((bf16[1024,512]{1,0:T(8,128)(2,1)S(1)}, bf16[1024,512]{1,0:T(8,128)(2,1)}, u32[]{:S(2)}) %copy-start.9) | copy-done | bytes 1048600
  24.1 4.1 %counts.3 = (bf16[1024,512]{1,0:T(8,128)(2,1)S(1)}, bf16[1024,512]{1,0:T(8,128)(2,1)S(1)}, bf16[1024,512]{1,0:T(8,128)(2,1)S(1)}, bf16[1024,512]{1,0:T(8,128)(2,...) custom-call(s32[1]{0:T(128)} %bitcast.1.here_ref, ...), custom_call_target="tpu_custom_call", output_to_operand_aliasing={{0}: (4, {}), {1}: (5, {}), {2}: (6, {}), {3}: (7, {}), {4}... | custom-call | flops 2000000000 | bytes 4500000 | tf_op jit(solution)/shard_map/counts/pallas_call | solution.py:125
  28.2 1.9 %collective-permute-start.2 = (bf16[256,256]{1,0:T(8,128)(2,1)S(1)}, bf16[256,256]{1,0:T(8,128)(2,1)S(1)}, u32[]{:S(2)}, u32[]{:S(2)}) collective-permute-start(bf16[256,256]{1,0:T(8,128)(2,1)S(1)} %pad_maximum_fusion.2), channel_id=1, source_target_pairs={{0,12},{4,8},{8,4},{12,0},{1,13},{5,9},{9,5},{13,1},{2,14},{6,10},... | collective-permute-start | bytes 393224 | tf_op jit(solution)/shard_map/ppermute | solution.py:24
  30.1 2.3 %collective-permute-start.4 = (bf16[256,256]{1,0:T(8,128)(2,1)S(1)}, bf16[256,256]{1,0:T(8,128)(2,1)S(1)}, u32[]{:S(2)}, u32[]{:S(2)}) collective-permute-start(bf16[256,256]{1,0:T(8,128)(2,1)S(1)} %pad_maximum_fusion.3), channel_id=1, source_target_pairs={{0,96},{32,64},{64,32},{96,0},{1,97},{33,65},{65,33},{97,1},{2,98}... | collective-permute-start | bytes 393224 | tf_op jit(solution)/shard_map/ppermute | solution.py:24
  32.5 0.9 %collective-permute-done.2 = bf16[256,256]{1,0:T(8,128)(2,1)S(1)} collective-permute-done((bf16[256,256]{1,0:T(8,128)(2,1)S(1)}, bf16[256,256]{1,0:T(8,128)(2,1)S(1)}, u32[]{:S(2)}, u32[]{:S(2)}) %collective-permute-start.2) | collective-permute-done | bytes 131104 | tf_op jit(solution)/shard_map/ppermute | solution.py:24
  33.4 2.7 %collective-permute-start.7 = (bf16[512,256]{1,0:T(8,128)(2,1)S(1)}, bf16[512,256]{1,0:T(8,128)(2,1)S(1)}, u32[]{:S(2)}, u32[]{:S(2)}) collective-permute-start(bf16[512,256]{1,0:T(8,128)(2,1)S(1)} %pad_maximum_fusion), channel_id=1, source_target_pairs={{0,96},{32,0},{64,32},{96,64},{1,97},{33,1},{65,33},{97,65},{2,98}... | collective-permute-start | bytes 786440 | tf_op jit(solution)/shard_map/ppermute | solution.py:24
  36.2 2.7 %collective-permute-start.8 = (bf16[512,256]{1,0:T(8,128)(2,1)S(1)}, bf16[512,256]{1,0:T(8,128)(2,1)S(1)}, u32[]{:S(2)}, u32[]{:S(2)}) collective-permute-start(bf16[512,256]{1,0:T(8,128)(2,1)S(1)} %pad_maximum_fusion.1), channel_id=1, source_target_pairs={{0,12},{4,0},{8,4},{12,8},{1,13},{5,1},{9,5},{13,9},{2,14},{6,2},{... | collective-permute-start | bytes 786440 | tf_op jit(solution)/shard_map/ppermute | solution.py:24
  39.3 1.4 %collective-permute-done.5 = bf16[512,256]{1,0:T(8,128)(2,1)S(1)} collective-permute-done((bf16[512,256]{1,0:T(8,128)(2,1)S(1)}, bf16[512,256]{1,0:T(8,128)(2,1)S(1)}, u32[]{:S(2)}, u32[]{:S(2)}) %collective-permute-start.5) | collective-permute-done | bytes 262176 | tf_op jit(solution)/shard_map/ppermute | solution.py:24
  41.2 1.7 %collective-permute-done.6 = bf16[512,256]{1,0:T(8,128)(2,1)S(1)} collective-permute-done((bf16[512,256]{1,0:T(8,128)(2,1)S(1)}, bf16[512,256]{1,0:T(8,128)(2,1)S(1)}, u32[]{:S(2)}, u32[]{:S(2)}) %collective-permute-start.6) | collective-permute-done | bytes 262176 | tf_op jit(solution)/shard_map/ppermute | solution.py:24
  45.6 4.1 %collective-permute-done.10 = bf16[512,256]{1,0:T(8,128)(2,1)S(1)} collective-permute-done((bf16[512,256]{1,0:T(8,128)(2,1)S(1)}, bf16[512,256]{1,0:T(8,128)(2,1)S(1)}, u32[]{:S(2)}, u32[]{:S(2)}) %collective-permute-start.10) | collective-permute-done | bytes 262176 | tf_op jit(solution)/shard_map/ppermute | solution.py:24
  52.0 5.0 %collective-permute-start.11 = (f16[512,512]{1,0:T(8,128)(2,1)S(1)}, f16[512,512]{1,0:T(8,128)(2,1)S(1)}, u32[]{:S(2)}, u32[]{:S(2)}) collective-permute-start(f16[512,512]{1,0:T(8,128)(2,1)S(1)} %convert_element_type.31), channel_id=1, source_target_pairs={{0,1},{1,0},{2,3},{3,2},{4,5},{5,4},{6,7},{7,6},{8,9},{9,8},{10,11... | collective-permute-start | bytes 1572872 | tf_op jit(solution)/shard_map/ppermute | solution.py:24
  57.6 0.9 %collective-permute-done.11 = f16[512,512]{1,0:T(8,128)(2,1)S(1)} collective-permute-done((f16[512,512]{1,0:T(8,128)(2,1)S(1)}, f16[512,512]{1,0:T(8,128)(2,1)S(1)}, u32[]{:S(2)}, u32[]{:S(2)}) %collective-permute-start.11) | collective-permute-done | bytes 524320 | tf_op jit(solution)/shard_map/ppermute | solution.py:24
  58.9 2.7 %collective-permute-start.12 = (f16[256,512]{1,0:T(8,128)(2,1)S(1)}, f16[256,512]{1,0:T(8,128)(2,1)S(1)}, u32[]{:S(2)}, u32[]{:S(2)}) collective-permute-start(f16[256,512]{1,0:T(8,128)(2,1)S(1)} %get-tuple-element.41), channel_id=1, source_target_pairs={{0,2},{2,0},{1,3},{3,1},{4,6},{6,4},{5,7},{7,5},{8,10},{10,8},{9,1... | collective-permute-start | bytes 786440 | tf_op jit(solution)/shard_map/ppermute | solution.py:24
  62.2 5.8 %collective-permute-done.12 = f16[256,512]{1,0:T(8,128)(2,1)S(1)} collective-permute-done((f16[256,512]{1,0:T(8,128)(2,1)S(1)}, f16[256,512]{1,0:T(8,128)(2,1)S(1)}, u32[]{:S(2)}, u32[]{:S(2)}) %collective-permute-start.12) | collective-permute-done | bytes 262176 | tf_op jit(solution)/shard_map/ppermute | solution.py:24
  68.0 5.1 %collective-permute-done.13 = f16[256,512]{1,0:T(8,128)(2,1)S(1)} collective-permute-done((f16[256,512]{1,0:T(8,128)(2,1)S(1)}, f16[256,512]{1,0:T(8,128)(2,1)S(1)}, u32[]{:S(2)}, u32[]{:S(2)}) %collective-permute-start.13) | collective-permute-done | bytes 262176 | tf_op jit(solution)/shard_map/ppermute | solution.py:24
  73.1 1.2 %collective-permute-done.14 = f16[256,512]{1,0:T(8,128)(2,1)S(1)} collective-permute-done((f16[256,512]{1,0:T(8,128)(2,1)S(1)}, f16[256,512]{1,0:T(8,128)(2,1)S(1)}, u32[]{:S(2)}, u32[]{:S(2)}) %collective-permute-start.14) | collective-permute-done | bytes 262176 | tf_op jit(solution)/shard_map/ppermute | solution.py:222
  75.1 0.8 %collective-permute-done.15 = f32[256]{0:T(256)S(1)} collective-permute-done((f32[256]{0:T(256)S(1)}, f32[256]{0:T(256)S(1)}, u32[]{:S(2)}, u32[]{:S(2)}) %collective-permute-start.15) | collective-permute-done | bytes 1056 | tf_op jit(solution)/shard_map/ppermute | solution.py:24
  (74 shorter events, 11.3 us)
Async XLA Ops:
  0.7 3.7 %copy-start.17 = (bf16[256,256]{1,0:T(8,128)(2,1)S(1)}, bf16[256,256]{1,0:T(8,128)(2,1)}, u32[]{:S(2)}) copy-start(bf16[256,256]{1,0:T(8,128)(2,1)} %param.7) | copy-start | bytes 393220
  2.2 5.1 %copy-start.14 = (s32[256,50]{0,1:T(8,128)S(1)}, s32[256,50]{0,1:T(8,128)}, u32[]{:S(2)}) copy-start(s32[256,50]{0,1:T(8,128)} %param.10) | copy-start | bytes 153604
  2.2 5.1 %copy-start.15 = (s32[256,50]{0,1:T(8,128)S(1)}, s32[256,50]{0,1:T(8,128)}, u32[]{:S(2)}) copy-start(s32[256,50]{0,1:T(8,128)} %param.9) | copy-start | bytes 153604
  2.2 14.8 %collective-permute-start = (s16[101,256]{1,0:T(8,128)(2,1)}, s16[101,256]{1,0:T(8,128)(2,1)}, u32[]{:S(2)}, u32[]{:S(2)}) collective-permute-start(s16[101,256]{1,0:T(8,128)(2,1)} %pad_add_fusion), channel_id=1, source_target_pairs={{0,16},{16,0},{1,17},{17,1},{2,18},{18,2},{3,19},{19,3},{4,20},{20... | collective-permute-start | bytes 155144 | tf_op jit(solution)/shard_map/ppermute | solution.py:24
  4.4 23.9 %collective-permute-start.1 = (bf16[128,256]{1,0:T(8,128)(2,1)S(1)}, bf16[128,256]{1,0:T(8,128)(2,1)S(1)}, u32[]{:S(2)}, u32[]{:S(2)}) collective-permute-start(bf16[128,256]{1,0:T(8,128)(2,1)S(1)} %get-tuple-element.43), channel_id=1, source_target_pairs={{0,4},{4,0},{8,12},{12,8},{1,5},{5,1},{9,13},{13,9},{2,6},{6,2},{1... | collective-permute-start | bytes 196616 | tf_op jit(solution)/shard_map/ppermute | solution.py:24
  5.6 24.5 %collective-permute-start.3 = (bf16[128,256]{1,0:T(8,128)(2,1)S(1)}, bf16[128,256]{1,0:T(8,128)(2,1)S(1)}, u32[]{:S(2)}, u32[]{:S(2)}) collective-permute-start(bf16[128,256]{1,0:T(8,128)(2,1)S(1)} %get-tuple-element.44), channel_id=1, source_target_pairs={{0,32},{32,0},{64,96},{96,64},{1,33},{33,1},{65,97},{97,65},{2,34}... | collective-permute-start | bytes 196616 | tf_op jit(solution)/shard_map/ppermute | solution.py:24
  13.0 1.0 %copy-start.2 = (bf16[1024,512]{1,0:T(8,128)(2,1)}, bf16[1024,512]{1,0:T(8,128)(2,1)S(1)}, u32[]{:S(2)}) copy-start(bf16[1024,512]{1,0:T(8,128)(2,1)S(1)} %get-tuple-element.26.rest_5_) | copy-start | bytes 3145732
  15.0 1.0 %copy-start.6 = (bf16[1024,512]{1,0:T(8,128)(2,1)}, bf16[1024,512]{1,0:T(8,128)(2,1)S(1)}, u32[]{:S(2)}) copy-start(bf16[1024,512]{1,0:T(8,128)(2,1)S(1)} %get-tuple-element.28.rest_7_) | copy-start | bytes 3145732
  16.1 1.0 %copy-start.8 = (bf16[1024,512]{1,0:T(8,128)(2,1)}, bf16[1024,512]{1,0:T(8,128)(2,1)S(1)}, u32[]{:S(2)}) copy-start(bf16[1024,512]{1,0:T(8,128)(2,1)S(1)} %get-tuple-element.21.rest_0_) | copy-start | bytes 3145732
  17.9 1.2 %copy-start.1 = (bf16[1024,512]{1,0:T(8,128)(2,1)S(1)}, bf16[1024,512]{1,0:T(8,128)(2,1)}, u32[]{:S(2)}) copy-start(bf16[1024,512]{1,0:T(8,128)(2,1)} %copy-done) | copy-start | bytes 3145732
  19.2 1.2 %copy-start.3 = (bf16[1024,512]{1,0:T(8,128)(2,1)S(1)}, bf16[1024,512]{1,0:T(8,128)(2,1)}, u32[]{:S(2)}) copy-start(bf16[1024,512]{1,0:T(8,128)(2,1)} %copy-done.2) | copy-start | bytes 3145732
  20.4 1.2 %copy-start.5 = (bf16[1024,512]{1,0:T(8,128)(2,1)S(1)}, bf16[1024,512]{1,0:T(8,128)(2,1)}, u32[]{:S(2)}) copy-start(bf16[1024,512]{1,0:T(8,128)(2,1)} %copy-done.4) | copy-start | bytes 3145732
  21.6 1.2 %copy-start.7 = (bf16[1024,512]{1,0:T(8,128)(2,1)S(1)}, bf16[1024,512]{1,0:T(8,128)(2,1)}, u32[]{:S(2)}) copy-start(bf16[1024,512]{1,0:T(8,128)(2,1)} %copy-done.6) | copy-start | bytes 3145732
  22.8 1.2 %copy-start.9 = (bf16[1024,512]{1,0:T(8,128)(2,1)S(1)}, bf16[1024,512]{1,0:T(8,128)(2,1)}, u32[]{:S(2)}) copy-start(bf16[1024,512]{1,0:T(8,128)(2,1)} %copy-done.8) | copy-start | bytes 3145732
  28.2 11.2 %copy-start.10 = (bf16[1024,512]{1,0:T(8,128)(2,1)}, bf16[1024,512]{1,0:T(8,128)(2,1)S(1)}, u32[]{:S(2)}) copy-start(bf16[1024,512]{1,0:T(8,128)(2,1)S(1)} %get-tuple-element.29) | copy-start | bytes 3145732
  28.2 5.1 %collective-permute-start.2 = (bf16[256,256]{1,0:T(8,128)(2,1)S(1)}, bf16[256,256]{1,0:T(8,128)(2,1)S(1)}, u32[]{:S(2)}, u32[]{:S(2)}) collective-permute-start(bf16[256,256]{1,0:T(8,128)(2,1)S(1)} %pad_maximum_fusion.2), channel_id=1, source_target_pairs={{0,12},{4,8},{8,4},{12,0},{1,13},{5,9},{9,5},{13,1},{2,14},{6,10},... | collective-permute-start | bytes 393224 | tf_op jit(solution)/shard_map/ppermute | solution.py:24
  30.1 6.0 %collective-permute-start.4 = (bf16[256,256]{1,0:T(8,128)(2,1)S(1)}, bf16[256,256]{1,0:T(8,128)(2,1)S(1)}, u32[]{:S(2)}, u32[]{:S(2)}) collective-permute-start(bf16[256,256]{1,0:T(8,128)(2,1)S(1)} %pad_maximum_fusion.3), channel_id=1, source_target_pairs={{0,96},{32,64},{64,32},{96,0},{1,97},{33,65},{65,33},{97,1},{2,98}... | collective-permute-start | bytes 393224 | tf_op jit(solution)/shard_map/ppermute | solution.py:24
  33.4 7.4 %collective-permute-start.5 = (bf16[512,256]{1,0:T(8,128)(2,1)S(1)}, bf16[512,256]{1,0:T(8,128)(2,1)S(1)}, u32[]{:S(2)}, u32[]{:S(2)}) collective-permute-start(bf16[512,256]{1,0:T(8,128)(2,1)S(1)} %pad_maximum_fusion), channel_id=1, source_target_pairs={{0,32},{32,64},{64,96},{96,0},{1,33},{33,65},{65,97},{97,1},{2,34}... | collective-permute-start | bytes 786440 | tf_op jit(solution)/shard_map/ppermute | solution.py:24
  33.4 9.9 %collective-permute-start.7 = (bf16[512,256]{1,0:T(8,128)(2,1)S(1)}, bf16[512,256]{1,0:T(8,128)(2,1)S(1)}, u32[]{:S(2)}, u32[]{:S(2)}) collective-permute-start(bf16[512,256]{1,0:T(8,128)(2,1)S(1)} %pad_maximum_fusion), channel_id=1, source_target_pairs={{0,96},{32,0},{64,32},{96,64},{1,97},{33,1},{65,33},{97,65},{2,98}... | collective-permute-start | bytes 786440 | tf_op jit(solution)/shard_map/ppermute | solution.py:24
  36.1 6.8 %collective-permute-start.6 = (bf16[512,256]{1,0:T(8,128)(2,1)S(1)}, bf16[512,256]{1,0:T(8,128)(2,1)S(1)}, u32[]{:S(2)}, u32[]{:S(2)}) collective-permute-start(bf16[512,256]{1,0:T(8,128)(2,1)S(1)} %pad_maximum_fusion.1), channel_id=1, source_target_pairs={{0,4},{4,8},{8,12},{12,0},{1,5},{5,9},{9,13},{13,1},{2,6},{6,10},{... | collective-permute-start | bytes 786440 | tf_op jit(solution)/shard_map/ppermute | solution.py:24
  36.2 7.6 %collective-permute-start.8 = (bf16[512,256]{1,0:T(8,128)(2,1)S(1)}, bf16[512,256]{1,0:T(8,128)(2,1)S(1)}, u32[]{:S(2)}, u32[]{:S(2)}) collective-permute-start(bf16[512,256]{1,0:T(8,128)(2,1)S(1)} %pad_maximum_fusion.1), channel_id=1, source_target_pairs={{0,12},{4,0},{8,4},{12,8},{1,13},{5,1},{9,5},{13,9},{2,14},{6,2},{... | collective-permute-start | bytes 786440 | tf_op jit(solution)/shard_map/ppermute | solution.py:24
  40.7 9.4 %collective-permute-start.9 = (bf16[512,256]{1,0:T(8,128)(2,1)S(1)}, bf16[512,256]{1,0:T(8,128)(2,1)S(1)}, u32[]{:S(2)}, u32[]{:S(2)}) collective-permute-start(bf16[512,256]{1,0:T(8,128)(2,1)S(1)} %collective-permute-done.5), channel_id=1, source_target_pairs={{0,32},{32,64},{64,96},{96,0},{1,33},{33,65},{65,97},{97,1},{2,34}... | collective-permute-start | bytes 786440 | tf_op jit(solution)/shard_map/ppermute | solution.py:24
  42.9 6.7 %collective-permute-start.10 = (bf16[512,256]{1,0:T(8,128)(2,1)S(1)}, bf16[512,256]{1,0:T(8,128)(2,1)S(1)}, u32[]{:S(2)}, u32[]{:S(2)}) collective-permute-start(bf16[512,256]{1,0:T(8,128)(2,1)S(1)} %collective-permute-done.6), channel_id=1, source_target_pairs={{0,4},{4,8},{8,12},{12,0},{1,5},{5,9},{9,13},{13,1},{2,6},{6,10},{... | collective-permute-start | bytes 786440 | tf_op jit(solution)/shard_map/ppermute | solution.py:24
  43.8 1.2 %copy-start.11 = (bf16[1024,512]{1,0:T(8,128)(2,1)S(1)}, bf16[1024,512]{1,0:T(8,128)(2,1)}, u32[]{:S(2)}) copy-start(bf16[1024,512]{1,0:T(8,128)(2,1)} %copy-done.10) | copy-start | bytes 3145732
  50.1 1.0 %copy-start.12 = (bf16[256,1024]{1,0:T(8,128)(2,1)S(1)}, bf16[256,1024]{1,0:T(8,128)(2,1)}, u32[]{:S(2)}) copy-start(bf16[256,1024]{1,0:T(8,128)(2,1)} %self_ref.3) | copy-start | bytes 1572868
  50.1 1.2 %copy-start.13 = (bf16[256,1024]{1,0:T(8,128)(2,1)S(1)}, bf16[256,1024]{1,0:T(8,128)(2,1)}, u32[]{:S(2)}) copy-start(bf16[256,1024]{1,0:T(8,128)(2,1)} %nbr_ref.3) | copy-start | bytes 1572868
  52.0 6.6 %collective-permute-start.11 = (f16[512,512]{1,0:T(8,128)(2,1)S(1)}, f16[512,512]{1,0:T(8,128)(2,1)S(1)}, u32[]{:S(2)}, u32[]{:S(2)}) collective-permute-start(f16[512,512]{1,0:T(8,128)(2,1)S(1)} %convert_element_type.31), channel_id=1, source_target_pairs={{0,1},{1,0},{2,3},{3,2},{4,5},{5,4},{6,7},{7,6},{8,9},{9,8},{10,11... | collective-permute-start | bytes 1572872 | tf_op jit(solution)/shard_map/ppermute | solution.py:24
  58.9 3.3 %copy-start.18 = (f32[1024]{0:T(1024)S(1)}, f32[1024]{0:T(1024)}, u32[]{:S(2)}) copy-start(f32[1024]{0:T(1024)} %param.13) | copy-start | bytes 12292
  58.9 9.1 %collective-permute-start.12 = (f16[256,512]{1,0:T(8,128)(2,1)S(1)}, f16[256,512]{1,0:T(8,128)(2,1)S(1)}, u32[]{:S(2)}, u32[]{:S(2)}) collective-permute-start(f16[256,512]{1,0:T(8,128)(2,1)S(1)} %get-tuple-element.41), channel_id=1, source_target_pairs={{0,2},{2,0},{1,3},{3,1},{4,6},{6,4},{5,7},{7,5},{8,10},{10,8},{9,1... | collective-permute-start | bytes 786440 | tf_op jit(solution)/shard_map/ppermute | solution.py:24
  61.6 11.5 %collective-permute-start.13 = (f16[256,512]{1,0:T(8,128)(2,1)S(1)}, f16[256,512]{1,0:T(8,128)(2,1)S(1)}, u32[]{:S(2)}, u32[]{:S(2)}) collective-permute-start(f16[256,512]{1,0:T(8,128)(2,1)S(1)} %get-tuple-element.42), channel_id=1, source_target_pairs={{0,16},{16,0},{1,17},{17,1},{2,18},{18,2},{3,19},{19,3},{4,20},{20... | collective-permute-start | bytes 786440 | tf_op jit(solution)/shard_map/ppermute | solution.py:24
  61.6 12.7 %collective-permute-start.14 = (f16[256,512]{1,0:T(8,128)(2,1)S(1)}, f16[256,512]{1,0:T(8,128)(2,1)S(1)}, u32[]{:S(2)}, u32[]{:S(2)}) collective-permute-start(f16[256,512]{1,0:T(8,128)(2,1)S(1)} %get-tuple-element.42), channel_id=1, source_target_pairs={{0,18},{2,16},{16,2},{18,0},{1,19},{3,17},{17,3},{19,1},{4,22},{6,... | collective-permute-start | bytes 786440 | tf_op jit(solution)/shard_map/ppermute | solution.py:222
  74.6 1.4 %collective-permute-start.15 = (f32[256]{0:T(256)S(1)}, f32[256]{0:T(256)S(1)}, u32[]{:S(2)}, u32[]{:S(2)}) collective-permute-start(f32[256]{0:T(256)S(1)} %get-tuple-element.37), channel_id=1, source_target_pairs={{0,1},{1,0},{2,3},{3,2},{4,5},{5,4},{6,7},{7,6},{8,9},{9,8},{10,11... | collective-permute-start | bytes 3080 | tf_op jit(solution)/shard_map/ppermute | solution.py:24
  (3 other events, 2.6 us)

commit v3 on v2

--- a/solution.py
+++ b/solution.py
@@ -12,8 +12,7 @@
 DOM = ("z", "yl", "x")
 LANES = 128
 SLOTS = 64
-TILES = 16
-WIDE = 2 * LANES
+TILES = 32
 EIGHT = 8
 GROUP = 16
 SCALE = 16.0
@@ -30,13 +29,10 @@
     nbr, nodes = ids_ref.shape
     counts_row, own_row = group * nodes, (2 + group) * nodes
     here = here_ref[0]
-    places = [(o, c) for o in range(len(out_refs)) for c in range(0, out_refs[o].shape[1], WIDE)]
+    places = [(o, c) for o in range(len(out_refs)) for c in range(0, out_refs[o].shape[1], LANES)]
 
     def column(row):
         return jnp.broadcast_to(row.astype(jnp.float32), (LANES, LANES)).T.astype(jnp.bfloat16)
-
-    def widened(value):
-        return jnp.concatenate([value] * (WIDE // LANES), axis=1)
 
     node = lax.broadcasted_iota(jnp.int32, (nbr, LANES), 1) & (EIGHT - 1)
     for part in range(nodes // LANES):
@@ -57,9 +53,9 @@
         own_low_ref[span, :] = column(own_low)
 
     row = lax.broadcasted_iota(jnp.int32, (GROUP, LANES), 0).astype(jnp.float32)
-    rows = [(row + r * GROUP).astype(jnp.bfloat16) for r in range(WIDE // GROUP)]
-    left = lax.broadcasted_iota(jnp.int32, (GROUP, LANES), 1) < SLOTS
-    lane = lax.broadcasted_iota(jnp.int32, (GROUP, WIDE), 1)
+    rows = [(row + r * GROUP).astype(jnp.bfloat16) for r in range(TILES * EIGHT // GROUP)]
+    lane = lax.broadcasted_iota(jnp.int32, (GROUP, LANES), 1)
+    left = lane < SLOTS
     lane = lane.astype(jnp.float32).astype(jnp.bfloat16)
     zero = jnp.zeros((GROUP, LANES), jnp.bfloat16)
     one = jnp.ones((GROUP, LANES), jnp.bfloat16)
@@ -81,13 +77,12 @@
             for n in range(eight, eight + EIGHT, 2):
                 code, low, times = (pair(t, n) for t in tables)
                 marks.append(
-                    jnp.concatenate(
-                        [jnp.where(code == r, times, zero) for r in rows[: TILES * EIGHT // GROUP]],
-                        axis=0,
-                    )
+                    jnp.concatenate([jnp.where(code == r, times, zero) for r in rows], axis=0)
                 )
                 lows.append(
-                    jnp.concatenate([jnp.where(low == r, one, zero) for r in rows], axis=0)
+                    jnp.concatenate(
+                        [jnp.where(low == r, one, zero) for r in rows[: LANES // GROUP]], axis=0
+                    )
                 )
             sides.append(
                 lax.dot_general(
@@ -97,26 +92,25 @@
                     preferred_element_type=jnp.float32,
                 )
             )
-        own_tile = widened(own_tile_ref[span, :])
-        hit = jnp.where(widened(own_low_ref[span, :]) == lane, widened(one), widened(zero))
+        own_tile = own_tile_ref[span, :]
+        hit = jnp.where(own_low_ref[span, :] == lane, one, zero)
         for t, (o, col) in enumerate(places):
             block = jnp.concatenate([side[t * EIGHT : t * EIGHT + EIGHT, :] for side in sides], axis=0)
-            out_refs[o][pl.ds(counts_row + first, GROUP), col : col + WIDE] = block.astype(jnp.bfloat16)
-            out_refs[o][pl.ds(own_row + first, GROUP), col : col + WIDE] = jnp.where(
-                own_tile == jnp.bfloat16(t), hit, widened(zero)
+            out_refs[o][pl.ds(counts_row + first, GROUP), col : col + LANES] = block.astype(jnp.bfloat16)
+            out_refs[o][pl.ds(own_row + first, GROUP), col : col + LANES] = jnp.where(
+                own_tile == jnp.bfloat16(t), hit, zero
             )
 
 
 def located(ids, here):
-    block = ids >> 8
-    dz = ((here >> 3) - (block >> 3)) & 3
-    dx = (here - block) & 3
-    same = (((here ^ block) >> 2) & 1) == 0
+    apart = here ^ (ids >> 8)
+    same = ((apart >> 2) & 1) == 0
+    dx, dz = apart & 3, (apart >> 3) & 3
     first_half = (ids & 128) == 0
     far = jnp.where(first_half, dz, dx)
-    near = jnp.where(first_half, here ^ block, (here ^ block) >> 3) & 3
+    near = jnp.where(first_half, dx, dz)
     tile = jnp.where(first_half, 0, 16) + (far ^ (far >> 1)) * 4 + (near ^ (near >> 1))
-    return jnp.where(same, tile >> 1, -1), ((tile & 1) << 7) + (ids & 127)
+    return jnp.where(same, tile, -1), ids & 127
 
 
 def count_blocks(group, given, here, table, nbr, widths):
@@ -197,8 +191,8 @@
         lines.append(jnp.concatenate([pair, rest], axis=0))
     pieces = []
     for line, (_, far) in zip(lines, axes):
-        up, down = moved(line, far, lambda i: i + 1), moved(line, far, lambda i: i + 3)
-        pieces += [line, up, down, moved(up, far, lambda i: i + 1)]
+        low, high = moved(line, far, lambda i: i ^ 1), moved(line, far, lambda i: i ^ 3)
+        pieces += [line, low, high, moved(high, far, lambda i: i ^ 1)]
 
     widths = [p.shape[0] for p in pieces]
     blocks = count_blocks(0, [], here, table, nbr, widths)
@@ -207,7 +201,6 @@
         jnp.dot(blocks[i], pieces[i], preferred_element_type=jnp.float32)
         for i in (0, 4, 1, 5, 2, 6, 3, 7)
     )
-    wide = 2 * share
     total = jnp.concatenate(
         [jnp.sum(t[nbr : 2 * nbr].astype(jnp.float32), axis=0) for t in (table, theirs)]
     )
@@ -216,19 +209,21 @@
     got = moved(given.astype(jnp.float16), "core", lambda i: i ^ 1)
     kept = projected(core, sums, total, w_self, w_neighbor)
     chip = kept + got.astype(jnp.float32)
-    sent = chip.astype(jnp.float16)
-    from_yh = moved(sent[:batch], "yh", lambda i: i ^ 1)
-    from_yl = moved(sent[batch:], "yl", lambda i: i ^ 1)
-    across = lax.ppermute(sent[batch:], ("yl", "yh"), [(i, i ^ 3) for i in range(4)])
-    pre = chip[:batch] + from_yh.astype(jnp.float32)
+    first, second = chip[:, :share], chip[:, share:]
+    here_part = jnp.where(yh == 0, first, second)
+    there_part = jnp.where(yh == 0, second, first).astype(jnp.float16)
+    from_yh = moved(there_part[:batch], "yh", lambda i: i ^ 1)
+    from_yl = moved(here_part[batch:].astype(jnp.float16), "yl", lambda i: i ^ 1)
+    across = lax.ppermute(there_part[batch:], ("yl", "yh"), [(i, i ^ 3) for i in range(4)])
+    pre = here_part[:batch] + from_yh.astype(jnp.float32)
     pre = pre + from_yl.astype(jnp.float32) + across.astype(jnp.float32)
-    my_bias = lax.dynamic_index_in_dim(bias.reshape(2, 2, share), core, 1, False).reshape(1, wide)
-    hidden = jnp.maximum(pre * (1.0 / SCALE) + my_bias, 0.0)
+    my_bias = lax.dynamic_slice_in_dim(bias, (2 * yh + core) * share, share, 0)
+    hidden = jnp.maximum(pre * (1.0 / SCALE) + my_bias[None, :], 0.0)
     squares = jnp.sum(hidden * hidden, axis=1)
     squares = squares + moved(squares, "core", lambda i: i ^ 1)
+    squares = squares + moved(squares, "yh", lambda i: i ^ 1)
     scale = jnp.sqrt(squares / bias.shape[0] + 1e-06)[:, None]
-    out = jnp.where(yh == 0, hidden[:, :share], hidden[:, share:])
-    return out / scale
+    return hidden / scale
 
 
 def solution(mesh):

time: 77.3 us -> 75.9 us (0.982)
  waiting for transfers between devices: 21.9 us -> 17.7 us
  starting transfers between devices: 23.7 us -> 25.5 us
  other arithmetic: 4.53 us -> 5.54 us
    ppermute x15 -> x16, waiting for transfers between devices: 20.7 us -> 14.7 us  [moved(): return lax.ppermute(value, axis, [(i, target(i) % n) for i in range(n)])]
    ppermute x15 -> x16, starting transfers between devices: 23 us -> 25.5 us  [moved(): return lax.ppermute(value, axis, [(i, target(i) % n) for i in range(n)])]
    ppermute x1, waiting for transfers between devices: 1.18 us -> 3.01 us  [shards(): lax.ppermute(there_part[batch:], ('yl', 'yh'), [(i, i ^ 3) for i in range...]
    add x0 -> x2, other arithmetic: none -> 1.2 us  [the longest x1 1.2 us: shards(): chip = kept + got.astype(jnp.float32)]
    unnamed x38 -> x36, local copies, waits for them, and re-layouts: 13.2 us -> 13.1 us
    another operation x2 -> x3, other arithmetic: 1.57 us -> 1.59 us
  transfers between devices with their start and end apart: 16 -> 17, of which waited for: 9 -> 9; matrix products, arithmetic and copies ran while one was open for 5% -> 6% of each run, Pallas kernels for 11% -> 11%
where the time goes in v3:
time: 75.9 us; the launch traced here: 75.3 us
  starting transfers between devices  25.5 us (34%)
  waiting for transfers between devices  17.7 us (23%)
  local copies, waits for them, and re-layouts  14.1 us (19%)
  Pallas kernels  8.68 us (11%)
  other arithmetic  5.54 us (7%)
  matrix products  3.49 us (5%)
    ppermute x16, starting transfers between devices, moved(): return lax.ppermute(value, axis, [(i, target(i) % n) for i in range(n)])  25.5 us
    ppermute x16, waiting for transfers between devices, moved(): return lax.ppermute(value, axis, [(i, target(i) % n) for i in range(n)])  14.7 us
    unnamed x36, local copies, waits for them, and re-layouts  13.1 us
    pallas_call x2, Pallas kernels, count_blocks(): pl.pallas_call(functools.partial(count_kernel, group, len(given)), out_sh...  7.5 us
    dot_general x8, matrix products, shards(): jnp.dot(blocks[i], pieces[i], preferred_element_type=jnp.float32)  3.49 us
    ppermute x1, waiting for transfers between devices, shards(): lax.ppermute(there_part[batch:], ('yl', 'yh'), [(i, i ^ 3) for i in range...  3.01 us
    another operation x3, other arithmetic  1.59 us
  transfers between devices with their start and end apart: 17, of which 9 were waited for; matrix products, arithmetic and copies ran while one was open for 6% of the time, Pallas kernels for 11%

profile of v3, /device:TPU:1, one launch (start us, length us, event | category | flops | bytes accessed | tf_op | source)
XLA Modules:
  0.0 75.3 jit_solution(5682811041605407595)
XLA Ops:
  0.7 0.9 %bitcast_convert_fusion = (s16[50,256]{1,0:T(8,128)(2,1)S(1)}, s16[50,256]{1,0:T(8,128)(2,1)S(1)}) fusion(s32[256,50]{0,1:T(8,128)} %param.10, s32[256,50]{0,1:T(8,128)} %param.9), kind=kLoop, calls=%fused_computation.28 | loop fusion | flops 25600 | bytes 153600 | tf_op jit(solution)/shard_map/convert.2
  2.2 2.1 %collective-permute-start = (s16[101,256]{1,0:T(8,128)(2,1)}, s16[101,256]{1,0:T(8,128)(2,1)}, u32[]{:S(2)}, u32[]{:S(2)}) collective-permute-start(s16[101,256]{1,0:T(8,128)(2,1)} %pad_add_fusion), channel_id=1, source_target_pairs={{0,16},{16,0},{1,17},{17,1},{2,18},{18,2},{3,19},{19,3},{4,20},{20... | collective-permute-start | bytes 155144 | tf_op jit(solution)/shard_map/ppermute | solution.py:23
  4.4 1.3 %collective-permute-start.1 = (bf16[128,256]{1,0:T(8,128)(2,1)S(1)}, bf16[128,256]{1,0:T(8,128)(2,1)S(1)}, u32[]{:S(2)}, u32[]{:S(2)}) collective-permute-start(bf16[128,256]{1,0:T(8,128)(2,1)S(1)} %get-tuple-element.41), channel_id=1, source_target_pairs={{0,4},{4,0},{8,12},{12,8},{1,5},{5,1},{9,13},{13,9},{2,6},{6,2},{1... | collective-permute-start | bytes 196616 | tf_op jit(solution)/shard_map/ppermute | solution.py:23
  5.6 1.6 %collective-permute-start.3 = (bf16[128,256]{1,0:T(8,128)(2,1)S(1)}, bf16[128,256]{1,0:T(8,128)(2,1)S(1)}, u32[]{:S(2)}, u32[]{:S(2)}) collective-permute-start(bf16[128,256]{1,0:T(8,128)(2,1)S(1)} %get-tuple-element.42), channel_id=1, source_target_pairs={{0,32},{32,0},{64,96},{96,64},{1,33},{33,1},{65,97},{97,65},{2,34}... | collective-permute-start | bytes 196616 | tf_op jit(solution)/shard_map/ppermute | solution.py:23
  8.0 3.8 %counts.2 = (bf16[1024,512]{1,0:T(8,128)(2,1)S(1)}, bf16[1024,512]{1,0:T(8,128)(2,1)S(1)}, bf16[1024,512]{1,0:T(8,128)(2,1)S(1)}, bf16[1024,512]{1,0:T(8,128)(2,...) custom-call(s32[1]{0:T(128)} %bitcast.1.here_ref, ...), custom_call_target="tpu_custom_call" | custom-call | flops 2000000000 | bytes 4500000 | tf_op jit(solution)/shard_map/counts/pallas_call | solution.py:119
  11.7 1.0 %copy-done = bf16[1024,512]{1,0:T(8,128)(2,1)} copy-done((bf16[1024,512]{1,0:T(8,128)(2,1)}, bf16[1024,512]{1,0:T(8,128)(2,1)S(1)}, u32[]{:S(2)}) %copy-start) | copy-done | bytes 1048600
  12.7 1.0 %copy-done.2 = bf16[1024,512]{1,0:T(8,128)(2,1)} copy-done((bf16[1024,512]{1,0:T(8,128)(2,1)}, bf16[1024,512]{1,0:T(8,128)(2,1)S(1)}, u32[]{:S(2)}) %copy-start.2) | copy-done | bytes 1048600
  13.7 1.0 %copy-done.4 = bf16[1024,512]{1,0:T(8,128)(2,1)} copy-done((bf16[1024,512]{1,0:T(8,128)(2,1)}, bf16[1024,512]{1,0:T(8,128)(2,1)S(1)}, u32[]{:S(2)}) %copy-start.4) | copy-done | bytes 1048600
  14.7 1.0 %copy-done.6 = bf16[1024,512]{1,0:T(8,128)(2,1)} copy-done((bf16[1024,512]{1,0:T(8,128)(2,1)}, bf16[1024,512]{1,0:T(8,128)(2,1)S(1)}, u32[]{:S(2)}) %copy-start.6) | copy-done | bytes 1048600
  15.7 1.0 %copy-done.8 = bf16[1024,512]{1,0:T(8,128)(2,1)} copy-done((bf16[1024,512]{1,0:T(8,128)(2,1)}, bf16[1024,512]{1,0:T(8,128)(2,1)S(1)}, u32[]{:S(2)}) %copy-start.8) | copy-done | bytes 1048600
  17.6 1.2 %copy-done.1 = bf16[1024,512]{1,0:T(8,128)(2,1)S(1)} copy-done((bf16[1024,512]{1,0:T(8,128)(2,1)S(1)}, bf16[1024,512]{1,0:T(8,128)(2,1)}, u32[]{:S(2)}) %copy-start.1) | copy-done | bytes 1048600
  18.8 1.2 %copy-done.3 = bf16[1024,512]{1,0:T(8,128)(2,1)S(1)} copy-done((bf16[1024,512]{1,0:T(8,128)(2,1)S(1)}, bf16[1024,512]{1,0:T(8,128)(2,1)}, u32[]{:S(2)}) %copy-start.3) | copy-done | bytes 1048600
  20.0 1.2 %copy-done.5 = bf16[1024,512]{1,0:T(8,128)(2,1)S(1)} copy-done((bf16[1024,512]{1,0:T(8,128)(2,1)S(1)}, bf16[1024,512]{1,0:T(8,128)(2,1)}, u32[]{:S(2)}) %copy-start.5) | copy-done | bytes 1048600
  21.2 1.2 %copy-done.7 = bf16[1024,512]{1,0:T(8,128)(2,1)S(1)} copy-done((bf16[1024,512]{1,0:T(8,128)(2,1)S(1)}, bf16[1024,512]{1,0:T(8,128)(2,1)}, u32[]{:S(2)}) %copy-start.7) | copy-done | bytes 1048600
  22.4 1.2 %copy-done.9 = bf16[1024,512]{1,0:T(8,128)(2,1)S(1)} copy-done((bf16[1024,512]{1,0:T(8,128)(2,1)S(1)}, bf16[1024,512]{1,0:T(8,128)(2,1)}, u32[]{:S(2)}) %copy-start.9) | copy-done | bytes 1048600
  23.7 3.8 %counts.3 = (bf16[1024,512]{1,0:T(8,128)(2,1)S(1)}, bf16[1024,512]{1,0:T(8,128)(2,1)S(1)}, bf16[1024,512]{1,0:T(8,128)(2,1)S(1)}, bf16[1024,512]{1,0:T(8,128)(2,...) custom-call(s32[1]{0:T(128)} %bitcast.1.here_ref, ...), custom_call_target="tpu_custom_call", output_to_operand_aliasing={{0}: (4, {}), {1}: (5, {}), {2}: (6, {}), {3}: (7, {}), {4}... | custom-call | flops 2000000000 | bytes 4500000 | tf_op jit(solution)/shard_map/counts/pallas_call | solution.py:119
  27.5 1.9 %collective-permute-start.2 = (bf16[256,256]{1,0:T(8,128)(2,1)S(1)}, bf16[256,256]{1,0:T(8,128)(2,1)S(1)}, u32[]{:S(2)}, u32[]{:S(2)}) collective-permute-start(bf16[256,256]{1,0:T(8,128)(2,1)S(1)} %pad_maximum_fusion.2), channel_id=1, source_target_pairs={{0,12},{4,8},{8,4},{12,0},{1,13},{5,9},{9,5},{13,1},{2,14},{6,10},... | collective-permute-start | bytes 393224 | tf_op jit(solution)/shard_map/ppermute | solution.py:23
  29.4 2.3 %collective-permute-start.4 = (bf16[256,256]{1,0:T(8,128)(2,1)S(1)}, bf16[256,256]{1,0:T(8,128)(2,1)S(1)}, u32[]{:S(2)}, u32[]{:S(2)}) collective-permute-start(bf16[256,256]{1,0:T(8,128)(2,1)S(1)} %pad_maximum_fusion.3), channel_id=1, source_target_pairs={{0,96},{32,64},{64,32},{96,0},{1,97},{33,65},{65,33},{97,1},{2,98}... | collective-permute-start | bytes 393224 | tf_op jit(solution)/shard_map/ppermute | solution.py:23
  32.7 3.6 %collective-permute-start.7 = (bf16[512,256]{1,0:T(8,128)(2,1)S(1)}, bf16[512,256]{1,0:T(8,128)(2,1)S(1)}, u32[]{:S(2)}, u32[]{:S(2)}) collective-permute-start(bf16[512,256]{1,0:T(8,128)(2,1)S(1)} %pad_maximum_fusion), channel_id=1, source_target_pairs={{0,96},{32,64},{64,32},{96,0},{1,97},{33,65},{65,33},{97,1},{2,98}... | collective-permute-start | bytes 786440 | tf_op jit(solution)/shard_map/ppermute | solution.py:23
  36.4 1.9 %collective-permute-start.8 = (bf16[512,256]{1,0:T(8,128)(2,1)S(1)}, bf16[512,256]{1,0:T(8,128)(2,1)S(1)}, u32[]{:S(2)}, u32[]{:S(2)}) collective-permute-start(bf16[512,256]{1,0:T(8,128)(2,1)S(1)} %pad_maximum_fusion.1), channel_id=1, source_target_pairs={{0,12},{4,8},{8,4},{12,0},{1,13},{5,9},{9,5},{13,1},{2,14},{6,10},... | collective-permute-start | bytes 786440 | tf_op jit(solution)/shard_map/ppermute | solution.py:23
  38.8 1.3 %collective-permute-done.7 = bf16[512,256]{1,0:T(8,128)(2,1)S(1)} collective-permute-done((bf16[512,256]{1,0:T(8,128)(2,1)S(1)}, bf16[512,256]{1,0:T(8,128)(2,1)S(1)}, u32[]{:S(2)}, u32[]{:S(2)}) %collective-permute-start.7) | collective-permute-done | bytes 262176 | tf_op jit(solution)/shard_map/ppermute | solution.py:23
  40.5 2.7 %collective-permute-done.8 = bf16[512,256]{1,0:T(8,128)(2,1)S(1)} collective-permute-done((bf16[512,256]{1,0:T(8,128)(2,1)S(1)}, bf16[512,256]{1,0:T(8,128)(2,1)S(1)}, u32[]{:S(2)}, u32[]{:S(2)}) %collective-permute-start.8) | collective-permute-done | bytes 262176 | tf_op jit(solution)/shard_map/ppermute | solution.py:23
  46.0 2.8 %collective-permute-done.10 = bf16[512,256]{1,0:T(8,128)(2,1)S(1)} collective-permute-done((bf16[512,256]{1,0:T(8,128)(2,1)S(1)}, bf16[512,256]{1,0:T(8,128)(2,1)S(1)}, u32[]{:S(2)}, u32[]{:S(2)}) %collective-permute-start.10) | collective-permute-done | bytes 262176 | tf_op jit(solution)/shard_map/ppermute | solution.py:23
  51.1 5.0 %collective-permute-start.11 = (f16[512,512]{1,0:T(8,128)(2,1)S(1)}, f16[512,512]{1,0:T(8,128)(2,1)}, u32[]{:S(2)}, u32[]{:S(2)}) collective-permute-start(f16[512,512]{1,0:T(8,128)(2,1)S(1)} %convert_element_type.32), channel_id=1, source_target_pairs={{0,1},{1,0},{2,3},{3,2},{4,5},{5,4},{6,7},{7,6},{8,9},{9,8},{10,11... | collective-permute-start | bytes 1572872 | tf_op jit(solution)/shard_map/ppermute | solution.py:23
  56.7 1.1 %collective-permute-done.11 = f16[512,512]{1,0:T(8,128)(2,1)} collective-permute-done((f16[512,512]{1,0:T(8,128)(2,1)S(1)}, f16[512,512]{1,0:T(8,128)(2,1)}, u32[]{:S(2)}, u32[]{:S(2)}) %collective-permute-start.11) | collective-permute-done | bytes 524320 | tf_op jit(solution)/shard_map/ppermute | solution.py:23
  57.8 1.2 %convert_add_fusion = f32[512,512]{1,0:T(8,128)S(1)} fusion(f32[512,512]{1,0:T(8,128)S(1)} %project.2, f16[512,512]{1,0:T(8,128)(2,1)} %collective-permute-done.11), kind=kLoop, calls=%fused_computation.7 | loop fusion | flops 524288 | bytes 2621440 | tf_op jit(solution)/shard_map/add | solution.py:211
  59.1 2.7 %collective-permute-start.12 = (f16[256,256]{1,0:T(8,128)(2,1)S(1)}, f16[256,256]{1,0:T(8,128)(2,1)S(1)}, u32[]{:S(2)}, u32[]{:S(2)}) collective-permute-start(f16[256,256]{1,0:T(8,128)(2,1)S(1)} %get-tuple-element.39), channel_id=1, source_target_pairs={{0,2},{2,0},{1,3},{3,1},{4,6},{6,4},{5,7},{7,5},{8,10},{10,8},{9,1... | collective-permute-start | bytes 393224 | tf_op jit(solution)/shard_map/ppermute | solution.py:23
  62.7 2.7 %collective-permute-done.12 = f16[256,256]{1,0:T(8,128)(2,1)S(1)} collective-permute-done((f16[256,256]{1,0:T(8,128)(2,1)S(1)}, f16[256,256]{1,0:T(8,128)(2,1)S(1)}, u32[]{:S(2)}, u32[]{:S(2)}) %collective-permute-start.12) | collective-permute-done | bytes 131104 | tf_op jit(solution)/shard_map/ppermute | solution.py:23
  65.4 3.0 %collective-permute-done.14 = f16[256,256]{1,0:T(8,128)(2,1)S(1)} collective-permute-done((f16[256,256]{1,0:T(8,128)(2,1)S(1)}, f16[256,256]{1,0:T(8,128)(2,1)S(1)}, u32[]{:S(2)}, u32[]{:S(2)}) %collective-permute-start.14) | collective-permute-done | bytes 131104 | tf_op jit(solution)/shard_map/ppermute | solution.py:217
  68.6 1.1 %collective-permute-start.15 = (f32[256]{0:T(256)S(1)}, f32[256]{0:T(256)S(1)}, u32[]{:S(2)}, u32[]{:S(2)}) collective-permute-start(f32[256]{0:T(256)S(1)} %multiply_reduce_fusion), channel_id=1, source_target_pairs={{0,1},{1,0},{2,3},{3,2},{4,5},{5,4},{6,7},{7,6},{8,9},{9,8},{10,11... | collective-permute-start | bytes 3080 | tf_op jit(solution)/shard_map/ppermute | solution.py:23
  70.5 1.5 %collective-permute-start.16 = (f32[256]{0:T(256)S(1)}, f32[256]{0:T(256)S(1)}, u32[]{:S(2)}, u32[]{:S(2)}) collective-permute-start(f32[256]{0:T(256)S(1)} %add.82), channel_id=1, source_target_pairs={{0,2},{2,0},{1,3},{3,1},{4,6},{6,4},{5,7},{7,5},{8,10},{10,8},{9,1... | collective-permute-start | bytes 3080 | tf_op jit(solution)/shard_map/ppermute | solution.py:23
  72.0 2.5 %collective-permute-done.16 = f32[256]{0:T(256)S(1)} collective-permute-done((f32[256]{0:T(256)S(1)}, f32[256]{0:T(256)S(1)}, u32[]{:S(2)}, u32[]{:S(2)}) %collective-permute-start.16) | collective-permute-done | bytes 1056 | tf_op jit(solution)/shard_map/ppermute | solution.py:23
  (76 shorter events, 13.3 us)
Async XLA Ops:
  0.7 3.7 %copy-start.17 = (bf16[256,256]{1,0:T(8,128)(2,1)S(1)}, bf16[256,256]{1,0:T(8,128)(2,1)}, u32[]{:S(2)}) copy-start(bf16[256,256]{1,0:T(8,128)(2,1)} %param.7) | copy-start | bytes 393220
  2.2 5.1 %copy-start.14 = (s32[256,50]{0,1:T(8,128)S(1)}, s32[256,50]{0,1:T(8,128)}, u32[]{:S(2)}) copy-start(s32[256,50]{0,1:T(8,128)} %param.10) | copy-start | bytes 153604
  2.2 5.1 %copy-start.15 = (s32[256,50]{0,1:T(8,128)S(1)}, s32[256,50]{0,1:T(8,128)}, u32[]{:S(2)}) copy-start(s32[256,50]{0,1:T(8,128)} %param.9) | copy-start | bytes 153604
  2.2 14.5 %collective-permute-start = (s16[101,256]{1,0:T(8,128)(2,1)}, s16[101,256]{1,0:T(8,128)(2,1)}, u32[]{:S(2)}, u32[]{:S(2)}) collective-permute-start(s16[101,256]{1,0:T(8,128)(2,1)} %pad_add_fusion), channel_id=1, source_target_pairs={{0,16},{16,0},{1,17},{17,1},{2,18},{18,2},{3,19},{19,3},{4,20},{20... | collective-permute-start | bytes 155144 | tf_op jit(solution)/shard_map/ppermute | solution.py:23
  4.4 23.1 %collective-permute-start.1 = (bf16[128,256]{1,0:T(8,128)(2,1)S(1)}, bf16[128,256]{1,0:T(8,128)(2,1)S(1)}, u32[]{:S(2)}, u32[]{:S(2)}) collective-permute-start(bf16[128,256]{1,0:T(8,128)(2,1)S(1)} %get-tuple-element.41), channel_id=1, source_target_pairs={{0,4},{4,0},{8,12},{12,8},{1,5},{5,1},{9,13},{13,9},{2,6},{6,2},{1... | collective-permute-start | bytes 196616 | tf_op jit(solution)/shard_map/ppermute | solution.py:23
  5.6 23.7 %collective-permute-start.3 = (bf16[128,256]{1,0:T(8,128)(2,1)S(1)}, bf16[128,256]{1,0:T(8,128)(2,1)S(1)}, u32[]{:S(2)}, u32[]{:S(2)}) collective-permute-start(bf16[128,256]{1,0:T(8,128)(2,1)S(1)} %get-tuple-element.42), channel_id=1, source_target_pairs={{0,32},{32,0},{64,96},{96,64},{1,33},{33,1},{65,97},{97,65},{2,34}... | collective-permute-start | bytes 196616 | tf_op jit(solution)/shard_map/ppermute | solution.py:23
  12.7 1.0 %copy-start.2 = (bf16[1024,512]{1,0:T(8,128)(2,1)}, bf16[1024,512]{1,0:T(8,128)(2,1)S(1)}, u32[]{:S(2)}) copy-start(bf16[1024,512]{1,0:T(8,128)(2,1)S(1)} %get-tuple-element.26.rest_5_) | copy-start | bytes 3145732
  14.6 1.0 %copy-start.6 = (bf16[1024,512]{1,0:T(8,128)(2,1)}, bf16[1024,512]{1,0:T(8,128)(2,1)S(1)}, u32[]{:S(2)}) copy-start(bf16[1024,512]{1,0:T(8,128)(2,1)S(1)} %get-tuple-element.28.rest_7_) | copy-start | bytes 3145732
  15.7 1.0 %copy-start.8 = (bf16[1024,512]{1,0:T(8,128)(2,1)}, bf16[1024,512]{1,0:T(8,128)(2,1)S(1)}, u32[]{:S(2)}) copy-start(bf16[1024,512]{1,0:T(8,128)(2,1)S(1)} %get-tuple-element.21.rest_0_) | copy-start | bytes 3145732
  17.5 1.2 %copy-start.1 = (bf16[1024,512]{1,0:T(8,128)(2,1)S(1)}, bf16[1024,512]{1,0:T(8,128)(2,1)}, u32[]{:S(2)}) copy-start(bf16[1024,512]{1,0:T(8,128)(2,1)} %copy-done) | copy-start | bytes 3145732
  18.8 1.2 %copy-start.3 = (bf16[1024,512]{1,0:T(8,128)(2,1)S(1)}, bf16[1024,512]{1,0:T(8,128)(2,1)}, u32[]{:S(2)}) copy-start(bf16[1024,512]{1,0:T(8,128)(2,1)} %copy-done.2) | copy-start | bytes 3145732
  20.0 1.2 %copy-start.5 = (bf16[1024,512]{1,0:T(8,128)(2,1)S(1)}, bf16[1024,512]{1,0:T(8,128)(2,1)}, u32[]{:S(2)}) copy-start(bf16[1024,512]{1,0:T(8,128)(2,1)} %copy-done.4) | copy-start | bytes 3145732
  21.2 1.2 %copy-start.7 = (bf16[1024,512]{1,0:T(8,128)(2,1)S(1)}, bf16[1024,512]{1,0:T(8,128)(2,1)}, u32[]{:S(2)}) copy-start(bf16[1024,512]{1,0:T(8,128)(2,1)} %copy-done.6) | copy-start | bytes 3145732
  22.4 1.2 %copy-start.9 = (bf16[1024,512]{1,0:T(8,128)(2,1)S(1)}, bf16[1024,512]{1,0:T(8,128)(2,1)}, u32[]{:S(2)}) copy-start(bf16[1024,512]{1,0:T(8,128)(2,1)} %copy-done.8) | copy-start | bytes 3145732
  27.4 11.3 %copy-start.10 = (bf16[1024,512]{1,0:T(8,128)(2,1)}, bf16[1024,512]{1,0:T(8,128)(2,1)S(1)}, u32[]{:S(2)}) copy-start(bf16[1024,512]{1,0:T(8,128)(2,1)S(1)} %get-tuple-element.29) | copy-start | bytes 3145732
  27.5 5.1 %collective-permute-start.2 = (bf16[256,256]{1,0:T(8,128)(2,1)S(1)}, bf16[256,256]{1,0:T(8,128)(2,1)S(1)}, u32[]{:S(2)}, u32[]{:S(2)}) collective-permute-start(bf16[256,256]{1,0:T(8,128)(2,1)S(1)} %pad_maximum_fusion.2), channel_id=1, source_target_pairs={{0,12},{4,8},{8,4},{12,0},{1,13},{5,9},{9,5},{13,1},{2,14},{6,10},... | collective-permute-start | bytes 393224 | tf_op jit(solution)/shard_map/ppermute | solution.py:23
  29.4 6.9 %collective-permute-start.4 = (bf16[256,256]{1,0:T(8,128)(2,1)S(1)}, bf16[256,256]{1,0:T(8,128)(2,1)S(1)}, u32[]{:S(2)}, u32[]{:S(2)}) collective-permute-start(bf16[256,256]{1,0:T(8,128)(2,1)S(1)} %pad_maximum_fusion.3), channel_id=1, source_target_pairs={{0,96},{32,64},{64,32},{96,0},{1,97},{33,65},{65,33},{97,1},{2,98}... | collective-permute-start | bytes 393224 | tf_op jit(solution)/shard_map/ppermute | solution.py:23
  32.6 11.2 %collective-permute-start.5 = (bf16[512,256]{1,0:T(8,128)(2,1)S(1)}, bf16[512,256]{1,0:T(8,128)(2,1)S(1)}, u32[]{:S(2)}, u32[]{:S(2)}) collective-permute-start(bf16[512,256]{1,0:T(8,128)(2,1)S(1)} %pad_maximum_fusion), channel_id=1, source_target_pairs={{0,32},{32,0},{64,96},{96,64},{1,33},{33,1},{65,97},{97,65},{2,34}... | collective-permute-start | bytes 786440 | tf_op jit(solution)/shard_map/ppermute | solution.py:23
  32.7 7.3 %collective-permute-start.7 = (bf16[512,256]{1,0:T(8,128)(2,1)S(1)}, bf16[512,256]{1,0:T(8,128)(2,1)S(1)}, u32[]{:S(2)}, u32[]{:S(2)}) collective-permute-start(bf16[512,256]{1,0:T(8,128)(2,1)S(1)} %pad_maximum_fusion), channel_id=1, source_target_pairs={{0,96},{32,64},{64,32},{96,0},{1,97},{33,65},{65,33},{97,1},{2,98}... | collective-permute-start | bytes 786440 | tf_op jit(solution)/shard_map/ppermute | solution.py:23
  36.3 7.9 %collective-permute-start.6 = (bf16[512,256]{1,0:T(8,128)(2,1)S(1)}, bf16[512,256]{1,0:T(8,128)(2,1)S(1)}, u32[]{:S(2)}, u32[]{:S(2)}) collective-permute-start(bf16[512,256]{1,0:T(8,128)(2,1)S(1)} %pad_maximum_fusion.1), channel_id=1, source_target_pairs={{0,4},{4,0},{8,12},{12,8},{1,5},{5,1},{9,13},{13,9},{2,6},{6,2},{1... | collective-permute-start | bytes 786440 | tf_op jit(solution)/shard_map/ppermute | solution.py:23
  36.4 6.8 %collective-permute-start.8 = (bf16[512,256]{1,0:T(8,128)(2,1)S(1)}, bf16[512,256]{1,0:T(8,128)(2,1)S(1)}, u32[]{:S(2)}, u32[]{:S(2)}) collective-permute-start(bf16[512,256]{1,0:T(8,128)(2,1)S(1)} %pad_maximum_fusion.1), channel_id=1, source_target_pairs={{0,12},{4,8},{8,4},{12,0},{1,13},{5,9},{9,5},{13,1},{2,14},{6,10},... | collective-permute-start | bytes 786440 | tf_op jit(solution)/shard_map/ppermute | solution.py:23
  40.0 9.1 %collective-permute-start.9 = (bf16[512,256]{1,0:T(8,128)(2,1)S(1)}, bf16[512,256]{1,0:T(8,128)(2,1)S(1)}, u32[]{:S(2)}, u32[]{:S(2)}) collective-permute-start(bf16[512,256]{1,0:T(8,128)(2,1)S(1)} %collective-permute-done.7), channel_id=1, source_target_pairs={{0,32},{32,0},{64,96},{96,64},{1,33},{33,1},{65,97},{97,65},{2,34}... | collective-permute-start | bytes 786440 | tf_op jit(solution)/shard_map/ppermute | solution.py:23
  43.2 5.5 %collective-permute-start.10 = (bf16[512,256]{1,0:T(8,128)(2,1)S(1)}, bf16[512,256]{1,0:T(8,128)(2,1)S(1)}, u32[]{:S(2)}, u32[]{:S(2)}) collective-permute-start(bf16[512,256]{1,0:T(8,128)(2,1)S(1)} %collective-permute-done.8), channel_id=1, source_target_pairs={{0,4},{4,0},{8,12},{12,8},{1,5},{5,1},{9,13},{13,9},{2,6},{6,2},{1... | collective-permute-start | bytes 786440 | tf_op jit(solution)/shard_map/ppermute | solution.py:23
  44.3 1.2 %copy-start.11 = (bf16[1024,512]{1,0:T(8,128)(2,1)S(1)}, bf16[1024,512]{1,0:T(8,128)(2,1)}, u32[]{:S(2)}) copy-start(bf16[1024,512]{1,0:T(8,128)(2,1)} %copy-done.10) | copy-start | bytes 3145732
  49.2 1.0 %copy-start.12 = (bf16[256,1024]{1,0:T(8,128)(2,1)S(1)}, bf16[256,1024]{1,0:T(8,128)(2,1)}, u32[]{:S(2)}) copy-start(bf16[256,1024]{1,0:T(8,128)(2,1)} %self_ref.3) | copy-start | bytes 1572868
  49.2 1.2 %copy-start.13 = (bf16[256,1024]{1,0:T(8,128)(2,1)S(1)}, bf16[256,1024]{1,0:T(8,128)(2,1)}, u32[]{:S(2)}) copy-start(bf16[256,1024]{1,0:T(8,128)(2,1)} %nbr_ref.3) | copy-start | bytes 1572868
  51.1 6.7 %collective-permute-start.11 = (f16[512,512]{1,0:T(8,128)(2,1)S(1)}, f16[512,512]{1,0:T(8,128)(2,1)}, u32[]{:S(2)}, u32[]{:S(2)}) collective-permute-start(f16[512,512]{1,0:T(8,128)(2,1)S(1)} %convert_element_type.32), channel_id=1, source_target_pairs={{0,1},{1,0},{2,3},{3,2},{4,5},{5,4},{6,7},{7,6},{8,9},{9,8},{10,11... | collective-permute-start | bytes 1572872 | tf_op jit(solution)/shard_map/ppermute | solution.py:23
  59.1 6.3 %collective-permute-start.12 = (f16[256,256]{1,0:T(8,128)(2,1)S(1)}, f16[256,256]{1,0:T(8,128)(2,1)S(1)}, u32[]{:S(2)}, u32[]{:S(2)}) collective-permute-start(f16[256,256]{1,0:T(8,128)(2,1)S(1)} %get-tuple-element.39), channel_id=1, source_target_pairs={{0,2},{2,0},{1,3},{3,1},{4,6},{6,4},{5,7},{7,5},{8,10},{10,8},{9,1... | collective-permute-start | bytes 393224 | tf_op jit(solution)/shard_map/ppermute | solution.py:23
  61.8 6.6 %collective-permute-start.14 = (f16[256,256]{1,0:T(8,128)(2,1)S(1)}, f16[256,256]{1,0:T(8,128)(2,1)S(1)}, u32[]{:S(2)}, u32[]{:S(2)}) collective-permute-start(f16[256,256]{1,0:T(8,128)(2,1)S(1)} %get-tuple-element.40), channel_id=1, source_target_pairs={{0,18},{2,16},{16,2},{18,0},{1,19},{3,17},{17,3},{19,1},{4,22},{6,... | collective-permute-start | bytes 393224 | tf_op jit(solution)/shard_map/ppermute | solution.py:217
  61.8 6.6 %collective-permute-start.13 = (f16[256,256]{1,0:T(8,128)(2,1)S(1)}, f16[256,256]{1,0:T(8,128)(2,1)S(1)}, u32[]{:S(2)}, u32[]{:S(2)}) collective-permute-start(f16[256,256]{1,0:T(8,128)(2,1)S(1)} %slice_convert_fusion), channel_id=1, source_target_pairs={{0,16},{16,0},{1,17},{17,1},{2,18},{18,2},{3,19},{19,3},{4,20},{20... | collective-permute-start | bytes 393224 | tf_op jit(solution)/shard_map/ppermute | solution.py:23
  68.6 1.9 %collective-permute-start.15 = (f32[256]{0:T(256)S(1)}, f32[256]{0:T(256)S(1)}, u32[]{:S(2)}, u32[]{:S(2)}) collective-permute-start(f32[256]{0:T(256)S(1)} %multiply_reduce_fusion), channel_id=1, source_target_pairs={{0,1},{1,0},{2,3},{3,2},{4,5},{5,4},{6,7},{7,6},{8,9},{9,8},{10,11... | collective-permute-start | bytes 3080 | tf_op jit(solution)/shard_map/ppermute | solution.py:23
  70.5 3.9 %collective-permute-start.16 = (f32[256]{0:T(256)S(1)}, f32[256]{0:T(256)S(1)}, u32[]{:S(2)}, u32[]{:S(2)}) collective-permute-start(f32[256]{0:T(256)S(1)} %add.82), channel_id=1, source_target_pairs={{0,2},{2,0},{1,3},{3,1},{4,6},{6,4},{5,7},{7,5},{8,10},{10,8},{9,1... | collective-permute-start | bytes 3080 | tf_op jit(solution)/shard_map/ppermute | solution.py:23
  (3 other events, 2.6 us)

commit v4 on v3

--- a/solution.py
+++ b/solution.py
@@ -180,7 +180,8 @@
     here = lax.axis_index(DOM).reshape(1)
 
     table = jnp.concatenate([neighbor_ids.T, visit_counts.T, self_ids[None, :]], axis=0)
-    theirs = moved(table.astype(jnp.int16), "yl", lambda i: i ^ 1).astype(jnp.int32)
+    sent = lax.optimization_barrier(table).astype(jnp.int16)
+    theirs = moved(sent, "yl", lambda i: i ^ 1).astype(jnp.int32)
 
     axes = [("x", "z"), ("z", "x")]
     halves = [items[:half], items[half:]]
@@ -191,8 +192,13 @@
         lines.append(jnp.concatenate([pair, rest], axis=0))
     pieces = []
     for line, (_, far) in zip(lines, axes):
-        low, high = moved(line, far, lambda i: i ^ 1), moved(line, far, lambda i: i ^ 3)
-        pieces += [line, low, high, moved(high, far, lambda i: i ^ 1)]
+        low = moved(line, far, lambda i: i ^ 1)
+        high = moved(line, far, lambda i: i ^ 3)
+        middle = line.shape[0] // 2
+        last = [
+            moved(high[:middle], far, lambda i: i ^ 1), moved(low[middle:], far, lambda i: i ^ 3)
+        ]
+        pieces += [line, low, high, jnp.concatenate(last, axis=0)]
 
     widths = [p.shape[0] for p in pieces]
     blocks = count_blocks(0, [], here, table, nbr, widths)

time: 75.9 us -> 77.3 us (1.018)
  starting transfers between devices: 25.5 us -> 31.1 us
  waiting for transfers between devices: 17.7 us -> 14.9 us
  local copies, waits for them, and re-layouts: 14.1 us -> 13.2 us
    ppermute x16 -> x18, starting transfers between devices: 25.5 us -> 31.1 us  [moved(): return lax.ppermute(value, axis, [(i, target(i) % n) for i in range(n)])]
    ppermute x16 -> x18, waiting for transfers between devices: 14.7 us -> 11.9 us  [moved(): return lax.ppermute(value, axis, [(i, target(i) % n) for i in range(n)])]
    another operation x3 -> x1, other arithmetic: 1.59 us -> 0.02 us
    unnamed x36 -> x32, local copies, waits for them, and re-layouts: 13.1 us -> 12.2 us
  transfers between devices with their start and end apart: 17 -> 19, of which waited for: 9 -> 10; matrix products, arithmetic and copies ran while one was open for 6% -> 6% of each run, Pallas kernels for 11% -> 11%
where the time goes in v4:
time: 77.3 us; the launch traced here: 76.6 us
  starting transfers between devices  31.1 us (40%)
  waiting for transfers between devices  14.9 us (19%)
  local copies, waits for them, and re-layouts  13.2 us (17%)
  Pallas kernels  8.68 us (11%)
  other arithmetic  4.82 us (6%)
  matrix products  3.57 us (5%)
    ppermute x18, starting transfers between devices, moved(): return lax.ppermute(value, axis, [(i, target(i) % n) for i in range(n)])  31.1 us
    unnamed x32, local copies, waits for them, and re-layouts  12.2 us
    ppermute x18, waiting for transfers between devices, moved(): return lax.ppermute(value, axis, [(i, target(i) % n) for i in range(n)])  11.9 us
    pallas_call x2, Pallas kernels, count_blocks(): pl.pallas_call(functools.partial(count_kernel, group, len(given)), out_sh...  7.5 us
    dot_general x8, matrix products, shards(): jnp.dot(blocks[i], pieces[i], preferred_element_type=jnp.float32)  3.57 us
    ppermute x1, waiting for transfers between devices, shards(): lax.ppermute(there_part[batch:], ('yl', 'yh'), [(i, i ^ 3) for i in range...  3 us
  transfers between devices with their start and end apart: 19, of which 10 were waited for; matrix products, arithmetic and copies ran while one was open for 6% of the time, Pallas kernels for 11%

profile of v4, /device:TPU:1, one launch (start us, length us, event | category | flops | bytes accessed | tf_op | source)
XLA Modules:
  0.0 76.6 jit_solution(14355405900453943608)
XLA Ops:
  2.2 2.1 %collective-permute-start = (s16[101,256]{1,0:T(8,128)(2,1)}, s16[101,256]{1,0:T(8,128)(2,1)}, u32[]{:S(2)}, u32[]{:S(2)}) collective-permute-start(s16[101,256]{1,0:T(8,128)(2,1)} %convert_element_type.31), channel_id=1, source_target_pairs={{0,16},{16,0},{1,17},{17,1},{2,18},{18,2},{3,19},{19,3},{4,20},{20... | collective-permute-start | bytes 155144 | tf_op jit(solution)/shard_map/ppermute | solution.py:23
  4.3 1.3 %collective-permute-start.1 = (bf16[128,256]{1,0:T(8,128)(2,1)S(1)}, bf16[128,256]{1,0:T(8,128)(2,1)S(1)}, u32[]{:S(2)}, u32[]{:S(2)}) collective-permute-start(bf16[128,256]{1,0:T(8,128)(2,1)S(1)} %get-tuple-element.41), channel_id=1, source_target_pairs={{0,4},{4,0},{8,12},{12,8},{1,5},{5,1},{9,13},{13,9},{2,6},{6,2},{1... | collective-permute-start | bytes 196616 | tf_op jit(solution)/shard_map/ppermute | solution.py:23
  5.6 1.6 %collective-permute-start.3 = (bf16[128,256]{1,0:T(8,128)(2,1)S(1)}, bf16[128,256]{1,0:T(8,128)(2,1)S(1)}, u32[]{:S(2)}, u32[]{:S(2)}) collective-permute-start(bf16[128,256]{1,0:T(8,128)(2,1)S(1)} %get-tuple-element.42), channel_id=1, source_target_pairs={{0,32},{32,0},{64,96},{96,64},{1,33},{33,1},{65,97},{97,65},{2,34}... | collective-permute-start | bytes 196616 | tf_op jit(solution)/shard_map/ppermute | solution.py:23
  7.3 3.7 %counts.2 = (bf16[1024,512]{1,0:T(8,128)(2,1)S(1)}, bf16[1024,512]{1,0:T(8,128)(2,1)S(1)}, bf16[1024,512]{1,0:T(8,128)(2,1)S(1)}, bf16[1024,512]{1,0:T(8,128)(2,...) custom-call(s32[1]{0:T(128)} %bitcast.1.here_ref, ...), custom_call_target="tpu_custom_call" | custom-call | flops 2000000000 | bytes 4500000 | tf_op jit(solution)/shard_map/counts/pallas_call | solution.py:119
  11.0 1.0 %copy-done = bf16[1024,512]{1,0:T(8,128)(2,1)} copy-done((bf16[1024,512]{1,0:T(8,128)(2,1)}, bf16[1024,512]{1,0:T(8,128)(2,1)S(1)}, u32[]{:S(2)}) %copy-start) | copy-done | bytes 1048600
  12.0 1.0 %copy-done.2 = bf16[1024,512]{1,0:T(8,128)(2,1)} copy-done((bf16[1024,512]{1,0:T(8,128)(2,1)}, bf16[1024,512]{1,0:T(8,128)(2,1)S(1)}, u32[]{:S(2)}) %copy-start.2) | copy-done | bytes 1048600
  13.0 1.0 %copy-done.4 = bf16[1024,512]{1,0:T(8,128)(2,1)} copy-done((bf16[1024,512]{1,0:T(8,128)(2,1)}, bf16[1024,512]{1,0:T(8,128)(2,1)S(1)}, u32[]{:S(2)}) %copy-start.4) | copy-done | bytes 1048600
  14.0 1.0 %copy-done.6 = bf16[1024,512]{1,0:T(8,128)(2,1)} copy-done((bf16[1024,512]{1,0:T(8,128)(2,1)}, bf16[1024,512]{1,0:T(8,128)(2,1)S(1)}, u32[]{:S(2)}) %copy-start.6) | copy-done | bytes 1048600
  14.9 1.0 %copy-done.8 = bf16[1024,512]{1,0:T(8,128)(2,1)} copy-done((bf16[1024,512]{1,0:T(8,128)(2,1)}, bf16[1024,512]{1,0:T(8,128)(2,1)S(1)}, u32[]{:S(2)}) %copy-start.8) | copy-done | bytes 1048600
  16.8 1.2 %copy-done.1 = bf16[1024,512]{1,0:T(8,128)(2,1)S(1)} copy-done((bf16[1024,512]{1,0:T(8,128)(2,1)S(1)}, bf16[1024,512]{1,0:T(8,128)(2,1)}, u32[]{:S(2)}) %copy-start.1) | copy-done | bytes 1048600
  18.1 1.2 %copy-done.3 = bf16[1024,512]{1,0:T(8,128)(2,1)S(1)} copy-done((bf16[1024,512]{1,0:T(8,128)(2,1)S(1)}, bf16[1024,512]{1,0:T(8,128)(2,1)}, u32[]{:S(2)}) %copy-start.3) | copy-done | bytes 1048600
  19.3 1.2 %copy-done.5 = bf16[1024,512]{1,0:T(8,128)(2,1)S(1)} copy-done((bf16[1024,512]{1,0:T(8,128)(2,1)S(1)}, bf16[1024,512]{1,0:T(8,128)(2,1)}, u32[]{:S(2)}) %copy-start.5) | copy-done | bytes 1048600
  20.5 1.2 %copy-done.7 = bf16[1024,512]{1,0:T(8,128)(2,1)S(1)} copy-done((bf16[1024,512]{1,0:T(8,128)(2,1)S(1)}, bf16[1024,512]{1,0:T(8,128)(2,1)}, u32[]{:S(2)}) %copy-start.7) | copy-done | bytes 1048600
  21.7 1.2 %copy-done.9 = bf16[1024,512]{1,0:T(8,128)(2,1)S(1)} copy-done((bf16[1024,512]{1,0:T(8,128)(2,1)S(1)}, bf16[1024,512]{1,0:T(8,128)(2,1)}, u32[]{:S(2)}) %copy-start.9) | copy-done | bytes 1048600
  23.0 3.8 %counts.3 = (bf16[1024,512]{1,0:T(8,128)(2,1)S(1)}, bf16[1024,512]{1,0:T(8,128)(2,1)S(1)}, bf16[1024,512]{1,0:T(8,128)(2,1)S(1)}, bf16[1024,512]{1,0:T(8,128)(2,...) custom-call(s32[1]{0:T(128)} %bitcast.1.here_ref, ...), custom_call_target="tpu_custom_call", output_to_operand_aliasing={{0}: (4, {}), {1}: (5, {}), {2}: (6, {}), {3}: (7, {}), {4}... | custom-call | flops 2000000000 | bytes 4500000 | tf_op jit(solution)/shard_map/counts/pallas_call | solution.py:119
  26.8 1.9 %collective-permute-start.2 = (bf16[256,256]{1,0:T(8,128)(2,1)S(1)}, bf16[256,256]{1,0:T(8,128)(2,1)S(1)}, u32[]{:S(2)}, u32[]{:S(2)}) collective-permute-start(bf16[256,256]{1,0:T(8,128)(2,1)S(1)} %pad_maximum_fusion.2), channel_id=1, source_target_pairs={{0,12},{4,8},{8,4},{12,0},{1,13},{5,9},{9,5},{13,1},{2,14},{6,10},... | collective-permute-start | bytes 393224 | tf_op jit(solution)/shard_map/ppermute | solution.py:23
  28.7 2.3 %collective-permute-start.4 = (bf16[256,256]{1,0:T(8,128)(2,1)S(1)}, bf16[256,256]{1,0:T(8,128)(2,1)S(1)}, u32[]{:S(2)}, u32[]{:S(2)}) collective-permute-start(bf16[256,256]{1,0:T(8,128)(2,1)S(1)} %pad_maximum_fusion.3), channel_id=1, source_target_pairs={{0,96},{32,64},{64,32},{96,0},{1,97},{33,65},{65,33},{97,1},{2,98}... | collective-permute-start | bytes 393224 | tf_op jit(solution)/shard_map/ppermute | solution.py:23
  32.0 3.6 %collective-permute-start.7 = (bf16[512,256]{1,0:T(8,128)(2,1)S(1)}, bf16[512,256]{1,0:T(8,128)(2,1)S(1)}, u32[]{:S(2)}, u32[]{:S(2)}) collective-permute-start(bf16[512,256]{1,0:T(8,128)(2,1)S(1)} %pad_maximum_fusion), channel_id=1, source_target_pairs={{0,96},{32,64},{64,32},{96,0},{1,97},{33,65},{65,33},{97,1},{2,98}... | collective-permute-start | bytes 786440 | tf_op jit(solution)/shard_map/ppermute | solution.py:23
  35.6 1.9 %collective-permute-start.8 = (bf16[512,256]{1,0:T(8,128)(2,1)S(1)}, bf16[512,256]{1,0:T(8,128)(2,1)S(1)}, u32[]{:S(2)}, u32[]{:S(2)}) collective-permute-start(bf16[512,256]{1,0:T(8,128)(2,1)S(1)} %pad_maximum_fusion.1), channel_id=1, source_target_pairs={{0,12},{4,8},{8,4},{12,0},{1,13},{5,9},{9,5},{13,1},{2,14},{6,10},... | collective-permute-start | bytes 786440 | tf_op jit(solution)/shard_map/ppermute | solution.py:23
  38.0 1.6 %collective-permute-start.10 = (bf16[256,256]{1,0:T(8,128)(2,1)S(1)}, bf16[256,256]{1,0:T(8,128)(2,1)S(1)}, u32[]{:S(2)}, u32[]{:S(2)}) collective-permute-start(bf16[256,256]{1,0:T(8,128)(2,1)S(1)} %slice.66), channel_id=1, source_target_pairs={{0,96},{32,64},{64,32},{96,0},{1,97},{33,65},{65,33},{97,1},{2,98}... | collective-permute-start | bytes 393224 | tf_op jit(solution)/shard_map/ppermute | solution.py:23
  40.4 2.0 %collective-permute-done.8 = bf16[512,256]{1,0:T(8,128)(2,1)S(1)} collective-permute-done((bf16[512,256]{1,0:T(8,128)(2,1)S(1)}, bf16[512,256]{1,0:T(8,128)(2,1)S(1)}, u32[]{:S(2)}, u32[]{:S(2)}) %collective-permute-start.8) | collective-permute-done | bytes 262176 | tf_op jit(solution)/shard_map/ppermute | solution.py:23
  43.0 1.4 %collective-permute-start.12 = (bf16[256,256]{1,0:T(8,128)(2,1)S(1)}, bf16[256,256]{1,0:T(8,128)(2,1)S(1)}, u32[]{:S(2)}, u32[]{:S(2)}) collective-permute-start(bf16[256,256]{1,0:T(8,128)(2,1)S(1)} %slice.68), channel_id=1, source_target_pairs={{0,12},{4,8},{8,4},{12,0},{1,13},{5,9},{9,5},{13,1},{2,14},{6,10},... | collective-permute-start | bytes 393224 | tf_op jit(solution)/shard_map/ppermute | solution.py:23
  46.6 1.4 %collective-permute-done.11 = bf16[256,256]{1,0:T(8,128)(2,1)S(1)} collective-permute-done((bf16[256,256]{1,0:T(8,128)(2,1)S(1)}, bf16[256,256]{1,0:T(8,128)(2,1)S(1)}, u32[]{:S(2)}, u32[]{:S(2)}) %collective-permute-start.11) | collective-permute-done | bytes 131104 | tf_op jit(solution)/shard_map/ppermute | solution.py:23
  50.5 7.0 %collective-permute-start.13 = (f16[512,512]{1,0:T(8,128)(2,1)S(1)}, f16[512,512]{1,0:T(8,128)(2,1)}, u32[]{:S(2)}, u32[]{:S(2)}) collective-permute-start(f16[512,512]{1,0:T(8,128)(2,1)S(1)} %convert_element_type.35), channel_id=1, source_target_pairs={{0,1},{1,0},{2,3},{3,2},{4,5},{5,4},{6,7},{7,6},{8,9},{9,8},{10,11... | collective-permute-start | bytes 1572872 | tf_op jit(solution)/shard_map/ppermute | solution.py:23
  58.1 1.1 %collective-permute-done.13 = f16[512,512]{1,0:T(8,128)(2,1)} collective-permute-done((f16[512,512]{1,0:T(8,128)(2,1)S(1)}, f16[512,512]{1,0:T(8,128)(2,1)}, u32[]{:S(2)}, u32[]{:S(2)}) %collective-permute-start.13) | collective-permute-done | bytes 524320 | tf_op jit(solution)/shard_map/ppermute | solution.py:23
  59.1 1.2 %convert_add_fusion = f32[512,512]{1,0:T(8,128)S(1)} fusion(f32[512,512]{1,0:T(8,128)S(1)} %project.2, f16[512,512]{1,0:T(8,128)(2,1)} %collective-permute-done.13), kind=kLoop, calls=%fused_computation.7 | loop fusion | flops 524288 | bytes 2621440 | tf_op jit(solution)/shard_map/add | solution.py:217
  60.5 2.7 %collective-permute-start.14 = (f16[256,256]{1,0:T(8,128)(2,1)S(1)}, f16[256,256]{1,0:T(8,128)(2,1)S(1)}, u32[]{:S(2)}, u32[]{:S(2)}) collective-permute-start(f16[256,256]{1,0:T(8,128)(2,1)S(1)} %get-tuple-element.39), channel_id=1, source_target_pairs={{0,2},{2,0},{1,3},{3,1},{4,6},{6,4},{5,7},{7,5},{8,10},{10,8},{9,1... | collective-permute-start | bytes 393224 | tf_op jit(solution)/shard_map/ppermute | solution.py:23
  64.1 2.7 %collective-permute-done.14 = f16[256,256]{1,0:T(8,128)(2,1)S(1)} collective-permute-done((f16[256,256]{1,0:T(8,128)(2,1)S(1)}, f16[256,256]{1,0:T(8,128)(2,1)S(1)}, u32[]{:S(2)}, u32[]{:S(2)}) %collective-permute-start.14) | collective-permute-done | bytes 131104 | tf_op jit(solution)/shard_map/ppermute | solution.py:23
  66.8 3.0 %collective-permute-done.16 = f16[256,256]{1,0:T(8,128)(2,1)S(1)} collective-permute-done((f16[256,256]{1,0:T(8,128)(2,1)S(1)}, f16[256,256]{1,0:T(8,128)(2,1)S(1)}, u32[]{:S(2)}, u32[]{:S(2)}) %collective-permute-start.16) | collective-permute-done | bytes 131104 | tf_op jit(solution)/shard_map/ppermute | solution.py:223
  69.9 1.1 %collective-permute-start.17 = (f32[256]{0:T(256)S(1)}, f32[256]{0:T(256)S(1)}, u32[]{:S(2)}, u32[]{:S(2)}) collective-permute-start(f32[256]{0:T(256)S(1)} %multiply_reduce_fusion), channel_id=1, source_target_pairs={{0,1},{1,0},{2,3},{3,2},{4,5},{5,4},{6,7},{7,6},{8,9},{9,8},{10,11... | collective-permute-start | bytes 3080 | tf_op jit(solution)/shard_map/ppermute | solution.py:23
  71.9 1.5 %collective-permute-start.18 = (f32[256]{0:T(256)S(1)}, f32[256]{0:T(256)S(1)}, u32[]{:S(2)}, u32[]{:S(2)}) collective-permute-start(f32[256]{0:T(256)S(1)} %add.82), channel_id=1, source_target_pairs={{0,2},{2,0},{1,3},{3,1},{4,6},{6,4},{5,7},{7,5},{8,10},{10,8},{9,1... | collective-permute-start | bytes 3080 | tf_op jit(solution)/shard_map/ppermute | solution.py:23
  73.3 2.5 %collective-permute-done.18 = f32[256]{0:T(256)S(1)} collective-permute-done((f32[256]{0:T(256)S(1)}, f32[256]{0:T(256)S(1)}, u32[]{:S(2)}, u32[]{:S(2)}) %collective-permute-start.18) | collective-permute-done | bytes 1056 | tf_op jit(solution)/shard_map/ppermute | solution.py:23
  (78 shorter events, 14.0 us)
Async XLA Ops:
  1.5 2.8 %copy-start.15 = (bf16[256,256]{1,0:T(8,128)(2,1)S(1)}, bf16[256,256]{1,0:T(8,128)(2,1)}, u32[]{:S(2)}) copy-start(bf16[256,256]{1,0:T(8,128)(2,1)} %param.7) | copy-start | bytes 393220
  2.2 5.1 %copy-start.12 = (s32[256,50]{0,1:T(8,128)S(1)}, s32[256,50]{0,1:T(8,128)}, u32[]{:S(2)}) copy-start(s32[256,50]{0,1:T(8,128)} %param.10) | copy-start | bytes 153604
  2.2 5.1 %copy-start.13 = (s32[256,50]{0,1:T(8,128)S(1)}, s32[256,50]{0,1:T(8,128)}, u32[]{:S(2)}) copy-start(s32[256,50]{0,1:T(8,128)} %param.9) | copy-start | bytes 153604
  2.2 13.8 %collective-permute-start = (s16[101,256]{1,0:T(8,128)(2,1)}, s16[101,256]{1,0:T(8,128)(2,1)}, u32[]{:S(2)}, u32[]{:S(2)}) collective-permute-start(s16[101,256]{1,0:T(8,128)(2,1)} %convert_element_type.31), channel_id=1, source_target_pairs={{0,16},{16,0},{1,17},{17,1},{2,18},{18,2},{3,19},{19,3},{4,20},{20... | collective-permute-start | bytes 155144 | tf_op jit(solution)/shard_map/ppermute | solution.py:23
  4.3 22.4 %collective-permute-start.1 = (bf16[128,256]{1,0:T(8,128)(2,1)S(1)}, bf16[128,256]{1,0:T(8,128)(2,1)S(1)}, u32[]{:S(2)}, u32[]{:S(2)}) collective-permute-start(bf16[128,256]{1,0:T(8,128)(2,1)S(1)} %get-tuple-element.41), channel_id=1, source_target_pairs={{0,4},{4,0},{8,12},{12,8},{1,5},{5,1},{9,13},{13,9},{2,6},{6,2},{1... | collective-permute-start | bytes 196616 | tf_op jit(solution)/shard_map/ppermute | solution.py:23
  5.6 23.1 %collective-permute-start.3 = (bf16[128,256]{1,0:T(8,128)(2,1)S(1)}, bf16[128,256]{1,0:T(8,128)(2,1)S(1)}, u32[]{:S(2)}, u32[]{:S(2)}) collective-permute-start(bf16[128,256]{1,0:T(8,128)(2,1)S(1)} %get-tuple-element.42), channel_id=1, source_target_pairs={{0,32},{32,0},{64,96},{96,64},{1,33},{33,1},{65,97},{97,65},{2,34}... | collective-permute-start | bytes 196616 | tf_op jit(solution)/shard_map/ppermute | solution.py:23
  11.0 1.0 %copy-start = (bf16[1024,512]{1,0:T(8,128)(2,1)}, bf16[1024,512]{1,0:T(8,128)(2,1)S(1)}, u32[]{:S(2)}) copy-start(bf16[1024,512]{1,0:T(8,128)(2,1)S(1)} %get-tuple-element.24.rest_3_) | copy-start | bytes 3145732
  13.0 1.0 %copy-start.4 = (bf16[1024,512]{1,0:T(8,128)(2,1)}, bf16[1024,512]{1,0:T(8,128)(2,1)S(1)}, u32[]{:S(2)}) copy-start(bf16[1024,512]{1,0:T(8,128)(2,1)S(1)} %get-tuple-element.26.rest_5_) | copy-start | bytes 3145732
  14.9 1.0 %copy-start.8 = (bf16[1024,512]{1,0:T(8,128)(2,1)}, bf16[1024,512]{1,0:T(8,128)(2,1)S(1)}, u32[]{:S(2)}) copy-start(bf16[1024,512]{1,0:T(8,128)(2,1)S(1)} %get-tuple-element.28.rest_7_) | copy-start | bytes 3145732
  16.8 1.2 %copy-start.1 = (bf16[1024,512]{1,0:T(8,128)(2,1)S(1)}, bf16[1024,512]{1,0:T(8,128)(2,1)}, u32[]{:S(2)}) copy-start(bf16[1024,512]{1,0:T(8,128)(2,1)} %copy-done) | copy-start | bytes 3145732
  18.1 1.2 %copy-start.3 = (bf16[1024,512]{1,0:T(8,128)(2,1)S(1)}, bf16[1024,512]{1,0:T(8,128)(2,1)}, u32[]{:S(2)}) copy-start(bf16[1024,512]{1,0:T(8,128)(2,1)} %copy-done.2) | copy-start | bytes 3145732
  19.3 1.2 %copy-start.5 = (bf16[1024,512]{1,0:T(8,128)(2,1)S(1)}, bf16[1024,512]{1,0:T(8,128)(2,1)}, u32[]{:S(2)}) copy-start(bf16[1024,512]{1,0:T(8,128)(2,1)} %copy-done.4) | copy-start | bytes 3145732
  20.5 1.2 %copy-start.7 = (bf16[1024,512]{1,0:T(8,128)(2,1)S(1)}, bf16[1024,512]{1,0:T(8,128)(2,1)}, u32[]{:S(2)}) copy-start(bf16[1024,512]{1,0:T(8,128)(2,1)} %copy-done.6) | copy-start | bytes 3145732
  21.7 1.2 %copy-start.9 = (bf16[1024,512]{1,0:T(8,128)(2,1)S(1)}, bf16[1024,512]{1,0:T(8,128)(2,1)}, u32[]{:S(2)}) copy-start(bf16[1024,512]{1,0:T(8,128)(2,1)} %copy-done.8) | copy-start | bytes 3145732
  26.8 5.1 %collective-permute-start.2 = (bf16[256,256]{1,0:T(8,128)(2,1)S(1)}, bf16[256,256]{1,0:T(8,128)(2,1)S(1)}, u32[]{:S(2)}, u32[]{:S(2)}) collective-permute-start(bf16[256,256]{1,0:T(8,128)(2,1)S(1)} %pad_maximum_fusion.2), channel_id=1, source_target_pairs={{0,12},{4,8},{8,4},{12,0},{1,13},{5,9},{9,5},{13,1},{2,14},{6,10},... | collective-permute-start | bytes 393224 | tf_op jit(solution)/shard_map/ppermute | solution.py:23
  28.7 6.9 %collective-permute-start.4 = (bf16[256,256]{1,0:T(8,128)(2,1)S(1)}, bf16[256,256]{1,0:T(8,128)(2,1)S(1)}, u32[]{:S(2)}, u32[]{:S(2)}) collective-permute-start(bf16[256,256]{1,0:T(8,128)(2,1)S(1)} %pad_maximum_fusion.3), channel_id=1, source_target_pairs={{0,96},{32,64},{64,32},{96,0},{1,97},{33,65},{65,33},{97,1},{2,98}... | collective-permute-start | bytes 393224 | tf_op jit(solution)/shard_map/ppermute | solution.py:23
  31.9 6.0 %collective-permute-start.5 = (bf16[512,256]{1,0:T(8,128)(2,1)S(1)}, bf16[512,256]{1,0:T(8,128)(2,1)S(1)}, u32[]{:S(2)}, u32[]{:S(2)}) collective-permute-start(bf16[512,256]{1,0:T(8,128)(2,1)S(1)} %pad_maximum_fusion), channel_id=1, source_target_pairs={{0,32},{32,0},{64,96},{96,64},{1,33},{33,1},{65,97},{97,65},{2,34}... | collective-permute-start | bytes 786440 | tf_op jit(solution)/shard_map/ppermute | solution.py:23
  32.0 7.5 %collective-permute-start.7 = (bf16[512,256]{1,0:T(8,128)(2,1)S(1)}, bf16[512,256]{1,0:T(8,128)(2,1)S(1)}, u32[]{:S(2)}, u32[]{:S(2)}) collective-permute-start(bf16[512,256]{1,0:T(8,128)(2,1)S(1)} %pad_maximum_fusion), channel_id=1, source_target_pairs={{0,96},{32,64},{64,32},{96,0},{1,97},{33,65},{65,33},{97,1},{2,98}... | collective-permute-start | bytes 786440 | tf_op jit(solution)/shard_map/ppermute | solution.py:23
  35.6 6.8 %collective-permute-start.8 = (bf16[512,256]{1,0:T(8,128)(2,1)S(1)}, bf16[512,256]{1,0:T(8,128)(2,1)S(1)}, u32[]{:S(2)}, u32[]{:S(2)}) collective-permute-start(bf16[512,256]{1,0:T(8,128)(2,1)S(1)} %pad_maximum_fusion.1), channel_id=1, source_target_pairs={{0,12},{4,8},{8,4},{12,0},{1,13},{5,9},{9,5},{13,1},{2,14},{6,10},... | collective-permute-start | bytes 786440 | tf_op jit(solution)/shard_map/ppermute | solution.py:23
  37.5 5.5 %collective-permute-start.6 = (bf16[512,256]{1,0:T(8,128)(2,1)S(1)}, bf16[512,256]{1,0:T(8,128)(2,1)S(1)}, u32[]{:S(2)}, u32[]{:S(2)}) collective-permute-start(bf16[512,256]{1,0:T(8,128)(2,1)S(1)} %pad_maximum_fusion.1), channel_id=1, source_target_pairs={{0,4},{4,0},{8,12},{12,8},{1,5},{5,1},{9,13},{13,9},{2,6},{6,2},{1... | collective-permute-start | bytes 786440 | tf_op jit(solution)/shard_map/ppermute | solution.py:23
  38.0 8.2 %collective-permute-start.10 = (bf16[256,256]{1,0:T(8,128)(2,1)S(1)}, bf16[256,256]{1,0:T(8,128)(2,1)S(1)}, u32[]{:S(2)}, u32[]{:S(2)}) collective-permute-start(bf16[256,256]{1,0:T(8,128)(2,1)S(1)} %slice.66), channel_id=1, source_target_pairs={{0,96},{32,64},{64,32},{96,0},{1,97},{33,65},{65,33},{97,1},{2,98}... | collective-permute-start | bytes 393224 | tf_op jit(solution)/shard_map/ppermute | solution.py:23
  39.6 6.6 %collective-permute-start.9 = (bf16[256,256]{1,0:T(8,128)(2,1)S(1)}, bf16[256,256]{1,0:T(8,128)(2,1)S(1)}, u32[]{:S(2)}, u32[]{:S(2)}) collective-permute-start(bf16[256,256]{1,0:T(8,128)(2,1)S(1)} %slice.65), channel_id=1, source_target_pairs={{0,32},{32,0},{64,96},{96,64},{1,33},{33,1},{65,97},{97,65},{2,34}... | collective-permute-start | bytes 393224 | tf_op jit(solution)/shard_map/ppermute | solution.py:23
  42.4 5.6 %collective-permute-start.11 = (bf16[256,256]{1,0:T(8,128)(2,1)S(1)}, bf16[256,256]{1,0:T(8,128)(2,1)S(1)}, u32[]{:S(2)}, u32[]{:S(2)}) collective-permute-start(bf16[256,256]{1,0:T(8,128)(2,1)S(1)} %slice.67), channel_id=1, source_target_pairs={{0,4},{4,0},{8,12},{12,8},{1,5},{5,1},{9,13},{13,9},{2,6},{6,2},{1... | collective-permute-start | bytes 393224 | tf_op jit(solution)/shard_map/ppermute | solution.py:23
  43.0 5.1 %collective-permute-start.12 = (bf16[256,256]{1,0:T(8,128)(2,1)S(1)}, bf16[256,256]{1,0:T(8,128)(2,1)S(1)}, u32[]{:S(2)}, u32[]{:S(2)}) collective-permute-start(bf16[256,256]{1,0:T(8,128)(2,1)S(1)} %slice.68), channel_id=1, source_target_pairs={{0,12},{4,8},{8,4},{12,0},{1,13},{5,9},{9,5},{13,1},{2,14},{6,10},... | collective-permute-start | bytes 393224 | tf_op jit(solution)/shard_map/ppermute | solution.py:23
  48.6 1.0 %copy-start.10 = (bf16[256,1024]{1,0:T(8,128)(2,1)S(1)}, bf16[256,1024]{1,0:T(8,128)(2,1)}, u32[]{:S(2)}) copy-start(bf16[256,1024]{1,0:T(8,128)(2,1)} %self_ref.3) | copy-start | bytes 1572868
  48.6 1.2 %copy-start.11 = (bf16[256,1024]{1,0:T(8,128)(2,1)S(1)}, bf16[256,1024]{1,0:T(8,128)(2,1)}, u32[]{:S(2)}) copy-start(bf16[256,1024]{1,0:T(8,128)(2,1)} %nbr_ref.3) | copy-start | bytes 1572868
  50.5 8.7 %collective-permute-start.13 = (f16[512,512]{1,0:T(8,128)(2,1)S(1)}, f16[512,512]{1,0:T(8,128)(2,1)}, u32[]{:S(2)}, u32[]{:S(2)}) collective-permute-start(f16[512,512]{1,0:T(8,128)(2,1)S(1)} %convert_element_type.35), channel_id=1, source_target_pairs={{0,1},{1,0},{2,3},{3,2},{4,5},{5,4},{6,7},{7,6},{8,9},{9,8},{10,11... | collective-permute-start | bytes 1572872 | tf_op jit(solution)/shard_map/ppermute | solution.py:23
  60.5 6.3 %collective-permute-start.14 = (f16[256,256]{1,0:T(8,128)(2,1)S(1)}, f16[256,256]{1,0:T(8,128)(2,1)S(1)}, u32[]{:S(2)}, u32[]{:S(2)}) collective-permute-start(f16[256,256]{1,0:T(8,128)(2,1)S(1)} %get-tuple-element.39), channel_id=1, source_target_pairs={{0,2},{2,0},{1,3},{3,1},{4,6},{6,4},{5,7},{7,5},{8,10},{10,8},{9,1... | collective-permute-start | bytes 393224 | tf_op jit(solution)/shard_map/ppermute | solution.py:23
  63.2 6.6 %collective-permute-start.16 = (f16[256,256]{1,0:T(8,128)(2,1)S(1)}, f16[256,256]{1,0:T(8,128)(2,1)S(1)}, u32[]{:S(2)}, u32[]{:S(2)}) collective-permute-start(f16[256,256]{1,0:T(8,128)(2,1)S(1)} %get-tuple-element.40), channel_id=1, source_target_pairs={{0,18},{2,16},{16,2},{18,0},{1,19},{3,17},{17,3},{19,1},{4,22},{6,... | collective-permute-start | bytes 393224 | tf_op jit(solution)/shard_map/ppermute | solution.py:223
  63.2 6.5 %collective-permute-start.15 = (f16[256,256]{1,0:T(8,128)(2,1)S(1)}, f16[256,256]{1,0:T(8,128)(2,1)S(1)}, u32[]{:S(2)}, u32[]{:S(2)}) collective-permute-start(f16[256,256]{1,0:T(8,128)(2,1)S(1)} %slice_convert_fusion), channel_id=1, source_target_pairs={{0,16},{16,0},{1,17},{17,1},{2,18},{18,2},{3,19},{19,3},{4,20},{20... | collective-permute-start | bytes 393224 | tf_op jit(solution)/shard_map/ppermute | solution.py:23
  69.9 1.9 %collective-permute-start.17 = (f32[256]{0:T(256)S(1)}, f32[256]{0:T(256)S(1)}, u32[]{:S(2)}, u32[]{:S(2)}) collective-permute-start(f32[256]{0:T(256)S(1)} %multiply_reduce_fusion), channel_id=1, source_target_pairs={{0,1},{1,0},{2,3},{3,2},{4,5},{5,4},{6,7},{7,6},{8,9},{9,8},{10,11... | collective-permute-start | bytes 3080 | tf_op jit(solution)/shard_map/ppermute | solution.py:23
  71.9 3.9 %collective-permute-start.18 = (f32[256]{0:T(256)S(1)}, f32[256]{0:T(256)S(1)}, u32[]{:S(2)}, u32[]{:S(2)}) collective-permute-start(f32[256]{0:T(256)S(1)} %add.82), channel_id=1, source_target_pairs={{0,2},{2,0},{1,3},{3,1},{4,6},{6,4},{5,7},{7,5},{8,10},{10,8},{9,1... | collective-permute-start | bytes 3080 | tf_op jit(solution)/shard_map/ppermute | solution.py:23
  (3 other events, 2.6 us)

commit v5 on v3

--- a/solution.py
+++ b/solution.py
@@ -28,7 +28,7 @@
     out_refs, (turned, code_ref, low_ref, times_ref, own_tile_ref, own_low_ref) = rest[:-6], rest[-6:]
     nbr, nodes = ids_ref.shape
     counts_row, own_row = group * nodes, (2 + group) * nodes
-    here = here_ref[0]
+    here = here_ref[0] >> 1
     places = [(o, c) for o in range(len(out_refs)) for c in range(0, out_refs[o].shape[1], LANES)]
 
     def column(row):
@@ -139,15 +139,16 @@
     )
 
 
-def project_kernel(which_ref, sums_ref, total_ref, self_ref, nbr_ref, out_ref):
+def project_kernel(flip, here_ref, sums_ref, total_ref, self_ref, nbr_ref, out_ref):
     nodes, share = sums_ref.shape[0] // 2, sums_ref.shape[1]
     total = jnp.concatenate([total_ref[...]] * (share // LANES), axis=1)
     own = sums_ref[nodes:, :].astype(jnp.bfloat16)
     pooled = sums_ref[:nodes, :] / total
     high = pooled.astype(jnp.bfloat16)
     low = (pooled - high.astype(jnp.float32)).astype(jnp.bfloat16)
+    which = (here_ref[0] & 1) ^ flip
     for part in range(2):
-        first = pl.multiple_of(part * 2 * share + which_ref[0] * share, share)
+        first = pl.multiple_of(part * 2 * share + which * share, share)
         columns = pl.ds(first, share)
         w_self, w_nbr = self_ref[:, columns], nbr_ref[:, columns]
         out = jnp.dot(own, w_self, preferred_element_type=jnp.float32)
@@ -156,11 +157,11 @@
         out_ref[:, part * share : (part + 1) * share] = out * SCALE
 
 
-def projected(which, sums, total, w_self, w_neighbor):
+def projected(flip, here, sums, total, w_self, w_neighbor):
     nodes, share = sums.shape[0] // 2, sums.shape[1]
     vmem = pl.BlockSpec(memory_space=pltpu.VMEM)
     return pl.pallas_call(
-        project_kernel,
+        functools.partial(project_kernel, flip),
         out_shape=jax.ShapeDtypeStruct((nodes, 2 * share), jnp.float32),
         in_specs=[pl.BlockSpec(memory_space=pltpu.SMEM)] + [vmem] * 4,
         out_specs=vmem,
@@ -169,7 +170,7 @@
             flops=400_000_000, bytes_accessed=4_000_000, transcendentals=0
         ),
         name="project",
-    )(which.reshape(1), sums, total, w_self, w_neighbor)
+    )(here, sums, total, w_self, w_neighbor)
 
 
 def shards(items, self_ids, neighbor_ids, visit_counts, w_self, w_neighbor, bias):
@@ -177,10 +178,7 @@
     batch, share = self_ids.shape[0], items.shape[1]
     nbr = neighbor_ids.shape[1]
     half = items.shape[0] // 2
-    here = lax.axis_index(DOM).reshape(1)
-
-    table = jnp.concatenate([neighbor_ids.T, visit_counts.T, self_ids[None, :]], axis=0)
-    theirs = moved(table.astype(jnp.int16), "yl", lambda i: i ^ 1).astype(jnp.int32)
+    here = lax.axis_index((*DOM, "core")).reshape(1)
 
     axes = [("x", "z"), ("z", "x")]
     halves = [items[:half], items[half:]]
@@ -191,9 +189,17 @@
         lines.append(jnp.concatenate([pair, rest], axis=0))
     pieces = []
     for line, (_, far) in zip(lines, axes):
-        low, high = moved(line, far, lambda i: i ^ 1), moved(line, far, lambda i: i ^ 3)
+        low = moved(line, far, lambda i: i ^ 1)
+        high = moved(line, far, lambda i: i ^ 3)
         pieces += [line, low, high, moved(high, far, lambda i: i ^ 1)]
 
+    table = (neighbor_ids.T, visit_counts.T, self_ids)
+    kept_back, _ = lax.optimization_barrier((table, lines))
+    sent = lax.optimization_barrier(
+        jnp.concatenate([kept_back[0], kept_back[1], kept_back[2][None, :]], axis=0)
+    )
+    theirs = moved(sent.astype(jnp.int16), "yl", lambda i: i ^ 1).astype(jnp.int32)
+    table = jnp.concatenate([table[0], table[1], table[2][None, :]], axis=0)
     widths = [p.shape[0] for p in pieces]
     blocks = count_blocks(0, [], here, table, nbr, widths)
     blocks = count_blocks(1, blocks, here, theirs, nbr, widths)
@@ -205,9 +211,9 @@
         [jnp.sum(t[nbr : 2 * nbr].astype(jnp.float32), axis=0) for t in (table, theirs)]
     )
     total = jnp.broadcast_to(total[:, None], (2 * batch, LANES))
-    given = projected(1 - core, sums, total, w_self, w_neighbor)
+    given = projected(1, here, sums, total, w_self, w_neighbor)
     got = moved(given.astype(jnp.float16), "core", lambda i: i ^ 1)
-    kept = projected(core, sums, total, w_self, w_neighbor)
+    kept = projected(0, here, sums, total, w_self, w_neighbor)
     chip = kept + got.astype(jnp.float32)
     first, second = chip[:, :share], chip[:, share:]
     here_part = jnp.where(yh == 0, first, second)

time: 75.9 us -> 56.7 us (0.75)
  local copies, waits for them, and re-layouts: 14.1 us -> 3.14 us
  waiting for transfers between devices: 17.7 us -> 13.3 us
  other arithmetic: 5.54 us -> 1.51 us
    unnamed x36 -> x10, local copies, waits for them, and re-layouts: 13.1 us -> 1.32 us
    ppermute x16, waiting for transfers between devices: 14.7 us -> 10.3 us  [moved(): return lax.ppermute(value, axis, [(i, target(i) % n) for i in range(n)])]
    another operation x3 -> x1, other arithmetic: 1.59 us -> 0.02 us
    add x1, other arithmetic: 1.2 us -> 0.16 us  [shards(): chip = kept + got.astype(jnp.float32)]
    slice x1, local copies, waits for them, and re-layouts: 0.01 us -> 0.88 us  [shards(): halves = [items[:half], items[half:]]]
    convert_element_type x1 -> x2, other arithmetic: 0.82 us -> 0.02 us  [the longest x1 0.01 us: shards(): moved(sent.astype(jnp.int16), 'yl', lambda i: i ^ 1).astype(jnp.int32)]
  transfers between devices with their start and end apart: 17 -> 17, of which waited for: 9 -> 8; matrix products, arithmetic and copies ran while one was open for 6% -> 7% of each run, Pallas kernels for 11% -> 14%
where the time goes in v5:
time: 56.7 us; the launch traced here: 56.3 us
  starting transfers between devices  25.9 us (46%)
  waiting for transfers between devices  13.3 us (23%)
  Pallas kernels  8.68 us (15%)
  matrix products  3.55 us (6%)
  local copies, waits for them, and re-layouts  3.14 us (6%)
  other arithmetic  1.51 us (3%)
    ppermute x16, starting transfers between devices, moved(): return lax.ppermute(value, axis, [(i, target(i) % n) for i in range(n)])  25.9 us
    ppermute x16, waiting for transfers between devices, moved(): return lax.ppermute(value, axis, [(i, target(i) % n) for i in range(n)])  10.3 us
    pallas_call x2, Pallas kernels, count_blocks(): pl.pallas_call(functools.partial(count_kernel, group, len(given)), out_sh...  7.5 us
    dot_general x8, matrix products, shards(): jnp.dot(blocks[i], pieces[i], preferred_element_type=jnp.float32)  3.55 us
    ppermute x1, waiting for transfers between devices, shards(): lax.ppermute(there_part[batch:], ('yl', 'yh'), [(i, i ^ 3) for i in range...  3.02 us
    unnamed x10, local copies, waits for them, and re-layouts  1.32 us
    pallas_call x2, Pallas kernels, projected(): pl.pallas_call(functools.partial(project_kernel, flip), out_shape=jax.Sha...  1.18 us
  transfers between devices with their start and end apart: 17, of which 8 were waited for; matrix products, arithmetic and copies ran while one was open for 7% of the time, Pallas kernels for 14%

profile of v5, /device:TPU:1, one launch (start us, length us, event | category | flops | bytes accessed | tf_op | source)
XLA Modules:
  0.0 56.3 jit_solution(1657649823485011011)
XLA Ops:
  0.0 0.9 %fusion.12 = (bf16[128,256]{1,0:T(8,128)(2,1)S(1)}, bf16[128,256]{1,0:T(8,128)(2,1)S(1)}) fusion(bf16[256,256]{1,0:T(8,128)(2,1)} %param.7), kind=kLoop, calls=%fused_computation.30 | loop fusion | bytes 262144 | tf_op jit(solution)/shard_map/slice | solution.py:184
  0.9 2.5 %collective-permute-start.2 = (bf16[128,256]{1,0:T(8,128)(2,1)S(1)}, bf16[128,256]{1,0:T(8,128)(2,1)S(1)}, u32[]{:S(2)}, u32[]{:S(2)}) collective-permute-start(bf16[128,256]{1,0:T(8,128)(2,1)S(1)} %get-tuple-element.47), channel_id=1, source_target_pairs={{0,32},{32,0},{64,96},{96,64},{1,33},{33,1},{65,97},{97,65},{2,34}... | collective-permute-start | bytes 196616 | tf_op jit(solution)/shard_map/ppermute | solution.py:23
  3.4 1.2 %collective-permute-start = (bf16[128,256]{1,0:T(8,128)(2,1)S(1)}, bf16[128,256]{1,0:T(8,128)(2,1)S(1)}, u32[]{:S(2)}, u32[]{:S(2)}) collective-permute-start(bf16[128,256]{1,0:T(8,128)(2,1)S(1)} %get-tuple-element.48), channel_id=1, source_target_pairs={{0,4},{4,0},{8,12},{12,8},{1,5},{5,1},{9,13},{13,9},{2,6},{6,2},{1... | collective-permute-start | bytes 196616 | tf_op jit(solution)/shard_map/ppermute | solution.py:23
  4.6 0.4 collective-permute-done.2
  5.1 3.7 %collective-permute-start.3 = (bf16[256,256]{1,0:T(8,128)(2,1)S(1)}, bf16[256,256]{1,0:T(8,128)(2,1)S(1)}, u32[]{:S(2)}, u32[]{:S(2)}) collective-permute-start(bf16[256,256]{1,0:T(8,128)(2,1)S(1)} %pad_maximum_fusion.3), channel_id=1, source_target_pairs={{0,96},{32,64},{64,32},{96,0},{1,97},{33,65},{65,33},{97,1},{2,98}... | collective-permute-start | bytes 393224 | tf_op jit(solution)/shard_map/ppermute | solution.py:23
  8.8 2.6 %collective-permute-start.1 = (bf16[256,256]{1,0:T(8,128)(2,1)S(1)}, bf16[256,256]{1,0:T(8,128)(2,1)S(1)}, u32[]{:S(2)}, u32[]{:S(2)}) collective-permute-start(bf16[256,256]{1,0:T(8,128)(2,1)S(1)} %pad_maximum_fusion.2), channel_id=1, source_target_pairs={{0,12},{4,8},{8,4},{12,0},{1,13},{5,9},{9,5},{13,1},{2,14},{6,10},... | collective-permute-start | bytes 393224 | tf_op jit(solution)/shard_map/ppermute | solution.py:23
  11.4 0.7 %copy-done.4 = s32[256]{0:T(256)S(1)} copy-done((s32[256]{0:T(256)S(1)}, s32[256]{0:T(256)}, u32[]{:S(2)}) %copy-start.4) | copy-done | bytes 1048
  12.0 3.7 %counts.2 = (bf16[1024,512]{1,0:T(8,128)(2,1)S(1)}, bf16[1024,512]{1,0:T(8,128)(2,1)S(1)}, bf16[1024,512]{1,0:T(8,128)(2,1)S(1)}, bf16[1024,512]{1,0:T(8,128)(2,...) custom-call(s32[1]{0:T(128)} %bitcast.here_ref, ...), custom_call_target="tpu_custom_call" | custom-call | flops 2000000000 | bytes 4500000 | tf_op jit(solution)/shard_map/counts/pallas_call | solution.py:119
  15.9 1.4 %collective-permute-start.4 = (s16[101,256]{1,0:T(8,128)(2,1)S(1)}, s16[101,256]{1,0:T(8,128)(2,1)S(1)}, u32[]{:S(2)}, u32[]{:S(2)}) collective-permute-start(s16[101,256]{1,0:T(8,128)(2,1)S(1)} %convert_element_type.31), channel_id=1, source_target_pairs={{0,16},{16,0},{1,17},{17,1},{2,18},{18,2},{3,19},{19,3},{4,20},{20... | collective-permute-start | bytes 155144 | tf_op jit(solution)/shard_map/ppermute | solution.py:23
  17.4 0.8 %collective-permute-start.8 = (bf16[512,256]{1,0:T(8,128)(2,1)S(1)}, bf16[512,256]{1,0:T(8,128)(2,1)S(1)}, u32[]{:S(2)}, u32[]{:S(2)}) collective-permute-start(bf16[512,256]{1,0:T(8,128)(2,1)S(1)} %pad_maximum_fusion.1), channel_id=1, source_target_pairs={{0,12},{4,8},{8,4},{12,0},{1,13},{5,9},{9,5},{13,1},{2,14},{6,10},... | collective-permute-start | bytes 786440 | tf_op jit(solution)/shard_map/ppermute | solution.py:23
  18.2 1.4 %collective-permute-start.7 = (bf16[512,256]{1,0:T(8,128)(2,1)S(1)}, bf16[512,256]{1,0:T(8,128)(2,1)S(1)}, u32[]{:S(2)}, u32[]{:S(2)}) collective-permute-start(bf16[512,256]{1,0:T(8,128)(2,1)S(1)} %pad_maximum_fusion), channel_id=1, source_target_pairs={{0,96},{32,64},{64,32},{96,0},{1,97},{33,65},{65,33},{97,1},{2,98}... | collective-permute-start | bytes 786440 | tf_op jit(solution)/shard_map/ppermute | solution.py:23
  19.7 3.8 %counts.3 = (bf16[1024,512]{1,0:T(8,128)(2,1)S(1)}, bf16[1024,512]{1,0:T(8,128)(2,1)S(1)}, bf16[1024,512]{1,0:T(8,128)(2,1)S(1)}, bf16[1024,512]{1,0:T(8,128)(2,...) custom-call(s32[1]{0:T(128)} %bitcast.here_ref, ...), custom_call_target="tpu_custom_call", output_to_operand_aliasing={{0}: (4, {}), {1}: (5, {}), {2}: (6, {}), {3}: (7, {}), {4}... | custom-call | flops 2000000000 | bytes 4500000 | tf_op jit(solution)/shard_map/counts/pallas_call | solution.py:119
  23.5 0.4 fusion.10
  23.9 0.7 %collective-permute-start.10 = (bf16[512,256]{1,0:T(8,128)(2,1)S(1)}, bf16[512,256]{1,0:T(8,128)(2,1)S(1)}, u32[]{:S(2)}, u32[]{:S(2)}) collective-permute-start(bf16[512,256]{1,0:T(8,128)(2,1)S(1)} %collective-permute-done.8), channel_id=1, source_target_pairs={{0,4},{4,0},{8,12},{12,8},{1,5},{5,1},{9,13},{13,9},{2,6},{6,2},{1... | collective-permute-start | bytes 786440 | tf_op jit(solution)/shard_map/ppermute | solution.py:23
  25.2 0.4 fusion.16
  26.6 0.5 fusion.4
  27.1 2.1 %collective-permute-done.10 = bf16[512,256]{1,0:T(8,128)(2,1)S(1)} collective-permute-done((bf16[512,256]{1,0:T(8,128)(2,1)S(1)}, bf16[512,256]{1,0:T(8,128)(2,1)S(1)}, u32[]{:S(2)}, u32[]{:S(2)}) %collective-permute-start.10) | collective-permute-done | bytes 262176 | tf_op jit(solution)/shard_map/ppermute | solution.py:23
  29.7 0.8 %collective-permute-done.9 = bf16[512,256]{1,0:T(8,128)(2,1)S(1)} collective-permute-done((bf16[512,256]{1,0:T(8,128)(2,1)S(1)}, bf16[512,256]{1,0:T(8,128)(2,1)S(1)}, u32[]{:S(2)}, u32[]{:S(2)}) %collective-permute-start.9) | collective-permute-done | bytes 262176 | tf_op jit(solution)/shard_map/ppermute | solution.py:23
  31.0 0.5 copy-done
  31.6 0.6 %project.3 = f32[512,512]{1,0:T(8,128)S(1)} custom-call(s32[1]{0:T(128)} %bitcast.here_ref, f32[1024,256]{1,0:T(8,128)S(1)} %fusion.sums_ref, f32[512,128]{1,0:T(8,128)S(1)} %broadcast_in_dim.5.total_ref, bf16[256,1024]{1,0:T(8,128)(2,1)S(1)} %copy-done, bf16[256,1024]{1,0:T(8,128)(2,1)S(1)} %copy-done.1), custom_call_target="tpu_custom_call" | custom-call | flops 400000000 | bytes 4000000 | tf_op jit(solution)/shard_map/project/pallas_call | solution.py:163
  32.3 6.0 %collective-permute-start.11 = (f16[512,512]{1,0:T(8,128)(2,1)S(1)}, f16[512,512]{1,0:T(8,128)(2,1)S(1)}, u32[]{:S(2)}, u32[]{:S(2)}) collective-permute-start(f16[512,512]{1,0:T(8,128)(2,1)S(1)} %convert_element_type.35), channel_id=1, source_target_pairs={{0,1},{1,0},{2,3},{3,2},{4,5},{5,4},{6,7},{7,6},{8,9},{9,8},{10,11... | collective-permute-start | bytes 1572872 | tf_op jit(solution)/shard_map/ppermute | solution.py:23
  38.3 0.6 %project.2 = f32[512,512]{1,0:T(8,128)S(1)} custom-call(s32[1]{0:T(128)} %bitcast.here_ref, f32[1024,256]{1,0:T(8,128)S(1)} %fusion.sums_ref, f32[512,128]{1,0:T(8,128)S(1)} %broadcast_in_dim.5.total_ref, bf16[256,1024]{1,0:T(8,128)(2,1)S(1)} %copy-done, bf16[256,1024]{1,0:T(8,128)(2,1)S(1)} %copy-done.1), custom_call_target="tpu_custom_call" | custom-call | flops 400000000 | bytes 4000000 | tf_op jit(solution)/shard_map/project/pallas_call | solution.py:163
  38.9 0.9 %collective-permute-done.11 = f16[512,512]{1,0:T(8,128)(2,1)S(1)} collective-permute-done((f16[512,512]{1,0:T(8,128)(2,1)S(1)}, f16[512,512]{1,0:T(8,128)(2,1)S(1)}, u32[]{:S(2)}, u32[]{:S(2)}) %collective-permute-start.11) | collective-permute-done | bytes 524320 | tf_op jit(solution)/shard_map/ppermute | solution.py:23
  40.2 2.7 %collective-permute-start.12 = (f16[256,256]{1,0:T(8,128)(2,1)S(1)}, f16[256,256]{1,0:T(8,128)(2,1)S(1)}, u32[]{:S(2)}, u32[]{:S(2)}) collective-permute-start(f16[256,256]{1,0:T(8,128)(2,1)S(1)} %get-tuple-element.45), channel_id=1, source_target_pairs={{0,2},{2,0},{1,3},{3,1},{4,6},{6,4},{5,7},{7,5},{8,10},{10,8},{9,1... | collective-permute-start | bytes 393224 | tf_op jit(solution)/shard_map/ppermute | solution.py:23
  43.0 0.8 %dynamic_slice.3 = f32[256]{0:T(256)S(1)} dynamic-slice(f32[1024]{0:T(1024)} %param.13, s32[]{:T(128)S(6)} %select_n.18), dynamic_slice_sizes={256} | dynamic-slice | bytes 2052 | tf_op jit(solution)/shard_map/dynamic_slice | solution.py:226
  43.8 2.7 %collective-permute-done.12 = f16[256,256]{1,0:T(8,128)(2,1)S(1)} collective-permute-done((f16[256,256]{1,0:T(8,128)(2,1)S(1)}, f16[256,256]{1,0:T(8,128)(2,1)S(1)}, u32[]{:S(2)}, u32[]{:S(2)}) %collective-permute-start.12) | collective-permute-done | bytes 131104 | tf_op jit(solution)/shard_map/ppermute | solution.py:23
  46.5 3.0 %collective-permute-done.14 = f16[256,256]{1,0:T(8,128)(2,1)S(1)} collective-permute-done((f16[256,256]{1,0:T(8,128)(2,1)S(1)}, f16[256,256]{1,0:T(8,128)(2,1)S(1)}, u32[]{:S(2)}, u32[]{:S(2)}) %collective-permute-start.14) | collective-permute-done | bytes 131104 | tf_op jit(solution)/shard_map/ppermute | solution.py:223
  49.7 1.1 %collective-permute-start.15 = (f32[256]{0:T(256)S(1)}, f32[256]{0:T(256)S(1)}, u32[]{:S(2)}, u32[]{:S(2)}) collective-permute-start(f32[256]{0:T(256)S(1)} %multiply_reduce_fusion), channel_id=1, source_target_pairs={{0,1},{1,0},{2,3},{3,2},{4,5},{5,4},{6,7},{7,6},{8,9},{9,8},{10,11... | collective-permute-start | bytes 3080 | tf_op jit(solution)/shard_map/ppermute | solution.py:23
  50.8 0.8 %collective-permute-done.15 = f32[256]{0:T(256)S(1)} collective-permute-done((f32[256]{0:T(256)S(1)}, f32[256]{0:T(256)S(1)}, u32[]{:S(2)}, u32[]{:S(2)}) %collective-permute-start.15) | collective-permute-done | bytes 1056 | tf_op jit(solution)/shard_map/ppermute | solution.py:23
  51.6 1.5 %collective-permute-start.16 = (f32[256]{0:T(256)S(1)}, f32[256]{0:T(256)S(1)}, u32[]{:S(2)}, u32[]{:S(2)}) collective-permute-start(f32[256]{0:T(256)S(1)} %add.86), channel_id=1, source_target_pairs={{0,2},{2,0},{1,3},{3,1},{4,6},{6,4},{5,7},{7,5},{8,10},{10,8},{9,1... | collective-permute-start | bytes 3080 | tf_op jit(solution)/shard_map/ppermute | solution.py:23
  53.0 2.5 %collective-permute-done.16 = f32[256]{0:T(256)S(1)} collective-permute-done((f32[256]{0:T(256)S(1)}, f32[256]{0:T(256)S(1)}, u32[]{:S(2)}, u32[]{:S(2)}) %collective-permute-start.16) | collective-permute-done | bytes 1056 | tf_op jit(solution)/shard_map/ppermute | solution.py:23
  55.5 0.8 %broadcast_divide_fusion = f32[256,256]{1,0:T(8,128)} fusion(f32[256]{0:T(256)S(1)} %add_sqrt_fusion, f32[256]{0:T(256)S(1)} %dynamic_slice.3, f16[256,256]{1,0:T(8,128)(2,1)S(1)} %collective-permute-done.14, f16[256,256]{1,0:T(8,128)(2,1)S(1)} %collective-permute-done.13, f16[256,256]{1,0:T(8,128)(2,1)S(1)} %collective-permute-done.12, ...), kind=kLoop, calls=%fused_computation.22 | loop fusion | flops 655360 | bytes 919552 | tf_op jit(solution)/shard_map/div | solution.py:232
  (48 shorter events, 3.5 us)
Async XLA Ops:
  0.9 4.2 %collective-permute-start.2 = (bf16[128,256]{1,0:T(8,128)(2,1)S(1)}, bf16[128,256]{1,0:T(8,128)(2,1)S(1)}, u32[]{:S(2)}, u32[]{:S(2)}) collective-permute-start(bf16[128,256]{1,0:T(8,128)(2,1)S(1)} %get-tuple-element.47), channel_id=1, source_target_pairs={{0,32},{32,0},{64,96},{96,64},{1,33},{33,1},{65,97},{97,65},{2,34}... | collective-permute-start | bytes 196616 | tf_op jit(solution)/shard_map/ppermute | solution.py:23
  3.4 5.4 %collective-permute-start = (bf16[128,256]{1,0:T(8,128)(2,1)S(1)}, bf16[128,256]{1,0:T(8,128)(2,1)S(1)}, u32[]{:S(2)}, u32[]{:S(2)}) collective-permute-start(bf16[128,256]{1,0:T(8,128)(2,1)S(1)} %get-tuple-element.48), channel_id=1, source_target_pairs={{0,4},{4,0},{8,12},{12,8},{1,5},{5,1},{9,13},{13,9},{2,6},{6,2},{1... | collective-permute-start | bytes 196616 | tf_op jit(solution)/shard_map/ppermute | solution.py:23
  5.1 6.3 %copy-start.2 = (s32[256,50]{0,1:T(8,128)S(1)}, s32[256,50]{0,1:T(8,128)}, u32[]{:S(2)}) copy-start(s32[256,50]{0,1:T(8,128)} %param.10) | copy-start | bytes 153604
  5.1 6.3 %copy-start.3 = (s32[256,50]{0,1:T(8,128)S(1)}, s32[256,50]{0,1:T(8,128)}, u32[]{:S(2)}) copy-start(s32[256,50]{0,1:T(8,128)} %param.9) | copy-start | bytes 153604
  5.1 10.7 %collective-permute-start.3 = (bf16[256,256]{1,0:T(8,128)(2,1)S(1)}, bf16[256,256]{1,0:T(8,128)(2,1)S(1)}, u32[]{:S(2)}, u32[]{:S(2)}) collective-permute-start(bf16[256,256]{1,0:T(8,128)(2,1)S(1)} %pad_maximum_fusion.3), channel_id=1, source_target_pairs={{0,96},{32,64},{64,32},{96,0},{1,97},{33,65},{65,33},{97,1},{2,98}... | collective-permute-start | bytes 393224 | tf_op jit(solution)/shard_map/ppermute | solution.py:23
  8.8 7.0 %collective-permute-start.1 = (bf16[256,256]{1,0:T(8,128)(2,1)S(1)}, bf16[256,256]{1,0:T(8,128)(2,1)S(1)}, u32[]{:S(2)}, u32[]{:S(2)}) collective-permute-start(bf16[256,256]{1,0:T(8,128)(2,1)S(1)} %pad_maximum_fusion.2), channel_id=1, source_target_pairs={{0,12},{4,8},{8,4},{12,0},{1,13},{5,9},{9,5},{13,1},{2,14},{6,10},... | collective-permute-start | bytes 393224 | tf_op jit(solution)/shard_map/ppermute | solution.py:23
  11.3 0.7 %copy-start.4 = (s32[256]{0:T(256)S(1)}, s32[256]{0:T(256)}, u32[]{:S(2)}) copy-start(s32[256]{0:T(256)} %param.8) | copy-start | bytes 3076
  15.9 3.7 %collective-permute-start.4 = (s16[101,256]{1,0:T(8,128)(2,1)S(1)}, s16[101,256]{1,0:T(8,128)(2,1)S(1)}, u32[]{:S(2)}, u32[]{:S(2)}) collective-permute-start(s16[101,256]{1,0:T(8,128)(2,1)S(1)} %convert_element_type.31), channel_id=1, source_target_pairs={{0,16},{16,0},{1,17},{17,1},{2,18},{18,2},{3,19},{19,3},{4,20},{20... | collective-permute-start | bytes 155144 | tf_op jit(solution)/shard_map/ppermute | solution.py:23
  17.3 8.4 %collective-permute-start.6 = (bf16[512,256]{1,0:T(8,128)(2,1)S(1)}, bf16[512,256]{1,0:T(8,128)(2,1)S(1)}, u32[]{:S(2)}, u32[]{:S(2)}) collective-permute-start(bf16[512,256]{1,0:T(8,128)(2,1)S(1)} %pad_maximum_fusion.1), channel_id=1, source_target_pairs={{0,4},{4,0},{8,12},{12,8},{1,5},{5,1},{9,13},{13,9},{2,6},{6,2},{1... | collective-permute-start | bytes 786440 | tf_op jit(solution)/shard_map/ppermute | solution.py:23
  17.4 6.5 %collective-permute-start.8 = (bf16[512,256]{1,0:T(8,128)(2,1)S(1)}, bf16[512,256]{1,0:T(8,128)(2,1)S(1)}, u32[]{:S(2)}, u32[]{:S(2)}) collective-permute-start(bf16[512,256]{1,0:T(8,128)(2,1)S(1)} %pad_maximum_fusion.1), channel_id=1, source_target_pairs={{0,12},{4,8},{8,4},{12,0},{1,13},{5,9},{9,5},{13,1},{2,14},{6,10},... | collective-permute-start | bytes 786440 | tf_op jit(solution)/shard_map/ppermute | solution.py:23
  18.2 7.9 %collective-permute-start.5 = (bf16[512,256]{1,0:T(8,128)(2,1)S(1)}, bf16[512,256]{1,0:T(8,128)(2,1)S(1)}, u32[]{:S(2)}, u32[]{:S(2)}) collective-permute-start(bf16[512,256]{1,0:T(8,128)(2,1)S(1)} %pad_maximum_fusion), channel_id=1, source_target_pairs={{0,32},{32,0},{64,96},{96,64},{1,33},{33,1},{65,97},{97,65},{2,34}... | collective-permute-start | bytes 786440 | tf_op jit(solution)/shard_map/ppermute | solution.py:23
  18.2 6.9 %collective-permute-start.7 = (bf16[512,256]{1,0:T(8,128)(2,1)S(1)}, bf16[512,256]{1,0:T(8,128)(2,1)S(1)}, u32[]{:S(2)}, u32[]{:S(2)}) collective-permute-start(bf16[512,256]{1,0:T(8,128)(2,1)S(1)} %pad_maximum_fusion), channel_id=1, source_target_pairs={{0,96},{32,64},{64,32},{96,0},{1,97},{33,65},{65,33},{97,1},{2,98}... | collective-permute-start | bytes 786440 | tf_op jit(solution)/shard_map/ppermute | solution.py:23
  23.9 5.3 %collective-permute-start.10 = (bf16[512,256]{1,0:T(8,128)(2,1)S(1)}, bf16[512,256]{1,0:T(8,128)(2,1)S(1)}, u32[]{:S(2)}, u32[]{:S(2)}) collective-permute-start(bf16[512,256]{1,0:T(8,128)(2,1)S(1)} %collective-permute-done.8), channel_id=1, source_target_pairs={{0,4},{4,0},{8,12},{12,8},{1,5},{5,1},{9,13},{13,9},{2,6},{6,2},{1... | collective-permute-start | bytes 786440 | tf_op jit(solution)/shard_map/ppermute | solution.py:23
  25.1 5.3 %collective-permute-start.9 = (bf16[512,256]{1,0:T(8,128)(2,1)S(1)}, bf16[512,256]{1,0:T(8,128)(2,1)S(1)}, u32[]{:S(2)}, u32[]{:S(2)}) collective-permute-start(bf16[512,256]{1,0:T(8,128)(2,1)S(1)} %collective-permute-done.7), channel_id=1, source_target_pairs={{0,32},{32,0},{64,96},{96,64},{1,33},{33,1},{65,97},{97,65},{2,34}... | collective-permute-start | bytes 786440 | tf_op jit(solution)/shard_map/ppermute | solution.py:23
  30.4 1.0 %copy-start = (bf16[256,1024]{1,0:T(8,128)(2,1)S(1)}, bf16[256,1024]{1,0:T(8,128)(2,1)}, u32[]{:S(2)}) copy-start(bf16[256,1024]{1,0:T(8,128)(2,1)} %self_ref.3) | copy-start | bytes 1572868
  30.4 1.2 %copy-start.1 = (bf16[256,1024]{1,0:T(8,128)(2,1)S(1)}, bf16[256,1024]{1,0:T(8,128)(2,1)}, u32[]{:S(2)}) copy-start(bf16[256,1024]{1,0:T(8,128)(2,1)} %nbr_ref.3) | copy-start | bytes 1572868
  32.3 7.5 %collective-permute-start.11 = (f16[512,512]{1,0:T(8,128)(2,1)S(1)}, f16[512,512]{1,0:T(8,128)(2,1)S(1)}, u32[]{:S(2)}, u32[]{:S(2)}) collective-permute-start(f16[512,512]{1,0:T(8,128)(2,1)S(1)} %convert_element_type.35), channel_id=1, source_target_pairs={{0,1},{1,0},{2,3},{3,2},{4,5},{5,4},{6,7},{7,6},{8,9},{9,8},{10,11... | collective-permute-start | bytes 1572872 | tf_op jit(solution)/shard_map/ppermute | solution.py:23
  40.2 6.3 %collective-permute-start.12 = (f16[256,256]{1,0:T(8,128)(2,1)S(1)}, f16[256,256]{1,0:T(8,128)(2,1)S(1)}, u32[]{:S(2)}, u32[]{:S(2)}) collective-permute-start(f16[256,256]{1,0:T(8,128)(2,1)S(1)} %get-tuple-element.45), channel_id=1, source_target_pairs={{0,2},{2,0},{1,3},{3,1},{4,6},{6,4},{5,7},{7,5},{8,10},{10,8},{9,1... | collective-permute-start | bytes 393224 | tf_op jit(solution)/shard_map/ppermute | solution.py:23
  42.9 6.6 %collective-permute-start.14 = (f16[256,256]{1,0:T(8,128)(2,1)S(1)}, f16[256,256]{1,0:T(8,128)(2,1)S(1)}, u32[]{:S(2)}, u32[]{:S(2)}) collective-permute-start(f16[256,256]{1,0:T(8,128)(2,1)S(1)} %get-tuple-element.46), channel_id=1, source_target_pairs={{0,18},{2,16},{16,2},{18,0},{1,19},{3,17},{17,3},{19,1},{4,22},{6,... | collective-permute-start | bytes 393224 | tf_op jit(solution)/shard_map/ppermute | solution.py:223
  42.9 6.6 %collective-permute-start.13 = (f16[256,256]{1,0:T(8,128)(2,1)S(1)}, f16[256,256]{1,0:T(8,128)(2,1)S(1)}, u32[]{:S(2)}, u32[]{:S(2)}) collective-permute-start(f16[256,256]{1,0:T(8,128)(2,1)S(1)} %slice_convert_fusion), channel_id=1, source_target_pairs={{0,16},{16,0},{1,17},{17,1},{2,18},{18,2},{3,19},{19,3},{4,20},{20... | collective-permute-start | bytes 393224 | tf_op jit(solution)/shard_map/ppermute | solution.py:23
  49.7 1.9 %collective-permute-start.15 = (f32[256]{0:T(256)S(1)}, f32[256]{0:T(256)S(1)}, u32[]{:S(2)}, u32[]{:S(2)}) collective-permute-start(f32[256]{0:T(256)S(1)} %multiply_reduce_fusion), channel_id=1, source_target_pairs={{0,1},{1,0},{2,3},{3,2},{4,5},{5,4},{6,7},{7,6},{8,9},{9,8},{10,11... | collective-permute-start | bytes 3080 | tf_op jit(solution)/shard_map/ppermute | solution.py:23
  51.6 3.9 %collective-permute-start.16 = (f32[256]{0:T(256)S(1)}, f32[256]{0:T(256)S(1)}, u32[]{:S(2)}, u32[]{:S(2)}) collective-permute-start(f32[256]{0:T(256)S(1)} %add.86), channel_id=1, source_target_pairs={{0,2},{2,0},{1,3},{3,1},{4,6},{6,4},{5,7},{7,5},{8,10},{10,8},{9,1... | collective-permute-start | bytes 3080 | tf_op jit(solution)/shard_map/ppermute | solution.py:23

commit v6 on v5

--- a/solution.py
+++ b/solution.py
@@ -182,9 +182,10 @@
 
     axes = [("x", "z"), ("z", "x")]
     halves = [items[:half], items[half:]]
-    lines = []
+    lines, pairs = [], []
     for block, (near, _) in zip(halves, axes):
         pair = jnp.concatenate([block, moved(block, near, lambda i: i ^ 1)], axis=0)
+        pairs.append(pair)
         rest = moved(pair, near, lambda i: i ^ 3)
         lines.append(jnp.concatenate([pair, rest], axis=0))
     pieces = []
@@ -194,7 +195,7 @@
         pieces += [line, low, high, moved(high, far, lambda i: i ^ 1)]
 
     table = (neighbor_ids.T, visit_counts.T, self_ids)
-    kept_back, _ = lax.optimization_barrier((table, lines))
+    kept_back, _ = lax.optimization_barrier((table, pairs))
     sent = lax.optimization_barrier(
         jnp.concatenate([kept_back[0], kept_back[1], kept_back[2][None, :]], axis=0)
     )

time: 56.7 us -> 57.5 us (1.014)
  waiting for transfers between devices: 13.3 us -> 15.3 us
  starting transfers between devices: 25.9 us -> 24.7 us
    ppermute x16, waiting for transfers between devices: 10.3 us -> 12.4 us  [moved(): return lax.ppermute(value, axis, [(i, target(i) % n) for i in range(n)])]
    ppermute x16, starting transfers between devices: 25.9 us -> 23.9 us  [moved(): return lax.ppermute(value, axis, [(i, target(i) % n) for i in range(n)])]
    ppermute x1, starting transfers between devices: 0.01 us -> 0.77 us  [shards(): lax.ppermute(there_part[batch:], ('yl', 'yh'), [(i, i ^ 3) for i in range...]
  transfers between devices with their start and end apart: 17 -> 17, of which waited for: 8 -> 9; matrix products, arithmetic and copies ran while one was open for 7% -> 7% of each run, Pallas kernels for 14% -> 14%
where the time goes in v6:
time: 57.5 us; the launch traced here: 57.2 us
  starting transfers between devices  24.7 us (43%)
  waiting for transfers between devices  15.3 us (27%)
  Pallas kernels  8.69 us (15%)
  matrix products  3.55 us (6%)
  local copies, waits for them, and re-layouts  3.15 us (5%)
  other arithmetic  1.51 us (3%)
    ppermute x16, starting transfers between devices, moved(): return lax.ppermute(value, axis, [(i, target(i) % n) for i in range(n)])  23.9 us
    ppermute x16, waiting for transfers between devices, moved(): return lax.ppermute(value, axis, [(i, target(i) % n) for i in range(n)])  12.4 us
    pallas_call x2, Pallas kernels, count_blocks(): pl.pallas_call(functools.partial(count_kernel, group, len(given)), out_sh...  7.52 us
    dot_general x8, matrix products, shards(): jnp.dot(blocks[i], pieces[i], preferred_element_type=jnp.float32)  3.55 us
    ppermute x1, waiting for transfers between devices, shards(): lax.ppermute(there_part[batch:], ('yl', 'yh'), [(i, i ^ 3) for i in range...  2.92 us
    unnamed x10, local copies, waits for them, and re-layouts  1.31 us
    pallas_call x2, Pallas kernels, projected(): pl.pallas_call(functools.partial(project_kernel, flip), out_shape=jax.Sha...  1.17 us
  transfers between devices with their start and end apart: 17, of which 9 were waited for; matrix products, arithmetic and copies ran while one was open for 7% of the time, Pallas kernels for 14%

profile of v6, /device:TPU:1, one launch (start us, length us, event | category | flops | bytes accessed | tf_op | source)
XLA Modules:
  0.0 57.2 jit_solution(14734941199360454717)
XLA Ops:
  0.0 0.9 %fusion.12 = (bf16[128,256]{1,0:T(8,128)(2,1)S(1)}, bf16[128,256]{1,0:T(8,128)(2,1)S(1)}) fusion(bf16[256,256]{1,0:T(8,128)(2,1)} %param.7), kind=kLoop, calls=%fused_computation.30 | loop fusion | bytes 262144 | tf_op jit(solution)/shard_map/slice | solution.py:184
  0.9 2.5 %collective-permute-start.1 = (bf16[128,256]{1,0:T(8,128)(2,1)S(1)}, bf16[128,256]{1,0:T(8,128)(2,1)S(1)}, u32[]{:S(2)}, u32[]{:S(2)}) collective-permute-start(bf16[128,256]{1,0:T(8,128)(2,1)S(1)} %get-tuple-element.47), channel_id=1, source_target_pairs={{0,32},{32,0},{64,96},{96,64},{1,33},{33,1},{65,97},{97,65},{2,34}... | collective-permute-start | bytes 196616 | tf_op jit(solution)/shard_map/ppermute | solution.py:23
  3.4 1.2 %collective-permute-start = (bf16[128,256]{1,0:T(8,128)(2,1)S(1)}, bf16[128,256]{1,0:T(8,128)(2,1)S(1)}, u32[]{:S(2)}, u32[]{:S(2)}) collective-permute-start(bf16[128,256]{1,0:T(8,128)(2,1)S(1)} %get-tuple-element.48), channel_id=1, source_target_pairs={{0,4},{4,0},{8,12},{12,8},{1,5},{5,1},{9,13},{13,9},{2,6},{6,2},{1... | collective-permute-start | bytes 196616 | tf_op jit(solution)/shard_map/ppermute | solution.py:23
  4.6 0.7 %copy-done.4 = s32[256]{0:T(256)S(1)} copy-done((s32[256]{0:T(256)S(1)}, s32[256]{0:T(256)}, u32[]{:S(2)}) %copy-start.4) | copy-done | bytes 1048
  5.3 3.8 %counts.2 = (bf16[1024,512]{1,0:T(8,128)(2,1)S(1)}, bf16[1024,512]{1,0:T(8,128)(2,1)S(1)}, bf16[1024,512]{1,0:T(8,128)(2,1)S(1)}, bf16[1024,512]{1,0:T(8,128)(2,...) custom-call(s32[1]{0:T(128)} %bitcast.here_ref, ...), custom_call_target="tpu_custom_call" | custom-call | flops 2000000000 | bytes 4500000 | tf_op jit(solution)/shard_map/counts/pallas_call | solution.py:119
  9.2 1.4 %collective-permute-start.2 = (s16[101,256]{1,0:T(8,128)(2,1)S(1)}, s16[101,256]{1,0:T(8,128)(2,1)S(1)}, u32[]{:S(2)}, u32[]{:S(2)}) collective-permute-start(s16[101,256]{1,0:T(8,128)(2,1)S(1)} %convert_element_type.31), channel_id=1, source_target_pairs={{0,16},{16,0},{1,17},{17,1},{2,18},{18,2},{3,19},{19,3},{4,20},{20... | collective-permute-start | bytes 155144 | tf_op jit(solution)/shard_map/ppermute | solution.py:23
  10.6 2.3 %collective-permute-start.4 = (bf16[256,256]{1,0:T(8,128)(2,1)S(1)}, bf16[256,256]{1,0:T(8,128)(2,1)S(1)}, u32[]{:S(2)}, u32[]{:S(2)}) collective-permute-start(bf16[256,256]{1,0:T(8,128)(2,1)S(1)} %pad_maximum_fusion.3), channel_id=1, source_target_pairs={{0,96},{32,64},{64,32},{96,0},{1,97},{33,65},{65,33},{97,1},{2,98}... | collective-permute-start | bytes 393224 | tf_op jit(solution)/shard_map/ppermute | solution.py:23
  12.9 1.8 %collective-permute-start.3 = (bf16[256,256]{1,0:T(8,128)(2,1)S(1)}, bf16[256,256]{1,0:T(8,128)(2,1)S(1)}, u32[]{:S(2)}, u32[]{:S(2)}) collective-permute-start(bf16[256,256]{1,0:T(8,128)(2,1)S(1)} %pad_maximum_fusion.2), channel_id=1, source_target_pairs={{0,12},{4,8},{8,4},{12,0},{1,13},{5,9},{9,5},{13,1},{2,14},{6,10},... | collective-permute-start | bytes 393224 | tf_op jit(solution)/shard_map/ppermute | solution.py:23
  14.8 3.8 %counts.3 = (bf16[1024,512]{1,0:T(8,128)(2,1)S(1)}, bf16[1024,512]{1,0:T(8,128)(2,1)S(1)}, bf16[1024,512]{1,0:T(8,128)(2,1)S(1)}, bf16[1024,512]{1,0:T(8,128)(2,...) custom-call(s32[1]{0:T(128)} %bitcast.here_ref, ...), custom_call_target="tpu_custom_call", output_to_operand_aliasing={{0}: (4, {}), {1}: (5, {}), {2}: (6, {}), {3}: (7, {}), {4}... | custom-call | flops 2000000000 | bytes 4500000 | tf_op jit(solution)/shard_map/counts/pallas_call | solution.py:119
  19.0 0.6 %collective-permute-start.8 = (bf16[512,256]{1,0:T(8,128)(2,1)S(1)}, bf16[512,256]{1,0:T(8,128)(2,1)S(1)}, u32[]{:S(2)}, u32[]{:S(2)}) collective-permute-start(bf16[512,256]{1,0:T(8,128)(2,1)S(1)} %pad_maximum_fusion.1), channel_id=1, source_target_pairs={{0,12},{4,8},{8,4},{12,0},{1,13},{5,9},{9,5},{13,1},{2,14},{6,10},... | collective-permute-start | bytes 786440 | tf_op jit(solution)/shard_map/ppermute | solution.py:23
  19.7 0.8 %collective-permute-start.5 = (bf16[512,256]{1,0:T(8,128)(2,1)S(1)}, bf16[512,256]{1,0:T(8,128)(2,1)S(1)}, u32[]{:S(2)}, u32[]{:S(2)}) collective-permute-start(bf16[512,256]{1,0:T(8,128)(2,1)S(1)} %pad_maximum_fusion), channel_id=1, source_target_pairs={{0,32},{32,0},{64,96},{96,64},{1,33},{33,1},{65,97},{97,65},{2,34}... | collective-permute-start | bytes 786440 | tf_op jit(solution)/shard_map/ppermute | solution.py:23
  20.5 2.1 %collective-permute-start.7 = (bf16[512,256]{1,0:T(8,128)(2,1)S(1)}, bf16[512,256]{1,0:T(8,128)(2,1)S(1)}, u32[]{:S(2)}, u32[]{:S(2)}) collective-permute-start(bf16[512,256]{1,0:T(8,128)(2,1)S(1)} %pad_maximum_fusion), channel_id=1, source_target_pairs={{0,96},{32,64},{64,32},{96,0},{1,97},{33,65},{65,33},{97,1},{2,98}... | collective-permute-start | bytes 786440 | tf_op jit(solution)/shard_map/ppermute | solution.py:23
  23.1 2.4 %collective-permute-done.8 = bf16[512,256]{1,0:T(8,128)(2,1)S(1)} collective-permute-done((bf16[512,256]{1,0:T(8,128)(2,1)S(1)}, bf16[512,256]{1,0:T(8,128)(2,1)S(1)}, u32[]{:S(2)}, u32[]{:S(2)}) %collective-permute-start.8) | collective-permute-done | bytes 262176 | tf_op jit(solution)/shard_map/ppermute | solution.py:23
  26.1 1.1 %collective-permute-done.7 = bf16[512,256]{1,0:T(8,128)(2,1)S(1)} collective-permute-done((bf16[512,256]{1,0:T(8,128)(2,1)S(1)}, bf16[512,256]{1,0:T(8,128)(2,1)S(1)}, u32[]{:S(2)}, u32[]{:S(2)}) %collective-permute-start.7) | collective-permute-done | bytes 262176 | tf_op jit(solution)/shard_map/ppermute | solution.py:23
  28.6 0.5 fusion.4
  29.1 1.6 %collective-permute-done.10 = bf16[512,256]{1,0:T(8,128)(2,1)S(1)} collective-permute-done((bf16[512,256]{1,0:T(8,128)(2,1)S(1)}, bf16[512,256]{1,0:T(8,128)(2,1)S(1)}, u32[]{:S(2)}, u32[]{:S(2)}) %collective-permute-start.10) | collective-permute-done | bytes 262176 | tf_op jit(solution)/shard_map/ppermute | solution.py:23
  31.1 1.6 %collective-permute-done.9 = bf16[512,256]{1,0:T(8,128)(2,1)S(1)} collective-permute-done((bf16[512,256]{1,0:T(8,128)(2,1)S(1)}, bf16[512,256]{1,0:T(8,128)(2,1)S(1)}, u32[]{:S(2)}, u32[]{:S(2)}) %collective-permute-start.9) | collective-permute-done | bytes 262176 | tf_op jit(solution)/shard_map/ppermute | solution.py:23
  33.3 0.5 copy-done
  33.9 0.6 %project.3 = f32[512,512]{1,0:T(8,128)S(1)} custom-call(s32[1]{0:T(128)} %bitcast.here_ref, f32[1024,256]{1,0:T(8,128)S(1)} %fusion.sums_ref, f32[512,128]{1,0:T(8,128)S(1)} %broadcast_in_dim.5.total_ref, bf16[256,1024]{1,0:T(8,128)(2,1)S(1)} %copy-done, bf16[256,1024]{1,0:T(8,128)(2,1)S(1)} %copy-done.1), custom_call_target="tpu_custom_call" | custom-call | flops 400000000 | bytes 4000000 | tf_op jit(solution)/shard_map/project/pallas_call | solution.py:163
  34.6 4.4 %collective-permute-start.11 = (f16[512,512]{1,0:T(8,128)(2,1)S(1)}, f16[512,512]{1,0:T(8,128)(2,1)S(1)}, u32[]{:S(2)}, u32[]{:S(2)}) collective-permute-start(f16[512,512]{1,0:T(8,128)(2,1)S(1)} %convert_element_type.35), channel_id=1, source_target_pairs={{0,1},{1,0},{2,3},{3,2},{4,5},{5,4},{6,7},{7,6},{8,9},{9,8},{10,11... | collective-permute-start | bytes 1572872 | tf_op jit(solution)/shard_map/ppermute | solution.py:23
  39.1 0.6 %project.2 = f32[512,512]{1,0:T(8,128)S(1)} custom-call(s32[1]{0:T(128)} %bitcast.here_ref, f32[1024,256]{1,0:T(8,128)S(1)} %fusion.sums_ref, f32[512,128]{1,0:T(8,128)S(1)} %broadcast_in_dim.5.total_ref, bf16[256,1024]{1,0:T(8,128)(2,1)S(1)} %copy-done, bf16[256,1024]{1,0:T(8,128)(2,1)S(1)} %copy-done.1), custom_call_target="tpu_custom_call" | custom-call | flops 400000000 | bytes 4000000 | tf_op jit(solution)/shard_map/project/pallas_call | solution.py:163
  39.7 0.9 %collective-permute-done.11 = f16[512,512]{1,0:T(8,128)(2,1)S(1)} collective-permute-done((f16[512,512]{1,0:T(8,128)(2,1)S(1)}, f16[512,512]{1,0:T(8,128)(2,1)S(1)}, u32[]{:S(2)}, u32[]{:S(2)}) %collective-permute-start.11) | collective-permute-done | bytes 524320 | tf_op jit(solution)/shard_map/ppermute | solution.py:23
  40.9 2.8 %collective-permute-start.12 = (f16[256,256]{1,0:T(8,128)(2,1)S(1)}, f16[256,256]{1,0:T(8,128)(2,1)S(1)}, u32[]{:S(2)}, u32[]{:S(2)}) collective-permute-start(f16[256,256]{1,0:T(8,128)(2,1)S(1)} %get-tuple-element.45), channel_id=1, source_target_pairs={{0,2},{2,0},{1,3},{3,1},{4,6},{6,4},{5,7},{7,5},{8,10},{10,8},{9,1... | collective-permute-start | bytes 393224 | tf_op jit(solution)/shard_map/ppermute | solution.py:23
  43.7 0.8 %collective-permute-start.14 = (f16[256,256]{1,0:T(8,128)(2,1)S(1)}, f16[256,256]{1,0:T(8,128)(2,1)S(1)}, u32[]{:S(2)}, u32[]{:S(2)}) collective-permute-start(f16[256,256]{1,0:T(8,128)(2,1)S(1)} %get-tuple-element.46), channel_id=1, source_target_pairs={{0,18},{2,16},{16,2},{18,0},{1,19},{3,17},{17,3},{19,1},{4,22},{6,... | collective-permute-start | bytes 393224 | tf_op jit(solution)/shard_map/ppermute | solution.py:224
  44.6 0.8 %dynamic_slice.3 = f32[256]{0:T(256)S(1)} dynamic-slice(f32[1024]{0:T(1024)} %param.13, s32[]{:T(128)S(6)} %select_n.18), dynamic_slice_sizes={256} | dynamic-slice | bytes 2052 | tf_op jit(solution)/shard_map/dynamic_slice | solution.py:227
  45.4 1.8 %collective-permute-done.12 = f16[256,256]{1,0:T(8,128)(2,1)S(1)} collective-permute-done((f16[256,256]{1,0:T(8,128)(2,1)S(1)}, f16[256,256]{1,0:T(8,128)(2,1)S(1)}, u32[]{:S(2)}, u32[]{:S(2)}) %collective-permute-start.12) | collective-permute-done | bytes 131104 | tf_op jit(solution)/shard_map/ppermute | solution.py:23
  47.2 2.9 %collective-permute-done.14 = f16[256,256]{1,0:T(8,128)(2,1)S(1)} collective-permute-done((f16[256,256]{1,0:T(8,128)(2,1)S(1)}, f16[256,256]{1,0:T(8,128)(2,1)S(1)}, u32[]{:S(2)}, u32[]{:S(2)}) %collective-permute-start.14) | collective-permute-done | bytes 131104 | tf_op jit(solution)/shard_map/ppermute | solution.py:224
  50.3 1.3 %collective-permute-start.15 = (f32[256]{0:T(256)S(1)}, f32[256]{0:T(256)S(1)}, u32[]{:S(2)}, u32[]{:S(2)}) collective-permute-start(f32[256]{0:T(256)S(1)} %multiply_reduce_fusion), channel_id=1, source_target_pairs={{0,1},{1,0},{2,3},{3,2},{4,5},{5,4},{6,7},{7,6},{8,9},{9,8},{10,11... | collective-permute-start | bytes 3080 | tf_op jit(solution)/shard_map/ppermute | solution.py:23
  51.6 0.8 %collective-permute-done.15 = f32[256]{0:T(256)S(1)} collective-permute-done((f32[256]{0:T(256)S(1)}, f32[256]{0:T(256)S(1)}, u32[]{:S(2)}, u32[]{:S(2)}) %collective-permute-start.15) | collective-permute-done | bytes 1056 | tf_op jit(solution)/shard_map/ppermute | solution.py:23
  52.4 1.8 %collective-permute-start.16 = (f32[256]{0:T(256)S(1)}, f32[256]{0:T(256)S(1)}, u32[]{:S(2)}, u32[]{:S(2)}) collective-permute-start(f32[256]{0:T(256)S(1)} %add.86), channel_id=1, source_target_pairs={{0,2},{2,0},{1,3},{3,1},{4,6},{6,4},{5,7},{7,5},{8,10},{10,8},{9,1... | collective-permute-start | bytes 3080 | tf_op jit(solution)/shard_map/ppermute | solution.py:23
  54.2 2.1 %collective-permute-done.16 = f32[256]{0:T(256)S(1)} collective-permute-done((f32[256]{0:T(256)S(1)}, f32[256]{0:T(256)S(1)}, u32[]{:S(2)}, u32[]{:S(2)}) %collective-permute-start.16) | collective-permute-done | bytes 1056 | tf_op jit(solution)/shard_map/ppermute | solution.py:23
  56.4 0.8 %broadcast_divide_fusion = f32[256,256]{1,0:T(8,128)} fusion(f32[256]{0:T(256)S(1)} %add_sqrt_fusion, f32[256]{0:T(256)S(1)} %dynamic_slice.3, f16[256,256]{1,0:T(8,128)(2,1)S(1)} %collective-permute-done.14, f16[256,256]{1,0:T(8,128)(2,1)S(1)} %collective-permute-done.13, f16[256,256]{1,0:T(8,128)(2,1)S(1)} %collective-permute-done.12, ...), kind=kLoop, calls=%fused_computation.22 | loop fusion | flops 655360 | bytes 919552 | tf_op jit(solution)/shard_map/div | solution.py:233
  (48 shorter events, 4.8 us)
Async XLA Ops:
  0.0 4.6 %copy-start.3 = (s32[256,50]{0,1:T(8,128)S(1)}, s32[256,50]{0,1:T(8,128)}, u32[]{:S(2)}) copy-start(s32[256,50]{0,1:T(8,128)} %param.9) | copy-start | bytes 153604
  0.0 4.6 %copy-start.2 = (s32[256,50]{0,1:T(8,128)S(1)}, s32[256,50]{0,1:T(8,128)}, u32[]{:S(2)}) copy-start(s32[256,50]{0,1:T(8,128)} %param.10) | copy-start | bytes 153604
  0.9 8.2 %collective-permute-start.1 = (bf16[128,256]{1,0:T(8,128)(2,1)S(1)}, bf16[128,256]{1,0:T(8,128)(2,1)S(1)}, u32[]{:S(2)}, u32[]{:S(2)}) collective-permute-start(bf16[128,256]{1,0:T(8,128)(2,1)S(1)} %get-tuple-element.47), channel_id=1, source_target_pairs={{0,32},{32,0},{64,96},{96,64},{1,33},{33,1},{65,97},{97,65},{2,34}... | collective-permute-start | bytes 196616 | tf_op jit(solution)/shard_map/ppermute | solution.py:23
  3.4 5.7 %collective-permute-start = (bf16[128,256]{1,0:T(8,128)(2,1)S(1)}, bf16[128,256]{1,0:T(8,128)(2,1)S(1)}, u32[]{:S(2)}, u32[]{:S(2)}) collective-permute-start(bf16[128,256]{1,0:T(8,128)(2,1)S(1)} %get-tuple-element.48), channel_id=1, source_target_pairs={{0,4},{4,0},{8,12},{12,8},{1,5},{5,1},{9,13},{13,9},{2,6},{6,2},{1... | collective-permute-start | bytes 196616 | tf_op jit(solution)/shard_map/ppermute | solution.py:23
  4.6 0.7 %copy-start.4 = (s32[256]{0:T(256)S(1)}, s32[256]{0:T(256)}, u32[]{:S(2)}) copy-start(s32[256]{0:T(256)} %param.8) | copy-start | bytes 3076
  9.2 5.5 %collective-permute-start.2 = (s16[101,256]{1,0:T(8,128)(2,1)S(1)}, s16[101,256]{1,0:T(8,128)(2,1)S(1)}, u32[]{:S(2)}, u32[]{:S(2)}) collective-permute-start(s16[101,256]{1,0:T(8,128)(2,1)S(1)} %convert_element_type.31), channel_id=1, source_target_pairs={{0,16},{16,0},{1,17},{17,1},{2,18},{18,2},{3,19},{19,3},{4,20},{20... | collective-permute-start | bytes 155144 | tf_op jit(solution)/shard_map/ppermute | solution.py:23
  10.6 8.0 %collective-permute-start.4 = (bf16[256,256]{1,0:T(8,128)(2,1)S(1)}, bf16[256,256]{1,0:T(8,128)(2,1)S(1)}, u32[]{:S(2)}, u32[]{:S(2)}) collective-permute-start(bf16[256,256]{1,0:T(8,128)(2,1)S(1)} %pad_maximum_fusion.3), channel_id=1, source_target_pairs={{0,96},{32,64},{64,32},{96,0},{1,97},{33,65},{65,33},{97,1},{2,98}... | collective-permute-start | bytes 393224 | tf_op jit(solution)/shard_map/ppermute | solution.py:23
  12.9 6.8 %collective-permute-start.3 = (bf16[256,256]{1,0:T(8,128)(2,1)S(1)}, bf16[256,256]{1,0:T(8,128)(2,1)S(1)}, u32[]{:S(2)}, u32[]{:S(2)}) collective-permute-start(bf16[256,256]{1,0:T(8,128)(2,1)S(1)} %pad_maximum_fusion.2), channel_id=1, source_target_pairs={{0,12},{4,8},{8,4},{12,0},{1,13},{5,9},{9,5},{13,1},{2,14},{6,10},... | collective-permute-start | bytes 393224 | tf_op jit(solution)/shard_map/ppermute | solution.py:23
  18.6 9.0 %collective-permute-start.6 = (bf16[512,256]{1,0:T(8,128)(2,1)S(1)}, bf16[512,256]{1,0:T(8,128)(2,1)S(1)}, u32[]{:S(2)}, u32[]{:S(2)}) collective-permute-start(bf16[512,256]{1,0:T(8,128)(2,1)S(1)} %pad_maximum_fusion.1), channel_id=1, source_target_pairs={{0,4},{4,0},{8,12},{12,8},{1,5},{5,1},{9,13},{13,9},{2,6},{6,2},{1... | collective-permute-start | bytes 786440 | tf_op jit(solution)/shard_map/ppermute | solution.py:23
  19.0 6.4 %collective-permute-start.8 = (bf16[512,256]{1,0:T(8,128)(2,1)S(1)}, bf16[512,256]{1,0:T(8,128)(2,1)S(1)}, u32[]{:S(2)}, u32[]{:S(2)}) collective-permute-start(bf16[512,256]{1,0:T(8,128)(2,1)S(1)} %pad_maximum_fusion.1), channel_id=1, source_target_pairs={{0,12},{4,8},{8,4},{12,0},{1,13},{5,9},{9,5},{13,1},{2,14},{6,10},... | collective-permute-start | bytes 786440 | tf_op jit(solution)/shard_map/ppermute | solution.py:23
  19.7 8.4 %collective-permute-start.5 = (bf16[512,256]{1,0:T(8,128)(2,1)S(1)}, bf16[512,256]{1,0:T(8,128)(2,1)S(1)}, u32[]{:S(2)}, u32[]{:S(2)}) collective-permute-start(bf16[512,256]{1,0:T(8,128)(2,1)S(1)} %pad_maximum_fusion), channel_id=1, source_target_pairs={{0,32},{32,0},{64,96},{96,64},{1,33},{33,1},{65,97},{97,65},{2,34}... | collective-permute-start | bytes 786440 | tf_op jit(solution)/shard_map/ppermute | solution.py:23
  20.5 6.7 %collective-permute-start.7 = (bf16[512,256]{1,0:T(8,128)(2,1)S(1)}, bf16[512,256]{1,0:T(8,128)(2,1)S(1)}, u32[]{:S(2)}, u32[]{:S(2)}) collective-permute-start(bf16[512,256]{1,0:T(8,128)(2,1)S(1)} %pad_maximum_fusion), channel_id=1, source_target_pairs={{0,96},{32,64},{64,32},{96,0},{1,97},{33,65},{65,33},{97,1},{2,98}... | collective-permute-start | bytes 786440 | tf_op jit(solution)/shard_map/ppermute | solution.py:23
  25.4 5.2 %collective-permute-start.10 = (bf16[512,256]{1,0:T(8,128)(2,1)S(1)}, bf16[512,256]{1,0:T(8,128)(2,1)S(1)}, u32[]{:S(2)}, u32[]{:S(2)}) collective-permute-start(bf16[512,256]{1,0:T(8,128)(2,1)S(1)} %collective-permute-done.8), channel_id=1, source_target_pairs={{0,4},{4,0},{8,12},{12,8},{1,5},{5,1},{9,13},{13,9},{2,6},{6,2},{1... | collective-permute-start | bytes 786440 | tf_op jit(solution)/shard_map/ppermute | solution.py:23
  27.2 5.5 %collective-permute-start.9 = (bf16[512,256]{1,0:T(8,128)(2,1)S(1)}, bf16[512,256]{1,0:T(8,128)(2,1)S(1)}, u32[]{:S(2)}, u32[]{:S(2)}) collective-permute-start(bf16[512,256]{1,0:T(8,128)(2,1)S(1)} %collective-permute-done.7), channel_id=1, source_target_pairs={{0,32},{32,0},{64,96},{96,64},{1,33},{33,1},{65,97},{97,65},{2,34}... | collective-permute-start | bytes 786440 | tf_op jit(solution)/shard_map/ppermute | solution.py:23
  32.7 1.0 %copy-start = (bf16[256,1024]{1,0:T(8,128)(2,1)S(1)}, bf16[256,1024]{1,0:T(8,128)(2,1)}, u32[]{:S(2)}) copy-start(bf16[256,1024]{1,0:T(8,128)(2,1)} %self_ref.3) | copy-start | bytes 1572868
  32.7 1.2 %copy-start.1 = (bf16[256,1024]{1,0:T(8,128)(2,1)S(1)}, bf16[256,1024]{1,0:T(8,128)(2,1)}, u32[]{:S(2)}) copy-start(bf16[256,1024]{1,0:T(8,128)(2,1)} %nbr_ref.3) | copy-start | bytes 1572868
  34.6 6.0 %collective-permute-start.11 = (f16[512,512]{1,0:T(8,128)(2,1)S(1)}, f16[512,512]{1,0:T(8,128)(2,1)S(1)}, u32[]{:S(2)}, u32[]{:S(2)}) collective-permute-start(f16[512,512]{1,0:T(8,128)(2,1)S(1)} %convert_element_type.35), channel_id=1, source_target_pairs={{0,1},{1,0},{2,3},{3,2},{4,5},{5,4},{6,7},{7,6},{8,9},{9,8},{10,11... | collective-permute-start | bytes 1572872 | tf_op jit(solution)/shard_map/ppermute | solution.py:23
  40.9 6.3 %collective-permute-start.12 = (f16[256,256]{1,0:T(8,128)(2,1)S(1)}, f16[256,256]{1,0:T(8,128)(2,1)S(1)}, u32[]{:S(2)}, u32[]{:S(2)}) collective-permute-start(f16[256,256]{1,0:T(8,128)(2,1)S(1)} %get-tuple-element.45), channel_id=1, source_target_pairs={{0,2},{2,0},{1,3},{3,1},{4,6},{6,4},{5,7},{7,5},{8,10},{10,8},{9,1... | collective-permute-start | bytes 393224 | tf_op jit(solution)/shard_map/ppermute | solution.py:23
  43.7 6.4 %collective-permute-start.14 = (f16[256,256]{1,0:T(8,128)(2,1)S(1)}, f16[256,256]{1,0:T(8,128)(2,1)S(1)}, u32[]{:S(2)}, u32[]{:S(2)}) collective-permute-start(f16[256,256]{1,0:T(8,128)(2,1)S(1)} %get-tuple-element.46), channel_id=1, source_target_pairs={{0,18},{2,16},{16,2},{18,0},{1,19},{3,17},{17,3},{19,1},{4,22},{6,... | collective-permute-start | bytes 393224 | tf_op jit(solution)/shard_map/ppermute | solution.py:224
  44.5 5.6 %collective-permute-start.13 = (f16[256,256]{1,0:T(8,128)(2,1)S(1)}, f16[256,256]{1,0:T(8,128)(2,1)S(1)}, u32[]{:S(2)}, u32[]{:S(2)}) collective-permute-start(f16[256,256]{1,0:T(8,128)(2,1)S(1)} %slice_convert_fusion), channel_id=1, source_target_pairs={{0,16},{16,0},{1,17},{17,1},{2,18},{18,2},{3,19},{19,3},{4,20},{20... | collective-permute-start | bytes 393224 | tf_op jit(solution)/shard_map/ppermute | solution.py:23
  50.3 2.1 %collective-permute-start.15 = (f32[256]{0:T(256)S(1)}, f32[256]{0:T(256)S(1)}, u32[]{:S(2)}, u32[]{:S(2)}) collective-permute-start(f32[256]{0:T(256)S(1)} %multiply_reduce_fusion), channel_id=1, source_target_pairs={{0,1},{1,0},{2,3},{3,2},{4,5},{5,4},{6,7},{7,6},{8,9},{9,8},{10,11... | collective-permute-start | bytes 3080 | tf_op jit(solution)/shard_map/ppermute | solution.py:23
  52.4 3.9 %collective-permute-start.16 = (f32[256]{0:T(256)S(1)}, f32[256]{0:T(256)S(1)}, u32[]{:S(2)}, u32[]{:S(2)}) collective-permute-start(f32[256]{0:T(256)S(1)} %add.86), channel_id=1, source_target_pairs={{0,2},{2,0},{1,3},{3,1},{4,6},{6,4},{5,7},{7,5},{8,10},{10,8},{9,1... | collective-permute-start | bytes 3080 | tf_op jit(solution)/shard_map/ppermute | solution.py:23

commit v7 on v6

--- a/solution.py
+++ b/solution.py
@@ -139,7 +139,7 @@
     )
 
 
-def project_kernel(flip, here_ref, sums_ref, total_ref, self_ref, nbr_ref, out_ref):
+def project_kernel(flip, here_ref, sums_ref, total_ref, weights_ref, out_ref):
     nodes, share = sums_ref.shape[0] // 2, sums_ref.shape[1]
     total = jnp.concatenate([total_ref[...]] * (share // LANES), axis=1)
     own = sums_ref[nodes:, :].astype(jnp.bfloat16)
@@ -150,27 +150,27 @@
     for part in range(2):
         first = pl.multiple_of(part * 2 * share + which * share, share)
         columns = pl.ds(first, share)
-        w_self, w_nbr = self_ref[:, columns], nbr_ref[:, columns]
+        w_self, w_nbr = weights_ref[:share, columns], weights_ref[share:, columns]
         out = jnp.dot(own, w_self, preferred_element_type=jnp.float32)
         out += jnp.dot(high, w_nbr, preferred_element_type=jnp.float32)
         out += jnp.dot(low, w_nbr, preferred_element_type=jnp.float32)
         out_ref[:, part * share : (part + 1) * share] = out * SCALE
 
 
-def projected(flip, here, sums, total, w_self, w_neighbor):
+def projected(flip, here, sums, total, weights):
     nodes, share = sums.shape[0] // 2, sums.shape[1]
     vmem = pl.BlockSpec(memory_space=pltpu.VMEM)
     return pl.pallas_call(
         functools.partial(project_kernel, flip),
         out_shape=jax.ShapeDtypeStruct((nodes, 2 * share), jnp.float32),
-        in_specs=[pl.BlockSpec(memory_space=pltpu.SMEM)] + [vmem] * 4,
+        in_specs=[pl.BlockSpec(memory_space=pltpu.SMEM)] + [vmem] * 3,
         out_specs=vmem,
         compiler_params=pltpu.CompilerParams(vmem_limit_bytes=12 * 2**20),
         cost_estimate=pl.CostEstimate(
             flops=400_000_000, bytes_accessed=4_000_000, transcendentals=0
         ),
         name="project",
-    )(here, sums, total, w_self, w_neighbor)
+    )(here, sums, total, weights)
 
 
 def shards(items, self_ids, neighbor_ids, visit_counts, w_self, w_neighbor, bias):
@@ -201,6 +201,7 @@
     )
     theirs = moved(sent.astype(jnp.int16), "yl", lambda i: i ^ 1).astype(jnp.int32)
     table = jnp.concatenate([table[0], table[1], table[2][None, :]], axis=0)
+    weights = jnp.concatenate([w_self, w_neighbor], axis=0)
     widths = [p.shape[0] for p in pieces]
     blocks = count_blocks(0, [], here, table, nbr, widths)
     blocks = count_blocks(1, blocks, here, theirs, nbr, widths)
@@ -212,9 +213,9 @@
         [jnp.sum(t[nbr : 2 * nbr].astype(jnp.float32), axis=0) for t in (table, theirs)]
     )
     total = jnp.broadcast_to(total[:, None], (2 * batch, LANES))
-    given = projected(1, here, sums, total, w_self, w_neighbor)
+    given = projected(1, here, sums, total, weights)
     got = moved(given.astype(jnp.float16), "core", lambda i: i ^ 1)
-    kept = projected(0, here, sums, total, w_self, w_neighbor)
+    kept = projected(0, here, sums, total, weights)
     chip = kept + got.astype(jnp.float32)
     first, second = chip[:, :share], chip[:, share:]
     here_part = jnp.where(yh == 0, first, second)

time: 57.5 us -> 58 us (level)
    unnamed x10 -> x9, local copies, waits for them, and re-layouts: 1.31 us -> 1.75 us
  transfers between devices with their start and end apart: 17 -> 17, of which waited for: 9 -> 9; matrix products, arithmetic and copies ran while one was open for 7% -> 9% of each run, Pallas kernels for 14% -> 14%
where the time goes in v7:
time: 58 us; the launch traced here: 57.7 us
  starting transfers between devices  24.6 us (42%)
  waiting for transfers between devices  15.4 us (27%)
  Pallas kernels  8.68 us (15%)
  local copies, waits for them, and re-layouts  3.61 us (6%)
  matrix products  3.55 us (6%)
  other arithmetic  1.51 us (3%)
    ppermute x16, starting transfers between devices, moved(): return lax.ppermute(value, axis, [(i, target(i) % n) for i in range(n)])  23.9 us
    ppermute x16, waiting for transfers between devices, moved(): return lax.ppermute(value, axis, [(i, target(i) % n) for i in range(n)])  12.4 us
    pallas_call x2, Pallas kernels, count_blocks(): pl.pallas_call(functools.partial(count_kernel, group, len(given)), out_sh...  7.51 us
    dot_general x8, matrix products, shards(): jnp.dot(blocks[i], pieces[i], preferred_element_type=jnp.float32)  3.55 us
    ppermute x1, waiting for transfers between devices, shards(): lax.ppermute(there_part[batch:], ('yl', 'yh'), [(i, i ^ 3) for i in range...  2.94 us
    unnamed x9, local copies, waits for them, and re-layouts  1.75 us
    pallas_call x2, Pallas kernels, projected(): pl.pallas_call(functools.partial(project_kernel, flip), out_shape=jax.Sha...  1.18 us
  transfers between devices with their start and end apart: 17, of which 9 were waited for; matrix products, arithmetic and copies ran while one was open for 9% of the time, Pallas kernels for 14%

profile of v7, /device:TPU:1, one launch (start us, length us, event | category | flops | bytes accessed | tf_op | source)
XLA Modules:
  0.0 57.7 jit_solution(16968573803185679382)
XLA Ops:
  0.0 0.9 %fusion.12 = (bf16[128,256]{1,0:T(8,128)(2,1)S(1)}, bf16[128,256]{1,0:T(8,128)(2,1)S(1)}) fusion(bf16[256,256]{1,0:T(8,128)(2,1)} %param.7), kind=kLoop, calls=%fused_computation.32 | loop fusion | bytes 262144 | tf_op jit(solution)/shard_map/slice | solution.py:184
  0.9 2.5 %collective-permute-start.1 = (bf16[128,256]{1,0:T(8,128)(2,1)S(1)}, bf16[128,256]{1,0:T(8,128)(2,1)S(1)}, u32[]{:S(2)}, u32[]{:S(2)}) collective-permute-start(bf16[128,256]{1,0:T(8,128)(2,1)S(1)} %get-tuple-element.47), channel_id=1, source_target_pairs={{0,32},{32,0},{64,96},{96,64},{1,33},{33,1},{65,97},{97,65},{2,34}... | collective-permute-start | bytes 196616 | tf_op jit(solution)/shard_map/ppermute | solution.py:23
  3.4 1.2 %collective-permute-start = (bf16[128,256]{1,0:T(8,128)(2,1)S(1)}, bf16[128,256]{1,0:T(8,128)(2,1)S(1)}, u32[]{:S(2)}, u32[]{:S(2)}) collective-permute-start(bf16[128,256]{1,0:T(8,128)(2,1)S(1)} %get-tuple-element.48), channel_id=1, source_target_pairs={{0,4},{4,0},{8,12},{12,8},{1,5},{5,1},{9,13},{13,9},{2,6},{6,2},{1... | collective-permute-start | bytes 196616 | tf_op jit(solution)/shard_map/ppermute | solution.py:23
  4.6 1.1 %constant_dynamic-update-slice_fusion.1 = bf16[512,1024]{1,0:T(8,128)(2,1)S(1)} fusion(bf16[256,1024]{1,0:T(8,128)(2,1)} %param.11), kind=kLoop, calls=%fused_computation.27 | loop fusion | bytes 1048576
  5.8 0.7 %copy-done.2 = s32[256]{0:T(256)S(1)} copy-done((s32[256]{0:T(256)S(1)}, s32[256]{0:T(256)}, u32[]{:S(2)}) %copy-start.2) | copy-done | bytes 1048
  6.4 3.7 %counts.2 = (bf16[1024,512]{1,0:T(8,128)(2,1)S(1)}, bf16[1024,512]{1,0:T(8,128)(2,1)S(1)}, bf16[1024,512]{1,0:T(8,128)(2,1)S(1)}, bf16[1024,512]{1,0:T(8,128)(2,...) custom-call(s32[1]{0:T(128)} %bitcast.here_ref, ...), custom_call_target="tpu_custom_call" | custom-call | flops 2000000000 | bytes 4500000 | tf_op jit(solution)/shard_map/counts/pallas_call | solution.py:119
  10.3 1.4 %collective-permute-start.2 = (s16[101,256]{1,0:T(8,128)(2,1)S(1)}, s16[101,256]{1,0:T(8,128)(2,1)S(1)}, u32[]{:S(2)}, u32[]{:S(2)}) collective-permute-start(s16[101,256]{1,0:T(8,128)(2,1)S(1)} %convert_element_type.31), channel_id=1, source_target_pairs={{0,16},{16,0},{1,17},{17,1},{2,18},{18,2},{3,19},{19,3},{4,20},{20... | collective-permute-start | bytes 155144 | tf_op jit(solution)/shard_map/ppermute | solution.py:23
  11.7 2.3 %collective-permute-start.4 = (bf16[256,256]{1,0:T(8,128)(2,1)S(1)}, bf16[256,256]{1,0:T(8,128)(2,1)S(1)}, u32[]{:S(2)}, u32[]{:S(2)}) collective-permute-start(bf16[256,256]{1,0:T(8,128)(2,1)S(1)} %pad_maximum_fusion.3), channel_id=1, source_target_pairs={{0,96},{32,64},{64,32},{96,0},{1,97},{33,65},{65,33},{97,1},{2,98}... | collective-permute-start | bytes 393224 | tf_op jit(solution)/shard_map/ppermute | solution.py:23
  14.1 1.8 %collective-permute-start.3 = (bf16[256,256]{1,0:T(8,128)(2,1)S(1)}, bf16[256,256]{1,0:T(8,128)(2,1)S(1)}, u32[]{:S(2)}, u32[]{:S(2)}) collective-permute-start(bf16[256,256]{1,0:T(8,128)(2,1)S(1)} %pad_maximum_fusion.2), channel_id=1, source_target_pairs={{0,12},{4,8},{8,4},{12,0},{1,13},{5,9},{9,5},{13,1},{2,14},{6,10},... | collective-permute-start | bytes 393224 | tf_op jit(solution)/shard_map/ppermute | solution.py:23
  15.9 3.8 %counts.3 = (bf16[1024,512]{1,0:T(8,128)(2,1)S(1)}, bf16[1024,512]{1,0:T(8,128)(2,1)S(1)}, bf16[1024,512]{1,0:T(8,128)(2,1)S(1)}, bf16[1024,512]{1,0:T(8,128)(2,...) custom-call(s32[1]{0:T(128)} %bitcast.here_ref, ...), custom_call_target="tpu_custom_call", output_to_operand_aliasing={{0}: (4, {}), {1}: (5, {}), {2}: (6, {}), {3}: (7, {}), {4}... | custom-call | flops 2000000000 | bytes 4500000 | tf_op jit(solution)/shard_map/counts/pallas_call | solution.py:119
  20.2 0.6 %collective-permute-start.8 = (bf16[512,256]{1,0:T(8,128)(2,1)S(1)}, bf16[512,256]{1,0:T(8,128)(2,1)S(1)}, u32[]{:S(2)}, u32[]{:S(2)}) collective-permute-start(bf16[512,256]{1,0:T(8,128)(2,1)S(1)} %pad_maximum_fusion.1), channel_id=1, source_target_pairs={{0,12},{4,8},{8,4},{12,0},{1,13},{5,9},{9,5},{13,1},{2,14},{6,10},... | collective-permute-start | bytes 786440 | tf_op jit(solution)/shard_map/ppermute | solution.py:23
  20.8 0.8 %collective-permute-start.5 = (bf16[512,256]{1,0:T(8,128)(2,1)S(1)}, bf16[512,256]{1,0:T(8,128)(2,1)S(1)}, u32[]{:S(2)}, u32[]{:S(2)}) collective-permute-start(bf16[512,256]{1,0:T(8,128)(2,1)S(1)} %pad_maximum_fusion), channel_id=1, source_target_pairs={{0,32},{32,0},{64,96},{96,64},{1,33},{33,1},{65,97},{97,65},{2,34}... | collective-permute-start | bytes 786440 | tf_op jit(solution)/shard_map/ppermute | solution.py:23
  21.7 2.1 %collective-permute-start.7 = (bf16[512,256]{1,0:T(8,128)(2,1)S(1)}, bf16[512,256]{1,0:T(8,128)(2,1)S(1)}, u32[]{:S(2)}, u32[]{:S(2)}) collective-permute-start(bf16[512,256]{1,0:T(8,128)(2,1)S(1)} %pad_maximum_fusion), channel_id=1, source_target_pairs={{0,96},{32,64},{64,32},{96,0},{1,97},{33,65},{65,33},{97,1},{2,98}... | collective-permute-start | bytes 786440 | tf_op jit(solution)/shard_map/ppermute | solution.py:23
  24.2 2.4 %collective-permute-done.8 = bf16[512,256]{1,0:T(8,128)(2,1)S(1)} collective-permute-done((bf16[512,256]{1,0:T(8,128)(2,1)S(1)}, bf16[512,256]{1,0:T(8,128)(2,1)S(1)}, u32[]{:S(2)}, u32[]{:S(2)}) %collective-permute-start.8) | collective-permute-done | bytes 262176 | tf_op jit(solution)/shard_map/ppermute | solution.py:23
  27.3 1.1 %collective-permute-done.7 = bf16[512,256]{1,0:T(8,128)(2,1)S(1)} collective-permute-done((bf16[512,256]{1,0:T(8,128)(2,1)S(1)}, bf16[512,256]{1,0:T(8,128)(2,1)S(1)}, u32[]{:S(2)}, u32[]{:S(2)}) %collective-permute-start.7) | collective-permute-done | bytes 262176 | tf_op jit(solution)/shard_map/ppermute | solution.py:23
  29.7 0.5 fusion.4
  30.2 1.6 %collective-permute-done.10 = bf16[512,256]{1,0:T(8,128)(2,1)S(1)} collective-permute-done((bf16[512,256]{1,0:T(8,128)(2,1)S(1)}, bf16[512,256]{1,0:T(8,128)(2,1)S(1)}, u32[]{:S(2)}, u32[]{:S(2)}) %collective-permute-start.10) | collective-permute-done | bytes 262176 | tf_op jit(solution)/shard_map/ppermute | solution.py:23
  32.3 1.6 %collective-permute-done.9 = bf16[512,256]{1,0:T(8,128)(2,1)S(1)} collective-permute-done((bf16[512,256]{1,0:T(8,128)(2,1)S(1)}, bf16[512,256]{1,0:T(8,128)(2,1)S(1)}, u32[]{:S(2)}, u32[]{:S(2)}) %collective-permute-start.9) | collective-permute-done | bytes 262176 | tf_op jit(solution)/shard_map/ppermute | solution.py:23
  34.5 0.6 %project.3 = f32[512,512]{1,0:T(8,128)S(1)} custom-call(s32[1]{0:T(128)} %bitcast.here_ref, f32[1024,256]{1,0:T(8,128)S(1)} %fusion.sums_ref, f32[512,128]{1,0:T(8,128)S(1)} %broadcast_in_dim.5.total_ref, bf16[512,1024]{1,0:T(8,128)(2,1)S(1)} %constant_dynamic-update-slice_fusion.weights_ref), custom_call_target="tpu_custom_call" | custom-call | flops 400000000 | bytes 4000000 | tf_op jit(solution)/shard_map/project/pallas_call | solution.py:163
  35.2 4.4 %collective-permute-start.11 = (f16[512,512]{1,0:T(8,128)(2,1)S(1)}, f16[512,512]{1,0:T(8,128)(2,1)S(1)}, u32[]{:S(2)}, u32[]{:S(2)}) collective-permute-start(f16[512,512]{1,0:T(8,128)(2,1)S(1)} %convert_element_type.35), channel_id=1, source_target_pairs={{0,1},{1,0},{2,3},{3,2},{4,5},{5,4},{6,7},{7,6},{8,9},{9,8},{10,11... | collective-permute-start | bytes 1572872 | tf_op jit(solution)/shard_map/ppermute | solution.py:23
  39.6 0.6 %project.2 = f32[512,512]{1,0:T(8,128)S(1)} custom-call(s32[1]{0:T(128)} %bitcast.here_ref, f32[1024,256]{1,0:T(8,128)S(1)} %fusion.sums_ref, f32[512,128]{1,0:T(8,128)S(1)} %broadcast_in_dim.5.total_ref, bf16[512,1024]{1,0:T(8,128)(2,1)S(1)} %constant_dynamic-update-slice_fusion.weights_ref), custom_call_target="tpu_custom_call" | custom-call | flops 400000000 | bytes 4000000 | tf_op jit(solution)/shard_map/project/pallas_call | solution.py:163
  40.2 0.9 %collective-permute-done.11 = f16[512,512]{1,0:T(8,128)(2,1)S(1)} collective-permute-done((f16[512,512]{1,0:T(8,128)(2,1)S(1)}, f16[512,512]{1,0:T(8,128)(2,1)S(1)}, u32[]{:S(2)}, u32[]{:S(2)}) %collective-permute-start.11) | collective-permute-done | bytes 524320 | tf_op jit(solution)/shard_map/ppermute | solution.py:23
  41.4 2.8 %collective-permute-start.12 = (f16[256,256]{1,0:T(8,128)(2,1)S(1)}, f16[256,256]{1,0:T(8,128)(2,1)S(1)}, u32[]{:S(2)}, u32[]{:S(2)}) collective-permute-start(f16[256,256]{1,0:T(8,128)(2,1)S(1)} %get-tuple-element.45), channel_id=1, source_target_pairs={{0,2},{2,0},{1,3},{3,1},{4,6},{6,4},{5,7},{7,5},{8,10},{10,8},{9,1... | collective-permute-start | bytes 393224 | tf_op jit(solution)/shard_map/ppermute | solution.py:23
  44.2 0.8 %collective-permute-start.14 = (f16[256,256]{1,0:T(8,128)(2,1)S(1)}, f16[256,256]{1,0:T(8,128)(2,1)S(1)}, u32[]{:S(2)}, u32[]{:S(2)}) collective-permute-start(f16[256,256]{1,0:T(8,128)(2,1)S(1)} %get-tuple-element.46), channel_id=1, source_target_pairs={{0,18},{2,16},{16,2},{18,0},{1,19},{3,17},{17,3},{19,1},{4,22},{6,... | collective-permute-start | bytes 393224 | tf_op jit(solution)/shard_map/ppermute | solution.py:225
  45.1 0.8 %dynamic_slice.3 = f32[256]{0:T(256)S(1)} dynamic-slice(f32[1024]{0:T(1024)} %param.13, s32[]{:T(128)S(6)} %select_n.18), dynamic_slice_sizes={256} | dynamic-slice | bytes 2052 | tf_op jit(solution)/shard_map/dynamic_slice | solution.py:228
  45.9 1.8 %collective-permute-done.12 = f16[256,256]{1,0:T(8,128)(2,1)S(1)} collective-permute-done((f16[256,256]{1,0:T(8,128)(2,1)S(1)}, f16[256,256]{1,0:T(8,128)(2,1)S(1)}, u32[]{:S(2)}, u32[]{:S(2)}) %collective-permute-start.12) | collective-permute-done | bytes 131104 | tf_op jit(solution)/shard_map/ppermute | solution.py:23
  47.7 2.9 %collective-permute-done.14 = f16[256,256]{1,0:T(8,128)(2,1)S(1)} collective-permute-done((f16[256,256]{1,0:T(8,128)(2,1)S(1)}, f16[256,256]{1,0:T(8,128)(2,1)S(1)}, u32[]{:S(2)}, u32[]{:S(2)}) %collective-permute-start.14) | collective-permute-done | bytes 131104 | tf_op jit(solution)/shard_map/ppermute | solution.py:225
  50.8 1.3 %collective-permute-start.15 = (f32[256]{0:T(256)S(1)}, f32[256]{0:T(256)S(1)}, u32[]{:S(2)}, u32[]{:S(2)}) collective-permute-start(f32[256]{0:T(256)S(1)} %multiply_reduce_fusion), channel_id=1, source_target_pairs={{0,1},{1,0},{2,3},{3,2},{4,5},{5,4},{6,7},{7,6},{8,9},{9,8},{10,11... | collective-permute-start | bytes 3080 | tf_op jit(solution)/shard_map/ppermute | solution.py:23
  52.1 0.8 %collective-permute-done.15 = f32[256]{0:T(256)S(1)} collective-permute-done((f32[256]{0:T(256)S(1)}, f32[256]{0:T(256)S(1)}, u32[]{:S(2)}, u32[]{:S(2)}) %collective-permute-start.15) | collective-permute-done | bytes 1056 | tf_op jit(solution)/shard_map/ppermute | solution.py:23
  52.9 1.8 %collective-permute-start.16 = (f32[256]{0:T(256)S(1)}, f32[256]{0:T(256)S(1)}, u32[]{:S(2)}, u32[]{:S(2)}) collective-permute-start(f32[256]{0:T(256)S(1)} %add.86), channel_id=1, source_target_pairs={{0,2},{2,0},{1,3},{3,1},{4,6},{6,4},{5,7},{7,5},{8,10},{10,8},{9,1... | collective-permute-start | bytes 3080 | tf_op jit(solution)/shard_map/ppermute | solution.py:23
  54.7 2.1 %collective-permute-done.16 = f32[256]{0:T(256)S(1)} collective-permute-done((f32[256]{0:T(256)S(1)}, f32[256]{0:T(256)S(1)}, u32[]{:S(2)}, u32[]{:S(2)}) %collective-permute-start.16) | collective-permute-done | bytes 1056 | tf_op jit(solution)/shard_map/ppermute | solution.py:23
  56.9 0.8 %broadcast_divide_fusion = f32[256,256]{1,0:T(8,128)} fusion(f32[256]{0:T(256)S(1)} %add_sqrt_fusion, f32[256]{0:T(256)S(1)} %dynamic_slice.3, f16[256,256]{1,0:T(8,128)(2,1)S(1)} %collective-permute-done.14, f16[256,256]{1,0:T(8,128)(2,1)S(1)} %collective-permute-done.13, f16[256,256]{1,0:T(8,128)(2,1)S(1)} %collective-permute-done.12, ...), kind=kLoop, calls=%fused_computation.22 | loop fusion | flops 655360 | bytes 919552 | tf_op jit(solution)/shard_map/div | solution.py:234
  (48 shorter events, 4.7 us)
Async XLA Ops:
  0.9 9.3 %collective-permute-start.1 = (bf16[128,256]{1,0:T(8,128)(2,1)S(1)}, bf16[128,256]{1,0:T(8,128)(2,1)S(1)}, u32[]{:S(2)}, u32[]{:S(2)}) collective-permute-start(bf16[128,256]{1,0:T(8,128)(2,1)S(1)} %get-tuple-element.47), channel_id=1, source_target_pairs={{0,32},{32,0},{64,96},{96,64},{1,33},{33,1},{65,97},{97,65},{2,34}... | collective-permute-start | bytes 196616 | tf_op jit(solution)/shard_map/ppermute | solution.py:23
  3.4 6.8 %collective-permute-start = (bf16[128,256]{1,0:T(8,128)(2,1)S(1)}, bf16[128,256]{1,0:T(8,128)(2,1)S(1)}, u32[]{:S(2)}, u32[]{:S(2)}) collective-permute-start(bf16[128,256]{1,0:T(8,128)(2,1)S(1)} %get-tuple-element.48), channel_id=1, source_target_pairs={{0,4},{4,0},{8,12},{12,8},{1,5},{5,1},{9,13},{13,9},{2,6},{6,2},{1... | collective-permute-start | bytes 196616 | tf_op jit(solution)/shard_map/ppermute | solution.py:23
  4.6 1.1 %copy-start = (s32[256,50]{0,1:T(8,128)S(1)}, s32[256,50]{0,1:T(8,128)}, u32[]{:S(2)}) copy-start(s32[256,50]{0,1:T(8,128)} %param.10) | copy-start | bytes 153604
  4.6 1.1 %copy-start.1 = (s32[256,50]{0,1:T(8,128)S(1)}, s32[256,50]{0,1:T(8,128)}, u32[]{:S(2)}) copy-start(s32[256,50]{0,1:T(8,128)} %param.9) | copy-start | bytes 153604
  5.7 0.7 %copy-start.2 = (s32[256]{0:T(256)S(1)}, s32[256]{0:T(256)}, u32[]{:S(2)}) copy-start(s32[256]{0:T(256)} %param.8) | copy-start | bytes 3076
  6.4 3.8 %copy-start.3 = (bf16[256,1024]{1,0:T(8,128)(2,1)S(1)}, bf16[256,1024]{1,0:T(8,128)(2,1)}, u32[]{:S(2)}) copy-start(bf16[256,1024]{1,0:T(8,128)(2,1)} %param.12) | copy-start | bytes 1572868
  10.3 5.5 %collective-permute-start.2 = (s16[101,256]{1,0:T(8,128)(2,1)S(1)}, s16[101,256]{1,0:T(8,128)(2,1)S(1)}, u32[]{:S(2)}, u32[]{:S(2)}) collective-permute-start(s16[101,256]{1,0:T(8,128)(2,1)S(1)} %convert_element_type.31), channel_id=1, source_target_pairs={{0,16},{16,0},{1,17},{17,1},{2,18},{18,2},{3,19},{19,3},{4,20},{20... | collective-permute-start | bytes 155144 | tf_op jit(solution)/shard_map/ppermute | solution.py:23
  11.7 8.0 %collective-permute-start.4 = (bf16[256,256]{1,0:T(8,128)(2,1)S(1)}, bf16[256,256]{1,0:T(8,128)(2,1)S(1)}, u32[]{:S(2)}, u32[]{:S(2)}) collective-permute-start(bf16[256,256]{1,0:T(8,128)(2,1)S(1)} %pad_maximum_fusion.3), channel_id=1, source_target_pairs={{0,96},{32,64},{64,32},{96,0},{1,97},{33,65},{65,33},{97,1},{2,98}... | collective-permute-start | bytes 393224 | tf_op jit(solution)/shard_map/ppermute | solution.py:23
  14.1 6.8 %collective-permute-start.3 = (bf16[256,256]{1,0:T(8,128)(2,1)S(1)}, bf16[256,256]{1,0:T(8,128)(2,1)S(1)}, u32[]{:S(2)}, u32[]{:S(2)}) collective-permute-start(bf16[256,256]{1,0:T(8,128)(2,1)S(1)} %pad_maximum_fusion.2), channel_id=1, source_target_pairs={{0,12},{4,8},{8,4},{12,0},{1,13},{5,9},{9,5},{13,1},{2,14},{6,10},... | collective-permute-start | bytes 393224 | tf_op jit(solution)/shard_map/ppermute | solution.py:23
  19.8 9.1 %collective-permute-start.6 = (bf16[512,256]{1,0:T(8,128)(2,1)S(1)}, bf16[512,256]{1,0:T(8,128)(2,1)S(1)}, u32[]{:S(2)}, u32[]{:S(2)}) collective-permute-start(bf16[512,256]{1,0:T(8,128)(2,1)S(1)} %pad_maximum_fusion.1), channel_id=1, source_target_pairs={{0,4},{4,0},{8,12},{12,8},{1,5},{5,1},{9,13},{13,9},{2,6},{6,2},{1... | collective-permute-start | bytes 786440 | tf_op jit(solution)/shard_map/ppermute | solution.py:23
  20.2 6.4 %collective-permute-start.8 = (bf16[512,256]{1,0:T(8,128)(2,1)S(1)}, bf16[512,256]{1,0:T(8,128)(2,1)S(1)}, u32[]{:S(2)}, u32[]{:S(2)}) collective-permute-start(bf16[512,256]{1,0:T(8,128)(2,1)S(1)} %pad_maximum_fusion.1), channel_id=1, source_target_pairs={{0,12},{4,8},{8,4},{12,0},{1,13},{5,9},{9,5},{13,1},{2,14},{6,10},... | collective-permute-start | bytes 786440 | tf_op jit(solution)/shard_map/ppermute | solution.py:23
  20.8 8.4 %collective-permute-start.5 = (bf16[512,256]{1,0:T(8,128)(2,1)S(1)}, bf16[512,256]{1,0:T(8,128)(2,1)S(1)}, u32[]{:S(2)}, u32[]{:S(2)}) collective-permute-start(bf16[512,256]{1,0:T(8,128)(2,1)S(1)} %pad_maximum_fusion), channel_id=1, source_target_pairs={{0,32},{32,0},{64,96},{96,64},{1,33},{33,1},{65,97},{97,65},{2,34}... | collective-permute-start | bytes 786440 | tf_op jit(solution)/shard_map/ppermute | solution.py:23
  21.7 6.7 %collective-permute-start.7 = (bf16[512,256]{1,0:T(8,128)(2,1)S(1)}, bf16[512,256]{1,0:T(8,128)(2,1)S(1)}, u32[]{:S(2)}, u32[]{:S(2)}) collective-permute-start(bf16[512,256]{1,0:T(8,128)(2,1)S(1)} %pad_maximum_fusion), channel_id=1, source_target_pairs={{0,96},{32,64},{64,32},{96,0},{1,97},{33,65},{65,33},{97,1},{2,98}... | collective-permute-start | bytes 786440 | tf_op jit(solution)/shard_map/ppermute | solution.py:23
  26.6 5.2 %collective-permute-start.10 = (bf16[512,256]{1,0:T(8,128)(2,1)S(1)}, bf16[512,256]{1,0:T(8,128)(2,1)S(1)}, u32[]{:S(2)}, u32[]{:S(2)}) collective-permute-start(bf16[512,256]{1,0:T(8,128)(2,1)S(1)} %collective-permute-done.8), channel_id=1, source_target_pairs={{0,4},{4,0},{8,12},{12,8},{1,5},{5,1},{9,13},{13,9},{2,6},{6,2},{1... | collective-permute-start | bytes 786440 | tf_op jit(solution)/shard_map/ppermute | solution.py:23
  28.4 5.5 %collective-permute-start.9 = (bf16[512,256]{1,0:T(8,128)(2,1)S(1)}, bf16[512,256]{1,0:T(8,128)(2,1)S(1)}, u32[]{:S(2)}, u32[]{:S(2)}) collective-permute-start(bf16[512,256]{1,0:T(8,128)(2,1)S(1)} %collective-permute-done.7), channel_id=1, source_target_pairs={{0,32},{32,0},{64,96},{96,64},{1,33},{33,1},{65,97},{97,65},{2,34}... | collective-permute-start | bytes 786440 | tf_op jit(solution)/shard_map/ppermute | solution.py:23
  35.2 6.0 %collective-permute-start.11 = (f16[512,512]{1,0:T(8,128)(2,1)S(1)}, f16[512,512]{1,0:T(8,128)(2,1)S(1)}, u32[]{:S(2)}, u32[]{:S(2)}) collective-permute-start(f16[512,512]{1,0:T(8,128)(2,1)S(1)} %convert_element_type.35), channel_id=1, source_target_pairs={{0,1},{1,0},{2,3},{3,2},{4,5},{5,4},{6,7},{7,6},{8,9},{9,8},{10,11... | collective-permute-start | bytes 1572872 | tf_op jit(solution)/shard_map/ppermute | solution.py:23
  41.4 6.3 %collective-permute-start.12 = (f16[256,256]{1,0:T(8,128)(2,1)S(1)}, f16[256,256]{1,0:T(8,128)(2,1)S(1)}, u32[]{:S(2)}, u32[]{:S(2)}) collective-permute-start(f16[256,256]{1,0:T(8,128)(2,1)S(1)} %get-tuple-element.45), channel_id=1, source_target_pairs={{0,2},{2,0},{1,3},{3,1},{4,6},{6,4},{5,7},{7,5},{8,10},{10,8},{9,1... | collective-permute-start | bytes 393224 | tf_op jit(solution)/shard_map/ppermute | solution.py:23
  44.2 6.4 %collective-permute-start.14 = (f16[256,256]{1,0:T(8,128)(2,1)S(1)}, f16[256,256]{1,0:T(8,128)(2,1)S(1)}, u32[]{:S(2)}, u32[]{:S(2)}) collective-permute-start(f16[256,256]{1,0:T(8,128)(2,1)S(1)} %get-tuple-element.46), channel_id=1, source_target_pairs={{0,18},{2,16},{16,2},{18,0},{1,19},{3,17},{17,3},{19,1},{4,22},{6,... | collective-permute-start | bytes 393224 | tf_op jit(solution)/shard_map/ppermute | solution.py:225
  45.0 5.6 %collective-permute-start.13 = (f16[256,256]{1,0:T(8,128)(2,1)S(1)}, f16[256,256]{1,0:T(8,128)(2,1)S(1)}, u32[]{:S(2)}, u32[]{:S(2)}) collective-permute-start(f16[256,256]{1,0:T(8,128)(2,1)S(1)} %slice_convert_fusion), channel_id=1, source_target_pairs={{0,16},{16,0},{1,17},{17,1},{2,18},{18,2},{3,19},{19,3},{4,20},{20... | collective-permute-start | bytes 393224 | tf_op jit(solution)/shard_map/ppermute | solution.py:23
  50.8 2.1 %collective-permute-start.15 = (f32[256]{0:T(256)S(1)}, f32[256]{0:T(256)S(1)}, u32[]{:S(2)}, u32[]{:S(2)}) collective-permute-start(f32[256]{0:T(256)S(1)} %multiply_reduce_fusion), channel_id=1, source_target_pairs={{0,1},{1,0},{2,3},{3,2},{4,5},{5,4},{6,7},{7,6},{8,9},{9,8},{10,11... | collective-permute-start | bytes 3080 | tf_op jit(solution)/shard_map/ppermute | solution.py:23
  52.9 3.9 %collective-permute-start.16 = (f32[256]{0:T(256)S(1)}, f32[256]{0:T(256)S(1)}, u32[]{:S(2)}, u32[]{:S(2)}) collective-permute-start(f32[256]{0:T(256)S(1)} %add.86), channel_id=1, source_target_pairs={{0,2},{2,0},{1,3},{3,1},{4,6},{6,4},{5,7},{7,5},{8,10},{10,8},{9,1... | collective-permute-start | bytes 3080 | tf_op jit(solution)/shard_map/ppermute | solution.py:23
